TPU v7x, 32 devices: a whole 2x2x4 slice. The times are simulated.
32 devices in a mesh: seq: 8 (over z, core), head: 4 (over y, x).
Axes of the slice: x: 2, y: 2, z: 4, core: 2. Of those that a mesh axis runs over, the one named last changes fastest.
Arguments:
- queries: bfloat16 [1024, 4096], P('seq', 'head'), may hold values from -360 to 360, as said below
- keys: bfloat16 [1024, 256], P('seq', 'head'), may hold values from -6 to 6
- values: bfloat16 [1024, 256], P('seq', 'head'), may hold values from -6 to 6
- directions: bfloat16 [1024, 256], P('seq', 'head'), may hold values from -6 to 6
- beta: float32 [1024, 2], P('seq'), may hold values from 0.25 to 2
- gain: float32 [128], replicated, may hold values from 0.25 to 1.75
Outputs:
- attended: bfloat16 [1024, 4096], P('seq', 'head')
Inputs may be any that keep to these rules, and one draw needn't show every extreme that they name: `queries`: queries of order one; some rows may be far larger.
All inputs are finite; a program needn't handle non-finite values.
Results may differ from a plain program's by a relative error of at most 0.04.
Values may be sent and summed in bfloat16 or wider, within the bound.
No kernel may reach another device: no remote copies, remote signals or barrier semaphores. Data moves between devices by JAX's collectives and lax.ppermute only.
A program may use at most 64 MiB of HBM per device.

v0:
```python
import jax
import jax.numpy as jnp
from jax import lax
from jax.sharding import PartitionSpec as P

exact_mode = lax.Precision.HIGHEST


def partner(value, axis, bit):
    mask = 2**bit
    pairs = [(source, source ^ mask) for source in range(lax.axis_size(axis))]
    return lax.ppermute(value, axis, pairs)


def shifted(shard, axis, by):
    size = lax.axis_size(axis)
    pairs = [(i, i + by) for i in range(size) if 0 <= i + by < size]
    return lax.ppermute(shard, axis, pairs)


def segment_terms(queries, keys, directions, beta):
    length, head_count, head_width = queries.shape
    raw_dirs = directions.astype(jnp.float32)
    unit_dirs = raw_dirs * lax.rsqrt(jnp.sum(raw_dirs * raw_dirs, axis=1, keepdims=True) + 1e-06)
    positions = jnp.arange(length)
    strict_mask = positions[:, None] > positions[None, :]
    causal_mask = positions[:, None] >= positions[None, :]
    intersections = jnp.where(
        strict_mask, jnp.dot(unit_dirs, unit_dirs.T, precision=exact_mode), 0.0
    )
    identity = jnp.eye(length, dtype=jnp.float32)
    scaled_dirs = beta[:, None] * unit_dirs
    keys_wide = keys.astype(jnp.float32)
    key_reach = jnp.where(strict_mask, jnp.dot(unit_dirs, keys_wide.T, precision=exact_mode), 0.0)
    solution = jax.scipy.linalg.solve_triangular(
        identity + intersections * beta[None, :],
        jnp.concatenate([key_reach, unit_dirs], axis=1),
        lower=True,
        unit_diagonal=True,
    )
    moved_keys = keys_wide - jnp.dot(solution[:, :length].T, scaled_dirs, precision=exact_mode)
    transform = jnp.eye(head_width, dtype=jnp.float32) - jnp.dot(
        unit_dirs.T, beta[:, None] * solution[:, length:], precision=exact_mode
    )
    queries_wide = queries.astype(jnp.float32)
    query_reach = jnp.einsum("te,ihe->thi", unit_dirs, queries_wide, precision=exact_mode)
    query_reach = jnp.where(causal_mask.T[:, None, :], query_reach, 0.0)
    coefficients = jax.scipy.linalg.solve_triangular(
        identity + beta[:, None] * intersections,
        query_reach.reshape(length, head_count * length),
        lower=True,
        trans=1,
        unit_diagonal=True,
    ).reshape(length, head_count, length)
    moved_queries = queries_wide - jnp.einsum(
        "thi,te->ihe", coefficients, scaled_dirs, precision=exact_mode
    )
    plain_scores = jnp.einsum("ihe,je->ihj", queries_wide, keys_wide, precision=exact_mode)
    correction = jnp.einsum(
        "thi,tj->ihj", coefficients, beta[:, None] * key_reach, precision=exact_mode
    )
    local_scores = jnp.where(
        causal_mask[:, None, :], (plain_scores - correction) * head_width ** (-0.5), -1e30
    )
    return (moved_queries, moved_keys, transform, local_scores)


def joined(parity, own_part, other_part, dim):
    first = jnp.concatenate([own_part, other_part], axis=dim)
    second = jnp.concatenate([other_part, own_part], axis=dim)
    return jnp.where(parity == 0, first, second)


def shards(queries, keys, values, directions, beta, gain):
    length = directions.shape[0]
    head_width = directions.shape[1] * 2
    head_count = queries.shape[1] // head_width
    head_place = lax.axis_index("head")
    parity = head_place % 2
    group_index = head_place // 2
    other_keys, other_values, other_dirs = partner((keys, values, directions), "head", 0)
    key_rows = joined(parity, keys, other_keys, 1)
    value_rows = joined(parity, values, other_values, 1)
    dir_rows = joined(parity, directions, other_dirs, 1)
    picker = (jnp.arange(beta.shape[1]) == group_index).astype(jnp.float32)
    beta_rows = jnp.sum(beta * picker[None, :], axis=1)
    moved_queries, moved_keys, transform, local_scores = segment_terms(
        queries.reshape(length, head_count, head_width), key_rows, dir_rows, beta_rows
    )
    query_rows = moved_queries.reshape(length * head_count, head_width).astype(jnp.bfloat16)
    local_flat = local_scores.reshape(length * head_count, length)
    running_max = jnp.max(local_flat, axis=1)
    weights_exp = jnp.exp(local_flat - running_max[:, None])
    running_sum = jnp.sum(weights_exp, axis=1)
    running_out = jnp.dot(
        weights_exp.astype(jnp.bfloat16), value_rows, preferred_element_type=jnp.float32
    )
    key_travel = moved_keys.astype(jnp.bfloat16)
    hop_matrix = transform.astype(jnp.bfloat16)
    segment_index = lax.axis_index("seq")
    scale = head_width ** (-0.5)

    def absorb(stats, key_block, value_block):
        old_max, old_sum, old_out = stats
        scores = jnp.dot(query_rows, key_block.T, preferred_element_type=jnp.float32) * scale
        new_max = jnp.maximum(old_max, jnp.max(scores, axis=1))
        fading = jnp.exp(old_max - new_max)
        block_exp = jnp.exp(scores - new_max[:, None])
        new_sum = old_sum * fading + jnp.sum(block_exp, axis=1)
        new_out = old_out * fading[:, None] + jnp.dot(
            block_exp.astype(jnp.bfloat16), value_block, preferred_element_type=jnp.float32
        )
        return (new_max, new_sum, new_out)

    def forward(key_block):
        return jnp.dot(key_block, hop_matrix.T, preferred_element_type=jnp.float32).astype(
            jnp.bfloat16
        )

    def keep(stats_now):
        return stats_now

    stats = (running_max, running_sum, running_out)

    def advance(step_index, carried):
        key_block, value_block = shifted((carried[0], carried[1]), "seq", 1)

        def take(stats_now):
            return absorb(stats_now, key_block, value_block)

        new_stats = lax.cond(step_index <= segment_index, take, keep, carried[2])
        return (forward(key_block), value_block, new_stats)

    carried = lax.fori_loop(1, lax.axis_size("seq"), advance, (key_travel, value_rows, stats))
    final_max, final_sum, final_out = carried[2]
    mixed = final_out / final_sum[:, None]
    strength = lax.rsqrt(jnp.mean(mixed * mixed, axis=1, keepdims=True) + 1e-06)
    normed = mixed * strength * gain[None, :]
    return normed.reshape(length, head_count * head_width).astype(jnp.bfloat16)


def solution(mesh):
    placed = (
        P("seq", "head"),
        P("seq", "head"),
        P("seq", "head"),
        P("seq", "head"),
        P("seq", None),
        P(),
    )
    return jax.shard_map(
        shards, mesh=mesh, in_specs=placed, out_specs=P("seq", "head"), check_vma=False
    )
```

profile of v0, /device:TPU:24, one launch (start us, length us, event | category | flops | bytes accessed | tf_op | source)
XLA Modules:
  0.0 91.4 jit_solution(8206682460453305803)
XLA Ops:
  8.0 9.8 %custom-call.9 = f32[1,128,128]{1,2,0:T(8,128)S(1)} custom-call(f32[1,128,128]{2,1,0:T(8,128)S(1)} %get-tuple-element.219), custom_call_target="InvertDiagBlocksLowerTriangular" | custom-call | tf_op jit(solution)/shard_map/jit(_solve_triangular)/triangular_solve | solution.py:48
  20.2 9.8 %custom-call.8 = f32[1,128,128]{1,2,0:T(8,128)S(1)} custom-call(f32[1,128,128]{2,1,0:T(8,128)S(1)} %get-tuple-element.220), custom_call_target="InvertDiagBlocksLowerTriangular" | custom-call | tf_op jit(solution)/shard_map/jit(_solve_triangular)/triangular_solve | solution.py:35
  33.1 56.2 %while.21 = (s32[]{:T(128)}, bf16[128,128]{1,0:T(8,128)(2,1)S(1)}, bf16[128,128]{1,0:T(8,128)(2,1)S(1)}, f32[1024]{0:T(1024)S(1)}, f32[1024]{0:T(1024)S(1)}, /*i...) while((s32[]{:T(128)}, bf16[128,128]{1,0:T(8,128)(2,1)S(1)}, ...), condition=%wide.region_9.10_spmd, body=%wide.region_4.9_spmd.sunk | while | flops 72370176 | bytes 3440939 | solution.py:134
  33.1 1.9 %collective-permute-start = (bf16[128,128]{1,0:T(8,128)(2,1)S(1)}, bf16[128,128]{1,0:T(8,128)(2,1)S(1)}, u32[]{:S(2)}, u32[]{:S(2)}) collective-permute-start(bf16[128,128]{1,0:T(8,128)(2,1)S(1)} %get-tuple-element.301), channel_id=1, source_target_pairs={{0,4},{4,8},{8,12},{12,16},{16,20},{20,24},{24,28},{1,5},{5,9},{9,... | collective-permute-start | bytes 98312 | tf_op jit(solution)/shard_map/while/body/eval_jaxpr/ppermute | solution.py:18
  35.0 1.9 %collective-permute-start.1 = (bf16[128,128]{1,0:T(8,128)(2,1)S(1)}, bf16[128,128]{1,0:T(8,128)(2,1)S(1)}, u32[]{:S(2)}, u32[]{:S(2)}) collective-permute-start(bf16[128,128]{1,0:T(8,128)(2,1)S(1)} %get-tuple-element.302), channel_id=1, source_target_pairs={{0,4},{4,8},{8,12},{12,16},{16,20},{20,24},{24,28},{1,5},{5,9},{9,... | collective-permute-start | bytes 98312 | tf_op jit(solution)/shard_map/while/body/eval_jaxpr/ppermute | solution.py:18
  38.3 1.9 %collective-permute-done.1 = bf16[128,128]{1,0:T(8,128)(2,1)S(1)} collective-permute-done((bf16[128,128]{1,0:T(8,128)(2,1)S(1)}, bf16[128,128]{1,0:T(8,128)(2,1)S(1)}, u32[]{:S(2)}, u32[]{:S(2)}) %collective-permute-start.1) | collective-permute-done | bytes 32800 | tf_op jit(solution)/shard_map/while/body/eval_jaxpr/ppermute | solution.py:18
  41.2 1.9 %collective-permute-start = (bf16[128,128]{1,0:T(8,128)(2,1)S(1)}, bf16[128,128]{1,0:T(8,128)(2,1)S(1)}, u32[]{:S(2)}, u32[]{:S(2)}) collective-permute-start(bf16[128,128]{1,0:T(8,128)(2,1)S(1)} %get-tuple-element.301), channel_id=1, source_target_pairs={{0,4},{4,8},{8,12},{12,16},{16,20},{20,24},{24,28},{1,5},{5,9},{9,... | collective-permute-start | bytes 98312 | tf_op jit(solution)/shard_map/while/body/eval_jaxpr/ppermute | solution.py:18
  43.1 1.9 %collective-permute-start.1 = (bf16[128,128]{1,0:T(8,128)(2,1)S(1)}, bf16[128,128]{1,0:T(8,128)(2,1)S(1)}, u32[]{:S(2)}, u32[]{:S(2)}) collective-permute-start(bf16[128,128]{1,0:T(8,128)(2,1)S(1)} %get-tuple-element.302), channel_id=1, source_target_pairs={{0,4},{4,8},{8,12},{12,16},{16,20},{20,24},{24,28},{1,5},{5,9},{9,... | collective-permute-start | bytes 98312 | tf_op jit(solution)/shard_map/while/body/eval_jaxpr/ppermute | solution.py:18
  46.5 1.9 %collective-permute-done.1 = bf16[128,128]{1,0:T(8,128)(2,1)S(1)} collective-permute-done((bf16[128,128]{1,0:T(8,128)(2,1)S(1)}, bf16[128,128]{1,0:T(8,128)(2,1)S(1)}, u32[]{:S(2)}, u32[]{:S(2)}) %collective-permute-start.1) | collective-permute-done | bytes 32800 | tf_op jit(solution)/shard_map/while/body/eval_jaxpr/ppermute | solution.py:18
  49.3 1.9 %collective-permute-start = (bf16[128,128]{1,0:T(8,128)(2,1)S(1)}, bf16[128,128]{1,0:T(8,128)(2,1)S(1)}, u32[]{:S(2)}, u32[]{:S(2)}) collective-permute-start(bf16[128,128]{1,0:T(8,128)(2,1)S(1)} %get-tuple-element.301), channel_id=1, source_target_pairs={{0,4},{4,8},{8,12},{12,16},{16,20},{20,24},{24,28},{1,5},{5,9},{9,... | collective-permute-start | bytes 98312 | tf_op jit(solution)/shard_map/while/body/eval_jaxpr/ppermute | solution.py:18
  51.3 1.9 %collective-permute-start.1 = (bf16[128,128]{1,0:T(8,128)(2,1)S(1)}, bf16[128,128]{1,0:T(8,128)(2,1)S(1)}, u32[]{:S(2)}, u32[]{:S(2)}) collective-permute-start(bf16[128,128]{1,0:T(8,128)(2,1)S(1)} %get-tuple-element.302), channel_id=1, source_target_pairs={{0,4},{4,8},{8,12},{12,16},{16,20},{20,24},{24,28},{1,5},{5,9},{9,... | collective-permute-start | bytes 98312 | tf_op jit(solution)/shard_map/while/body/eval_jaxpr/ppermute | solution.py:18
  54.6 1.9 %collective-permute-done.1 = bf16[128,128]{1,0:T(8,128)(2,1)S(1)} collective-permute-done((bf16[128,128]{1,0:T(8,128)(2,1)S(1)}, bf16[128,128]{1,0:T(8,128)(2,1)S(1)}, u32[]{:S(2)}, u32[]{:S(2)}) %collective-permute-start.1) | collective-permute-done | bytes 32800 | tf_op jit(solution)/shard_map/while/body/eval_jaxpr/ppermute | solution.py:18
  57.5 1.9 %collective-permute-start = (bf16[128,128]{1,0:T(8,128)(2,1)S(1)}, bf16[128,128]{1,0:T(8,128)(2,1)S(1)}, u32[]{:S(2)}, u32[]{:S(2)}) collective-permute-start(bf16[128,128]{1,0:T(8,128)(2,1)S(1)} %get-tuple-element.301), channel_id=1, source_target_pairs={{0,4},{4,8},{8,12},{12,16},{16,20},{20,24},{24,28},{1,5},{5,9},{9,... | collective-permute-start | bytes 98312 | tf_op jit(solution)/shard_map/while/body/eval_jaxpr/ppermute | solution.py:18
  59.4 1.9 %collective-permute-start.1 = (bf16[128,128]{1,0:T(8,128)(2,1)S(1)}, bf16[128,128]{1,0:T(8,128)(2,1)S(1)}, u32[]{:S(2)}, u32[]{:S(2)}) collective-permute-start(bf16[128,128]{1,0:T(8,128)(2,1)S(1)} %get-tuple-element.302), channel_id=1, source_target_pairs={{0,4},{4,8},{8,12},{12,16},{16,20},{20,24},{24,28},{1,5},{5,9},{9,... | collective-permute-start | bytes 98312 | tf_op jit(solution)/shard_map/while/body/eval_jaxpr/ppermute | solution.py:18
  62.7 1.9 %collective-permute-done.1 = bf16[128,128]{1,0:T(8,128)(2,1)S(1)} collective-permute-done((bf16[128,128]{1,0:T(8,128)(2,1)S(1)}, bf16[128,128]{1,0:T(8,128)(2,1)S(1)}, u32[]{:S(2)}, u32[]{:S(2)}) %collective-permute-start.1) | collective-permute-done | bytes 32800 | tf_op jit(solution)/shard_map/while/body/eval_jaxpr/ppermute | solution.py:18
  65.6 1.9 %collective-permute-start = (bf16[128,128]{1,0:T(8,128)(2,1)S(1)}, bf16[128,128]{1,0:T(8,128)(2,1)S(1)}, u32[]{:S(2)}, u32[]{:S(2)}) collective-permute-start(bf16[128,128]{1,0:T(8,128)(2,1)S(1)} %get-tuple-element.301), channel_id=1, source_target_pairs={{0,4},{4,8},{8,12},{12,16},{16,20},{20,24},{24,28},{1,5},{5,9},{9,... | collective-permute-start | bytes 98312 | tf_op jit(solution)/shard_map/while/body/eval_jaxpr/ppermute | solution.py:18
  67.6 1.9 %collective-permute-start.1 = (bf16[128,128]{1,0:T(8,128)(2,1)S(1)}, bf16[128,128]{1,0:T(8,128)(2,1)S(1)}, u32[]{:S(2)}, u32[]{:S(2)}) collective-permute-start(bf16[128,128]{1,0:T(8,128)(2,1)S(1)} %get-tuple-element.302), channel_id=1, source_target_pairs={{0,4},{4,8},{8,12},{12,16},{16,20},{20,24},{24,28},{1,5},{5,9},{9,... | collective-permute-start | bytes 98312 | tf_op jit(solution)/shard_map/while/body/eval_jaxpr/ppermute | solution.py:18
  70.9 1.9 %collective-permute-done.1 = bf16[128,128]{1,0:T(8,128)(2,1)S(1)} collective-permute-done((bf16[128,128]{1,0:T(8,128)(2,1)S(1)}, bf16[128,128]{1,0:T(8,128)(2,1)S(1)}, u32[]{:S(2)}, u32[]{:S(2)}) %collective-permute-start.1) | collective-permute-done | bytes 32800 | tf_op jit(solution)/shard_map/while/body/eval_jaxpr/ppermute | solution.py:18
  73.8 1.9 %collective-permute-start = (bf16[128,128]{1,0:T(8,128)(2,1)S(1)}, bf16[128,128]{1,0:T(8,128)(2,1)S(1)}, u32[]{:S(2)}, u32[]{:S(2)}) collective-permute-start(bf16[128,128]{1,0:T(8,128)(2,1)S(1)} %get-tuple-element.301), channel_id=1, source_target_pairs={{0,4},{4,8},{8,12},{12,16},{16,20},{20,24},{24,28},{1,5},{5,9},{9,... | collective-permute-start | bytes 98312 | tf_op jit(solution)/shard_map/while/body/eval_jaxpr/ppermute | solution.py:18
  75.7 1.9 %collective-permute-start.1 = (bf16[128,128]{1,0:T(8,128)(2,1)S(1)}, bf16[128,128]{1,0:T(8,128)(2,1)S(1)}, u32[]{:S(2)}, u32[]{:S(2)}) collective-permute-start(bf16[128,128]{1,0:T(8,128)(2,1)S(1)} %get-tuple-element.302), channel_id=1, source_target_pairs={{0,4},{4,8},{8,12},{12,16},{16,20},{20,24},{24,28},{1,5},{5,9},{9,... | collective-permute-start | bytes 98312 | tf_op jit(solution)/shard_map/while/body/eval_jaxpr/ppermute | solution.py:18
  79.0 1.9 %collective-permute-done.1 = bf16[128,128]{1,0:T(8,128)(2,1)S(1)} collective-permute-done((bf16[128,128]{1,0:T(8,128)(2,1)S(1)}, bf16[128,128]{1,0:T(8,128)(2,1)S(1)}, u32[]{:S(2)}, u32[]{:S(2)}) %collective-permute-start.1) | collective-permute-done | bytes 32800 | tf_op jit(solution)/shard_map/while/body/eval_jaxpr/ppermute | solution.py:18
  81.9 1.9 %collective-permute-start = (bf16[128,128]{1,0:T(8,128)(2,1)S(1)}, bf16[128,128]{1,0:T(8,128)(2,1)S(1)}, u32[]{:S(2)}, u32[]{:S(2)}) collective-permute-start(bf16[128,128]{1,0:T(8,128)(2,1)S(1)} %get-tuple-element.301), channel_id=1, source_target_pairs={{0,4},{4,8},{8,12},{12,16},{16,20},{20,24},{24,28},{1,5},{5,9},{9,... | collective-permute-start | bytes 98312 | tf_op jit(solution)/shard_map/while/body/eval_jaxpr/ppermute | solution.py:18
  83.9 1.9 %collective-permute-start.1 = (bf16[128,128]{1,0:T(8,128)(2,1)S(1)}, bf16[128,128]{1,0:T(8,128)(2,1)S(1)}, u32[]{:S(2)}, u32[]{:S(2)}) collective-permute-start(bf16[128,128]{1,0:T(8,128)(2,1)S(1)} %get-tuple-element.302), channel_id=1, source_target_pairs={{0,4},{4,8},{8,12},{12,16},{16,20},{20,24},{24,28},{1,5},{5,9},{9,... | collective-permute-start | bytes 98312 | tf_op jit(solution)/shard_map/while/body/eval_jaxpr/ppermute | solution.py:18
  87.2 1.9 %collective-permute-done.1 = bf16[128,128]{1,0:T(8,128)(2,1)S(1)} collective-permute-done((bf16[128,128]{1,0:T(8,128)(2,1)S(1)}, bf16[128,128]{1,0:T(8,128)(2,1)S(1)}, u32[]{:S(2)}, u32[]{:S(2)}) %collective-permute-start.1) | collective-permute-done | bytes 32800 | tf_op jit(solution)/shard_map/while/body/eval_jaxpr/ppermute | solution.py:18
  (115 shorter events, 35.4 us)
Async XLA Ops:
  0.0 2.4 %copy-start = (bf16[128,64]{0,1:T(8,128)(2,1)S(1)}, bf16[128,64]{0,1:T(8,128)(2,1)}, u32[]{:S(2)}) copy-start(bf16[128,64]{0,1:T(8,128)(2,1)} %param.11) | copy-start | bytes 49156
  0.8 2.3 %copy-start.1 = (bf16[128,64]{0,1:T(8,128)(2,1)S(1)}, bf16[128,64]{0,1:T(8,128)(2,1)}, u32[]{:S(2)}) copy-start(bf16[128,64]{0,1:T(8,128)(2,1)} %param.12) | copy-start | bytes 49156
  0.9 6.1 %collective-permute-start.3 = (bf16[128,64]{1,0:T(8,128)(2,1)S(1)}, bf16[128,64]{1,0:T(8,128)(2,1)S(1)}, u32[]{:S(2)}, u32[]{:S(2)}) collective-permute-start(bf16[128,64]{1,0:T(8,128)(2,1)S(1)} %copy.42), channel_id=1, source_target_pairs={{0,1},{1,0},{2,3},{3,2},{4,5},{5,4},{6,7},{7,6},{8,9},{9,8},{10,11... | collective-permute-start | bytes 49160 | tf_op jit(solution)/shard_map/ppermute | solution.py:12
  2.5 16.7 %collective-permute-start.2 = (bf16[128,64]{1,0:T(8,128)(2,1)S(1)}, bf16[128,64]{1,0:T(8,128)(2,1)S(1)}, u32[]{:S(2)}, u32[]{:S(2)}) collective-permute-start(bf16[128,64]{1,0:T(8,128)(2,1)S(1)} %copy.39), channel_id=1, source_target_pairs={{0,1},{1,0},{2,3},{3,2},{4,5},{5,4},{6,7},{7,6},{8,9},{9,8},{10,11... | collective-permute-start | bytes 49160 | tf_op jit(solution)/shard_map/ppermute | solution.py:12
  3.2 29.2 %collective-permute-start.4 = (bf16[128,64]{1,0:T(8,128)(2,1)S(1)}, bf16[128,64]{1,0:T(8,128)(2,1)S(1)}, u32[]{:S(2)}, u32[]{:S(2)}) collective-permute-start(bf16[128,64]{1,0:T(8,128)(2,1)S(1)} %copy.46), channel_id=1, source_target_pairs={{0,1},{1,0},{2,3},{3,2},{4,5},{5,4},{6,7},{7,6},{8,9},{9,8},{10,11... | collective-permute-start | bytes 49160 | tf_op jit(solution)/shard_map/ppermute | solution.py:12
  4.9 0.7 copy-start.2
  33.1 5.2 %collective-permute-start = (bf16[128,128]{1,0:T(8,128)(2,1)S(1)}, bf16[128,128]{1,0:T(8,128)(2,1)S(1)}, u32[]{:S(2)}, u32[]{:S(2)}) collective-permute-start(bf16[128,128]{1,0:T(8,128)(2,1)S(1)} %get-tuple-element.301), channel_id=1, source_target_pairs={{0,4},{4,8},{8,12},{12,16},{16,20},{20,24},{24,28},{1,5},{5,9},{9,... | collective-permute-start | bytes 98312 | tf_op jit(solution)/shard_map/while/body/eval_jaxpr/ppermute | solution.py:18
  35.0 5.2 %collective-permute-start.1 = (bf16[128,128]{1,0:T(8,128)(2,1)S(1)}, bf16[128,128]{1,0:T(8,128)(2,1)S(1)}, u32[]{:S(2)}, u32[]{:S(2)}) collective-permute-start(bf16[128,128]{1,0:T(8,128)(2,1)S(1)} %get-tuple-element.302), channel_id=1, source_target_pairs={{0,4},{4,8},{8,12},{12,16},{16,20},{20,24},{24,28},{1,5},{5,9},{9,... | collective-permute-start | bytes 98312 | tf_op jit(solution)/shard_map/while/body/eval_jaxpr/ppermute | solution.py:18
  41.2 5.3 %collective-permute-start = (bf16[128,128]{1,0:T(8,128)(2,1)S(1)}, bf16[128,128]{1,0:T(8,128)(2,1)S(1)}, u32[]{:S(2)}, u32[]{:S(2)}) collective-permute-start(bf16[128,128]{1,0:T(8,128)(2,1)S(1)} %get-tuple-element.301), channel_id=1, source_target_pairs={{0,4},{4,8},{8,12},{12,16},{16,20},{20,24},{24,28},{1,5},{5,9},{9,... | collective-permute-start | bytes 98312 | tf_op jit(solution)/shard_map/while/body/eval_jaxpr/ppermute | solution.py:18
  43.1 5.2 %collective-permute-start.1 = (bf16[128,128]{1,0:T(8,128)(2,1)S(1)}, bf16[128,128]{1,0:T(8,128)(2,1)S(1)}, u32[]{:S(2)}, u32[]{:S(2)}) collective-permute-start(bf16[128,128]{1,0:T(8,128)(2,1)S(1)} %get-tuple-element.302), channel_id=1, source_target_pairs={{0,4},{4,8},{8,12},{12,16},{16,20},{20,24},{24,28},{1,5},{5,9},{9,... | collective-permute-start | bytes 98312 | tf_op jit(solution)/shard_map/while/body/eval_jaxpr/ppermute | solution.py:18
  49.3 5.3 %collective-permute-start = (bf16[128,128]{1,0:T(8,128)(2,1)S(1)}, bf16[128,128]{1,0:T(8,128)(2,1)S(1)}, u32[]{:S(2)}, u32[]{:S(2)}) collective-permute-start(bf16[128,128]{1,0:T(8,128)(2,1)S(1)} %get-tuple-element.301), channel_id=1, source_target_pairs={{0,4},{4,8},{8,12},{12,16},{16,20},{20,24},{24,28},{1,5},{5,9},{9,... | collective-permute-start | bytes 98312 | tf_op jit(solution)/shard_map/while/body/eval_jaxpr/ppermute | solution.py:18
  51.3 5.2 %collective-permute-start.1 = (bf16[128,128]{1,0:T(8,128)(2,1)S(1)}, bf16[128,128]{1,0:T(8,128)(2,1)S(1)}, u32[]{:S(2)}, u32[]{:S(2)}) collective-permute-start(bf16[128,128]{1,0:T(8,128)(2,1)S(1)} %get-tuple-element.302), channel_id=1, source_target_pairs={{0,4},{4,8},{8,12},{12,16},{16,20},{20,24},{24,28},{1,5},{5,9},{9,... | collective-permute-start | bytes 98312 | tf_op jit(solution)/shard_map/while/body/eval_jaxpr/ppermute | solution.py:18
  57.5 5.3 %collective-permute-start = (bf16[128,128]{1,0:T(8,128)(2,1)S(1)}, bf16[128,128]{1,0:T(8,128)(2,1)S(1)}, u32[]{:S(2)}, u32[]{:S(2)}) collective-permute-start(bf16[128,128]{1,0:T(8,128)(2,1)S(1)} %get-tuple-element.301), channel_id=1, source_target_pairs={{0,4},{4,8},{8,12},{12,16},{16,20},{20,24},{24,28},{1,5},{5,9},{9,... | collective-permute-start | bytes 98312 | tf_op jit(solution)/shard_map/while/body/eval_jaxpr/ppermute | solution.py:18
  59.4 5.2 %collective-permute-start.1 = (bf16[128,128]{1,0:T(8,128)(2,1)S(1)}, bf16[128,128]{1,0:T(8,128)(2,1)S(1)}, u32[]{:S(2)}, u32[]{:S(2)}) collective-permute-start(bf16[128,128]{1,0:T(8,128)(2,1)S(1)} %get-tuple-element.302), channel_id=1, source_target_pairs={{0,4},{4,8},{8,12},{12,16},{16,20},{20,24},{24,28},{1,5},{5,9},{9,... | collective-permute-start | bytes 98312 | tf_op jit(solution)/shard_map/while/body/eval_jaxpr/ppermute | solution.py:18
  65.6 5.3 %collective-permute-start = (bf16[128,128]{1,0:T(8,128)(2,1)S(1)}, bf16[128,128]{1,0:T(8,128)(2,1)S(1)}, u32[]{:S(2)}, u32[]{:S(2)}) collective-permute-start(bf16[128,128]{1,0:T(8,128)(2,1)S(1)} %get-tuple-element.301), channel_id=1, source_target_pairs={{0,4},{4,8},{8,12},{12,16},{16,20},{20,24},{24,28},{1,5},{5,9},{9,... | collective-permute-start | bytes 98312 | tf_op jit(solution)/shard_map/while/body/eval_jaxpr/ppermute | solution.py:18
  67.6 5.2 %collective-permute-start.1 = (bf16[128,128]{1,0:T(8,128)(2,1)S(1)}, bf16[128,128]{1,0:T(8,128)(2,1)S(1)}, u32[]{:S(2)}, u32[]{:S(2)}) collective-permute-start(bf16[128,128]{1,0:T(8,128)(2,1)S(1)} %get-tuple-element.302), channel_id=1, source_target_pairs={{0,4},{4,8},{8,12},{12,16},{16,20},{20,24},{24,28},{1,5},{5,9},{9,... | collective-permute-start | bytes 98312 | tf_op jit(solution)/shard_map/while/body/eval_jaxpr/ppermute | solution.py:18
  73.8 5.3 %collective-permute-start = (bf16[128,128]{1,0:T(8,128)(2,1)S(1)}, bf16[128,128]{1,0:T(8,128)(2,1)S(1)}, u32[]{:S(2)}, u32[]{:S(2)}) collective-permute-start(bf16[128,128]{1,0:T(8,128)(2,1)S(1)} %get-tuple-element.301), channel_id=1, source_target_pairs={{0,4},{4,8},{8,12},{12,16},{16,20},{20,24},{24,28},{1,5},{5,9},{9,... | collective-permute-start | bytes 98312 | tf_op jit(solution)/shard_map/while/body/eval_jaxpr/ppermute | solution.py:18
  75.7 5.2 %collective-permute-start.1 = (bf16[128,128]{1,0:T(8,128)(2,1)S(1)}, bf16[128,128]{1,0:T(8,128)(2,1)S(1)}, u32[]{:S(2)}, u32[]{:S(2)}) collective-permute-start(bf16[128,128]{1,0:T(8,128)(2,1)S(1)} %get-tuple-element.302), channel_id=1, source_target_pairs={{0,4},{4,8},{8,12},{12,16},{16,20},{20,24},{24,28},{1,5},{5,9},{9,... | collective-permute-start | bytes 98312 | tf_op jit(solution)/shard_map/while/body/eval_jaxpr/ppermute | solution.py:18
  81.9 5.3 %collective-permute-start = (bf16[128,128]{1,0:T(8,128)(2,1)S(1)}, bf16[128,128]{1,0:T(8,128)(2,1)S(1)}, u32[]{:S(2)}, u32[]{:S(2)}) collective-permute-start(bf16[128,128]{1,0:T(8,128)(2,1)S(1)} %get-tuple-element.301), channel_id=1, source_target_pairs={{0,4},{4,8},{8,12},{12,16},{16,20},{20,24},{24,28},{1,5},{5,9},{9,... | collective-permute-start | bytes 98312 | tf_op jit(solution)/shard_map/while/body/eval_jaxpr/ppermute | solution.py:18
  83.9 5.2 %collective-permute-start.1 = (bf16[128,128]{1,0:T(8,128)(2,1)S(1)}, bf16[128,128]{1,0:T(8,128)(2,1)S(1)}, u32[]{:S(2)}, u32[]{:S(2)}) collective-permute-start(bf16[128,128]{1,0:T(8,128)(2,1)S(1)} %get-tuple-element.302), channel_id=1, source_target_pairs={{0,4},{4,8},{8,12},{12,16},{16,20},{20,24},{24,28},{1,5},{5,9},{9,... | collective-permute-start | bytes 98312 | tf_op jit(solution)/shard_map/while/body/eval_jaxpr/ppermute | solution.py:18
  89.6 0.7 copy-start.3
where the time goes:
time: 92 us; the launch traced here: 91.4 us
  starting transfers between devices  30.7 us (33%)
  waiting for transfers between devices  23.1 us (25%)
  other arithmetic  22 us (24%)
  matrix products  9.75 us (11%)
  local copies, waits for them, and re-layouts  5.09 us (6%)
    ppermute x14, starting transfers between devices, shifted(): return lax.ppermute(shard, axis, pairs)  27 us
    ppermute x14, waiting for transfers between devices, shifted(): return lax.ppermute(shard, axis, pairs)  23.1 us
    another operation x2, other arithmetic, segment_terms(): jax.scipy.linalg.solve_triangular(identity + intersections * beta[None, :...  9.81 us
    another operation x1, other arithmetic, segment_terms(): jax.scipy.linalg.solve_triangular(identity + beta[:, None] * intersection...  9.81 us
    ppermute x3, starting transfers between devices, partner(): return lax.ppermute(value, axis, pairs)  3.71 us
    unnamed x12, local copies, waits for them, and re-layouts  3.49 us
    dot_general x6, matrix products, absorb(): jnp.dot(block_exp.astype(jnp.bfloat16), value_block, preferred_element_ty...  2.59 us
  transfers between devices with their start and end apart: 17, of which 14 were waited for; matrix products, arithmetic and copies ran while one was open for 30% of the time, Pallas kernels for 0%

commit v1 on v0

v1 whole, which is shorter than its diff:
```python
import functools

import jax
import jax.numpy as jnp
from jax import lax
from jax.experimental import pallas as pl
from jax.experimental.pallas import tpu as pltpu
from jax.sharding import PartitionSpec as P

WIDE = jnp.float32
NARROW = jnp.bfloat16
MASKED = -1e30


def halves(x):
    top = x.astype(NARROW)
    return top, (x - top.astype(WIDE)).astype(NARROW)


def dot(a, b):
    return jnp.dot(a, b, preferred_element_type=WIDE)


def dot3(a, b):
    a_top, a_low = a
    b_top, b_low = b
    return dot(
        jnp.concatenate([a_top, a_low, a_top], axis=1),
        jnp.concatenate([b_top, b_top, b_low], axis=0),
    )


def prepare(own_ref, other_ref, beta_ref, pack_ref, solved_ref, sides_ref, coef_ref, full_ref):
    half, length = own_ref.shape[0] // 3, own_ref.shape[1]
    width = 2 * half
    place = lax.axis_index("head")
    parity = place % 2
    for part in range(3):
        rows = pl.ds(part * half, half)
        full_ref[part, pl.ds(parity * half, half), :] = own_ref[rows, :]
        full_ref[part, pl.ds((1 - parity) * half, half), :] = other_ref[rows, :]
    keys_t, values_t, dirs_t = full_ref[0], full_ref[1], full_ref[2]
    dirs_wide = dirs_t.astype(WIDE)
    dirs = dirs_wide.T.astype(NARROW)
    power = jnp.sum(dirs_wide * dirs_wide, axis=0, keepdims=True) + 1e-06
    coef = beta_ref[pl.ds(place // 2, 1), :] / power

    row = lax.broadcasted_iota(jnp.int32, (length, length), 0)
    col = lax.broadcasted_iota(jnp.int32, (length, length), 1)
    sides = jnp.concatenate([dirs_t, keys_t], axis=1)
    meets = dot(dirs, sides)
    below = jnp.where(row > col, meets[:, :length] * coef, 0.0)
    reach = jnp.where(row > col, meets[:, length:], 0.0)

    inverse = jnp.where(row == col, 1.0, 0.0) - jnp.where((row ^ col) == 1, below, 0.0)
    block = 2
    while block < length:
        joint = jnp.where((row // block) ^ (col // block) == 1, below, 0.0)
        parts = halves(inverse)
        inverse = inverse - dot3(parts, halves(dot3(halves(joint), parts)))
        block *= 2

    top, low = halves(inverse)
    reach_top, reach_low = halves(reach)
    right = jnp.concatenate([reach_top, dirs], axis=1)
    solved = dot(jnp.concatenate([top, low], axis=1), jnp.concatenate([right, right], axis=0))
    solved_reach = solved[:, :length] + dot(top, reach_low)
    solved = jnp.concatenate([solved_reach, solved[:, length:]], axis=1)
    solved_parts = halves(solved)
    change = dot3(halves(dirs_wide * coef), solved_parts)
    pack_ref[:, :length] = (keys_t.astype(WIDE) - change[:, :length]).astype(NARROW)
    row_w = lax.broadcasted_iota(jnp.int32, (width, width), 0)
    col_w = lax.broadcasted_iota(jnp.int32, (width, width), 1)
    unit = jnp.where(row_w == col_w, 1.0, 0.0)
    pack_ref[:, length : length + width] = (unit - change[:, length:]).astype(NARROW)
    pack_ref[:, length + width :] = values_t.astype(WIDE).T.astype(NARROW)
    solved_ref[0] = solved_parts[0]
    solved_ref[1] = solved_parts[1]
    sides_ref[...] = sides
    coef_ref[...] = jnp.broadcast_to(coef, coef_ref.shape)


def own_segment(queries_ref, solved_ref, sides_ref, coef_ref, moved_ref, local_ref):
    length = queries_ref.shape[0]
    width = sides_ref.shape[0]
    heads = queries_ref.shape[1] // width
    coef = coef_ref[:1, :]
    sides = sides_ref[...]
    top, low = solved_ref[0], solved_ref[1]
    right = jnp.concatenate([top, top, low], axis=0)
    row = lax.broadcasted_iota(jnp.int32, (length, length), 0)
    col = lax.broadcasted_iota(jnp.int32, (length, length), 1)
    for head in range(heads):
        cols = pl.ds(head * width, width)
        query = queries_ref[:, cols]
        plain = dot(query, sides)
        met = jnp.where(row >= col, plain[:, :length] * coef, 0.0)
        met_top, met_low = halves(met)
        change = dot(jnp.concatenate([met_top, met_low, met_top], axis=1), right)
        moved_ref[:, cols] = (query.astype(WIDE) - change[:, length:]).astype(NARROW)
        scores = (plain[:, length:] - change[:, :length]) * width ** (-0.5)
        local_ref[:, pl.ds(head * length, length)] = jnp.where(row >= col, scores, MASKED)


def attend(moved_ref, local_ref, all_ref, gain_ref, out_ref, keys_ref, values_ref):
    length = moved_ref.shape[0]
    width = gain_ref.shape[1]
    heads = moved_ref.shape[1] // width
    segments = all_ref.shape[0] // length
    place = lax.axis_index("seq")
    travel = None
    for step in range(1, segments):
        rows = pl.ds(pl.multiple_of(jnp.maximum(place - step, 0) * length, length), length)
        block = all_ref[rows, pl.ds(0, length + width)]
        at = pl.ds((step - 1) * length, length)
        values_ref[at, :] = all_ref[rows, pl.ds(length + width, width)]
        if step == 1:
            keys_ref[:, at] = block[:, :length]
            travel = block[:, length:].astype(WIDE)
        else:
            both = dot(
                jnp.concatenate(halves(travel), axis=1), jnp.concatenate([block, block], axis=0)
            )
            keys_ref[:, at] = both[:, :length].astype(NARROW)
            travel = both[:, length:]
    last = pl.ds((segments - 1) * length, length)
    values_ref[last, :] = all_ref[
        pl.ds(pl.multiple_of(place * length, length), length), pl.ds(length + width, width)
    ]
    gain = gain_ref[...]
    scale = width ** (-0.5)
    for head in range(heads):
        cols = pl.ds(head * width, width)
        cross = dot(moved_ref[:, cols], keys_ref[...]) * scale
        column = lax.broadcasted_iota(jnp.int32, cross.shape, 1)
        cross = jnp.where(column < place * length, cross, MASKED)
        scores = jnp.concatenate([cross, local_ref[:, pl.ds(head * length, length)]], axis=1)
        peak = jnp.max(scores, axis=1, keepdims=True)
        weights = jnp.exp(scores - peak)
        total = jnp.sum(weights, axis=1, keepdims=True)
        mixed = dot(weights.astype(NARROW), values_ref[...]) / total
        strength = lax.rsqrt(jnp.mean(mixed * mixed, axis=1, keepdims=True) + 1e-06)
        out_ref[:, cols] = (mixed * strength * gain).astype(NARROW)


def call(kernel, outs, scratch=(), flops=1e8):
    return pl.pallas_call(
        kernel,
        out_shape=outs,
        scratch_shapes=list(scratch),
        cost_estimate=pl.CostEstimate(
            flops=int(flops), bytes_accessed=1 << 20, transcendentals=1 << 17
        ),
    )


def shards(queries, keys, values, directions, beta, gain):
    length, half = directions.shape
    width = 2 * half
    heads = queries.shape[1] // width
    segments = lax.axis_size("seq")
    own = jnp.concatenate([keys.T, values.T, directions.T], axis=0)
    places = range(lax.axis_size("head"))
    other = lax.ppermute(own, "head", [(place, place ^ 1) for place in places])
    shape = jax.ShapeDtypeStruct
    pack, solved, sides, coef = call(
        prepare,
        (
            shape((width, 2 * length + width), NARROW),
            shape((2, length, length + width), NARROW),
            shape((width, 2 * length), NARROW),
            shape((8, length), WIDE),
        ),
        [pltpu.VMEM((3, width, length), NARROW)],
    )(own, other, beta.T)
    everyone = lax.all_gather(pack, "seq", tiled=True)
    moved, local = call(
        own_segment,
        (shape((length, heads * width), NARROW), shape((length, heads * length), WIDE)),
    )(queries, solved, sides, coef)
    return call(
        attend,
        shape((length, heads * width), NARROW),
        [
            pltpu.VMEM((width, (segments - 1) * length), NARROW),
            pltpu.VMEM((segments * length, width), NARROW),
        ],
        flops=1e9,
    )(moved, local, everyone, gain.reshape(1, -1))


def solution(mesh):
    placed = (
        P("seq", "head"),
        P("seq", "head"),
        P("seq", "head"),
        P("seq", "head"),
        P("seq", None),
        P(),
    )
    return jax.shard_map(
        shards, mesh=mesh, in_specs=placed, out_specs=P("seq", "head"), check_vma=False
    )
```

time: 92 us -> 37.2 us (0.40)
  the two profiles are of different devices: /device:TPU:24 before, /device:TPU:0 now
where the time goes in v1:
time: 37.2 us; the launch traced here: 36.9 us
  blocking collectives  17.6 us (47%)
  Pallas kernels  12.9 us (35%)
  starting transfers between devices  2.97 us (8%)
  waiting for transfers between devices  2.07 us (6%)
  other arithmetic  0.76 us (2%)
  local copies, waits for them, and re-layouts  0.61 us (2%)
    all_gather x1, blocking collectives, shards(): everyone = lax.all_gather(pack, 'seq', tiled=True)  17.6 us
    pallas_call x1, Pallas kernels, shards(): call(attend, shape((length, heads * width), NARROW), [pltpu.VMEM((width,...  6.04 us
    pallas_call x1, Pallas kernels, shards(): call(prepare, (shape((width, 2 * length + width), NARROW), shape((2, leng...  3.97 us
    ppermute x1, starting transfers between devices, shards(): other = lax.ppermute(own, 'head', [(place, place ^ 1) for place in places])  2.97 us
    pallas_call x1, Pallas kernels, shards(): call(own_segment, (shape((length, heads * width), NARROW), shape((length,...  2.9 us
    ppermute x1, waiting for transfers between devices, shards(): other = lax.ppermute(own, 'head', [(place, place ^ 1) for place in places])  2.07 us
    concatenate x1, other arithmetic, shards(): own = jnp.concatenate([keys.T, values.T, directions.T], axis=0)  0.76 us
  transfers between devices with their start and end apart: 1, of which 1 were waited for; matrix products, arithmetic and copies ran while one was open for 0% of the time, Pallas kernels for 0%

profile of v1, /device:TPU:0, one launch (start us, length us, event | category | flops | bytes accessed | tf_op | source)
XLA Modules:
  0.0 36.9 jit_solution(6682527322686045109)
XLA Ops:
  0.0 0.8 %pad_maximum_fusion.own_ref = bf16[192,128]{1,0:T(8,128)(2,1)S(1)} fusion(bf16[64,128]{1,0:T(8,128)(2,1)} %bitcast.5, bf16[64,128]{1,0:T(8,128)(2,1)} %bitcast.6, bf16[64,128]{1,0:T(8,128)(2,1)} %bitcast.7), kind=kLoop, calls=%fused_computation | loop fusion | flops 147456 | bytes 98304 | tf_op jit(solution)/shard_map/concatenate | solution.py:162
  0.8 0.0 copy-start
  0.8 3.0 %collective-permute-start = (bf16[192,128]{1,0:T(8,128)(2,1)S(1)}, bf16[192,128]{1,0:T(8,128)(2,1)S(1)}, u32[]{:S(2)}, u32[]{:S(2)}) collective-permute-start(bf16[192,128]{1,0:T(8,128)(2,1)S(1)} %pad_maximum_fusion.own_ref), channel_id=1, source_target_pairs={{0,1},{1,0},{2,3},{3,2},{4,5},{5,4},{6,7},{7,6},{8,9},{9,8},{10,11... | collective-permute-start | bytes 147464 | tf_op jit(solution)/shard_map/ppermute | solution.py:164
  3.7 2.1 %collective-permute-done.other_ref = bf16[192,128]{1,0:T(8,128)(2,1)S(1)} collective-permute-done((bf16[192,128]{1,0:T(8,128)(2,1)S(1)}, bf16[192,128]{1,0:T(8,128)(2,1)S(1)}, u32[]{:S(2)}, u32[]{:S(2)}) %collective-permute-start) | collective-permute-done | bytes 49184 | tf_op jit(solution)/shard_map/ppermute | solution.py:164
  5.8 0.0 copy-start.1
  5.8 0.0 copy-done
  5.8 0.6 %copy-done.1 = bf16[192,128]{1,0:T(8,128)(2,1)} copy-done((bf16[192,128]{1,0:T(8,128)(2,1)}, bf16[192,128]{1,0:T(8,128)(2,1)S(1)}, u32[]{:S(2)}) %copy-start.1) | copy-done | bytes 49176
  6.4 4.0 %shard_map.64 = (bf16[128,384]{1,0:T(8,128)(2,1)}, bf16[2,128,256]{2,1,0:T(8,128)(2,1)}, bf16[128,256]{1,0:T(8,128)(2,1)}, f32[8,128]{1,0:T(8,128)}) custom-call(bf16[192,128]{1,0:T(8,128)(2,1)} %copy-done, bf16[192,128]{1,0:T(8,128)(2,1)} %copy-done.1, f32[2,128]{1,0:T(2,128)} %bitcast.8), custom_call_target="tpu_custom_call" | custom-call | flops 100000000 | bytes 1048576 | tf_op jit(solution)/shard_map/pallas_call | solution.py:166
  10.4 17.6 %all_gather.3.all_ref = bf16[1024,384]{1,0:T(8,128)(2,1)} all-gather(bf16[128,384]{1,0:T(8,128)(2,1)} %get-tuple-element.16), channel_id=1, replica_groups=mesh['seq'=8,'head'=4] {'seq'}, dimensions={0}, use_global_device_ids=true | all-gather | bytes 884736 | tf_op jit(solution)/shard_map/all_gather | solution.py:176
  27.9 2.9 %shard_map.65 = (bf16[128,1024]{1,0:T(8,128)(2,1)}, f32[128,1024]{1,0:T(8,128)}) custom-call(bf16[128,1024]{1,0:T(8,128)(2,1)} %queries_ref.1, bf16[2,128,256]{2,1,0:T(8,128)(2,1)} %get-tuple-element.11.solved_ref, bf16[128,256]{1,0:T(8,128)(2,1)} %get-tuple-element.12.sides_ref, f32[8,128]{1,0:T(8,128)} %get-tuple-element.13.coef_ref), custom_call_target="tpu_custom_call" | custom-call | flops 100000000 | bytes 1048576 | tf_op jit(solution)/shard_map/pallas_call | solution.py:177
  30.8 6.0 %shard_map.66 = bf16[128,1024]{1,0:T(8,128)(2,1)} custom-call(bf16[128,1024]{1,0:T(8,128)(2,1)} %get-tuple-element.14.moved_ref, f32[128,1024]{1,0:T(8,128)} %get-tuple-element.15.local_ref, bf16[1024,384]{1,0:T(8,128)(2,1)} %all_gather.3.all_ref, f32[1,128]{1,0:T(1,128)} %bitcast.9), custom_call_target="tpu_custom_call" | custom-call | flops 1000000000 | bytes 1048576 | tf_op jit(solution)/shard_map/pallas_call | solution.py:181
Async XLA Ops:
  0.8 5.0 %copy-start = (bf16[192,128]{1,0:T(8,128)(2,1)}, bf16[192,128]{1,0:T(8,128)(2,1)S(1)}, u32[]{:S(2)}) copy-start(bf16[192,128]{1,0:T(8,128)(2,1)S(1)} %pad_maximum_fusion.own_ref) | copy-start | bytes 147460
  0.8 5.0 %collective-permute-start = (bf16[192,128]{1,0:T(8,128)(2,1)S(1)}, bf16[192,128]{1,0:T(8,128)(2,1)S(1)}, u32[]{:S(2)}, u32[]{:S(2)}) collective-permute-start(bf16[192,128]{1,0:T(8,128)(2,1)S(1)} %pad_maximum_fusion.own_ref), channel_id=1, source_target_pairs={{0,1},{1,0},{2,3},{3,2},{4,5},{5,4},{6,7},{7,6},{8,9},{9,8},{10,11... | collective-permute-start | bytes 147464 | tf_op jit(solution)/shard_map/ppermute | solution.py:164
  5.8 0.6 %copy-start.1 = (bf16[192,128]{1,0:T(8,128)(2,1)}, bf16[192,128]{1,0:T(8,128)(2,1)S(1)}, u32[]{:S(2)}) copy-start(bf16[192,128]{1,0:T(8,128)(2,1)S(1)} %collective-permute-done.other_ref) | copy-start | bytes 147460

commit v2 on v1

--- a/solution.py
+++ b/solution.py
@@ -1,4 +1,4 @@
-import functools
+import math
 
 import jax
 import jax.numpy as jnp
@@ -6,6 +6,7 @@
 from jax.experimental import pallas as pl
 from jax.experimental.pallas import tpu as pltpu
 from jax.sharding import PartitionSpec as P
+
 
 WIDE = jnp.float32
 NARROW = jnp.bfloat16
@@ -43,7 +44,7 @@
     dirs_wide = dirs_t.astype(WIDE)
     dirs = dirs_wide.T.astype(NARROW)
     power = jnp.sum(dirs_wide * dirs_wide, axis=0, keepdims=True) + 1e-06
-    coef = beta_ref[pl.ds(place // 2, 1), :] / power
+    coef = beta_ref[...] / power
 
     row = lax.broadcasted_iota(jnp.int32, (length, length), 0)
     col = lax.broadcasted_iota(jnp.int32, (length, length), 1)
@@ -80,7 +81,9 @@
     coef_ref[...] = jnp.broadcast_to(coef, coef_ref.shape)
 
 
-def own_segment(queries_ref, solved_ref, sides_ref, coef_ref, moved_ref, local_ref):
+def own_segment(
+    queries_ref, solved_ref, sides_ref, coef_ref, pack_ref, moved_ref, peak_ref, sum_ref, mix_ref
+):
     length = queries_ref.shape[0]
     width = sides_ref.shape[0]
     heads = queries_ref.shape[1] // width
@@ -88,6 +91,7 @@
     sides = sides_ref[...]
     top, low = solved_ref[0], solved_ref[1]
     right = jnp.concatenate([top, top, low], axis=0)
+    values = counted(pack_ref[:, length + width :])
     row = lax.broadcasted_iota(jnp.int32, (length, length), 0)
     col = lax.broadcasted_iota(jnp.int32, (length, length), 1)
     for head in range(heads):
@@ -98,56 +102,133 @@
         met_top, met_low = halves(met)
         change = dot(jnp.concatenate([met_top, met_low, met_top], axis=1), right)
         moved_ref[:, cols] = (query.astype(WIDE) - change[:, length:]).astype(NARROW)
-        scores = (plain[:, length:] - change[:, :length]) * width ** (-0.5)
-        local_ref[:, pl.ds(head * length, length)] = jnp.where(row >= col, scores, MASKED)
-
-
-def attend(moved_ref, local_ref, all_ref, gain_ref, out_ref, keys_ref, values_ref):
-    length = moved_ref.shape[0]
-    width = gain_ref.shape[1]
+        scores = jnp.where(row >= col, plain[:, length:] - change[:, :length], MASKED)
+        peak = jnp.max(scores, axis=1, keepdims=True)
+        mixed = dot(powers(scores, peak, width).astype(NARROW), values)
+        peak_ref[:, cols] = jnp.broadcast_to(peak, (length, width))
+        mix_ref[:, cols] = mixed[:, :width]
+        sum_ref[:, cols] = mixed[:, width:]
+
+
+def counted(values):
+    return jnp.concatenate([values, jnp.ones_like(values)], axis=1)
+
+
+def powers(scores, peak, width):
+    return jnp.exp2((scores - peak) * (width ** (-0.5) * math.log2(math.e)))
+
+
+def carry(travel, block, length):
+    both = dot(jnp.concatenate(halves(travel), axis=1), jnp.concatenate([block, block], axis=0))
+    return both[:, :length].astype(NARROW), both[:, length:]
+
+
+def take_in(head, moved_ref, keys, values, peak, total, mix, width):
+    scores = dot(moved_ref[:, pl.ds(head * width, width)], keys)
+    above = jnp.maximum(peak, jnp.max(scores, axis=1, keepdims=True))
+    fade = powers(peak, above, width)
+    mixed = dot(powers(scores, above[:, :1], width).astype(NARROW), values)
+    return above, total * fade + mixed[:, width:], mix * fade + mixed[:, :width]
+
+
+def attend(*refs):
+    moved_ref, peak_ref, sum_ref, mix_ref, gain_hbm, mate_ref = refs[:6]
+    out_ref, keys_ref, values_ref, done_ref, gain_ref, sem, gain_sem = refs[-7:]
+    far = refs[6:-7]
+    width, length = keys_ref.shape[0], moved_ref.shape[0]
     heads = moved_ref.shape[1] // width
-    segments = all_ref.shape[0] // length
+    chips = len(far) // 2
     place = lax.axis_index("seq")
-    travel = None
-    for step in range(1, segments):
-        rows = pl.ds(pl.multiple_of(jnp.maximum(place - step, 0) * length, length), length)
-        block = all_ref[rows, pl.ds(0, length + width)]
-        at = pl.ds((step - 1) * length, length)
-        values_ref[at, :] = all_ref[rows, pl.ds(length + width, width)]
-        if step == 1:
-            keys_ref[:, at] = block[:, :length]
-            travel = block[:, length:].astype(WIDE)
+    core = place % 2
+    chip_place = place // 2
+    fetch = pltpu.make_async_copy(gain_hbm, gain_ref, gain_sem)
+    fetch.start()
+
+    def grab(ref, slot):
+        if isinstance(ref, tuple):
+            block = jnp.where(core == 1, ref[0][...], ref[1][...])
         else:
-            both = dot(
-                jnp.concatenate(halves(travel), axis=1), jnp.concatenate([block, block], axis=0)
+            block = ref[...]
+        at = pl.ds(slot * length, length)
+        values_ref[at, :] = counted(block[:, length + width :])
+        return block[:, : length + width], at
+
+    def state(head):
+        cols = pl.ds(head * width, width)
+        return peak_ref[:, cols], sum_ref[:, cols], mix_ref[:, cols]
+
+    def finish(head, total, mix):
+        cols = pl.ds(head * width, width)
+        mixed = mix / total
+        strength = lax.rsqrt(jnp.mean(mixed * mixed, axis=1, keepdims=True) + 1e-06)
+        done_ref[:, cols] = (mixed * strength * gain_ref[...]).astype(NARROW)
+        pltpu.make_async_copy(
+            done_ref.at[:, cols], out_ref.at[:, cols], sem.at[head]
+        ).start()
+
+    @pl.when(chip_place > 0)
+    def _():
+        row = lax.broadcasted_iota(jnp.int32, (width, width), 0)
+        col = lax.broadcasted_iota(jnp.int32, (width, width), 1)
+        order = [mate_ref]
+        for chip in range(chips):
+            straight, crossed = far[2 * chip], far[2 * chip + 1]
+            order += [(straight, crossed), (crossed, straight)]
+        travel = None
+        for slot, ref in enumerate(order):
+            block, at = grab(ref, slot)
+            if slot == 0:
+                keys_ref[:, at] = block[:, :length]
+                near = block[:, length:].astype(WIDE)
+                travel = jnp.where(core == 1, near, jnp.where(row == col, 1.0, 0.0))
+            else:
+                keys_ref[:, at], travel = carry(travel, block, length)
+        first, last = (1 - core) * length, (1 + 2 * chip_place) * length
+        fetch.wait()
+        for head in range(heads):
+            peak, total, mix = state(head)
+            scores = dot(moved_ref[:, pl.ds(head * width, width)], keys_ref[...])
+            column = lax.broadcasted_iota(jnp.int32, scores.shape, 1)
+            scores = jnp.where((column >= first) & (column < last), scores, MASKED)
+            above = jnp.maximum(peak, jnp.max(scores, axis=1, keepdims=True))
+            fade = powers(peak, above, width)
+            mixed = dot(powers(scores, above[:, :1], width).astype(NARROW), values_ref[...])
+            finish(head, total * fade + mixed[:, width:], mix * fade + mixed[:, :width])
+
+    @pl.when((chip_place == 0) & (core == 1))
+    def _():
+        block, at = grab(mate_ref, 0)
+        fetch.wait()
+        for head in range(heads):
+            _, total, mix = take_in(
+                head, moved_ref, block[:, :length], values_ref[at, :], *state(head), width
             )
-            keys_ref[:, at] = both[:, :length].astype(NARROW)
-            travel = both[:, length:]
-    last = pl.ds((segments - 1) * length, length)
-    values_ref[last, :] = all_ref[
-        pl.ds(pl.multiple_of(place * length, length), length), pl.ds(length + width, width)
-    ]
-    gain = gain_ref[...]
-    scale = width ** (-0.5)
+            finish(head, total, mix)
+
+    @pl.when((chip_place == 0) & (core == 0))
+    def _():
+        fetch.wait()
+        for head in range(heads):
+            _, total, mix = state(head)
+            finish(head, total, mix)
+
     for head in range(heads):
         cols = pl.ds(head * width, width)
-        cross = dot(moved_ref[:, cols], keys_ref[...]) * scale
-        column = lax.broadcasted_iota(jnp.int32, cross.shape, 1)
-        cross = jnp.where(column < place * length, cross, MASKED)
-        scores = jnp.concatenate([cross, local_ref[:, pl.ds(head * length, length)]], axis=1)
-        peak = jnp.max(scores, axis=1, keepdims=True)
-        weights = jnp.exp(scores - peak)
-        total = jnp.sum(weights, axis=1, keepdims=True)
-        mixed = dot(weights.astype(NARROW), values_ref[...]) / total
-        strength = lax.rsqrt(jnp.mean(mixed * mixed, axis=1, keepdims=True) + 1e-06)
-        out_ref[:, cols] = (mixed * strength * gain).astype(NARROW)
-
-
-def call(kernel, outs, scratch=(), flops=1e8):
+        pltpu.make_async_copy(done_ref.at[:, cols], out_ref.at[:, cols], sem.at[head]).wait()
+
+
+LOCAL = pl.BlockSpec(memory_space=pltpu.VMEM)
+ANYWHERE = pl.BlockSpec(memory_space=pltpu.HBM)
+
+
+def call(kernel, outs, count, scratch=(), flops=1e8, spots=None, far=()):
     return pl.pallas_call(
         kernel,
         out_shape=outs,
+        in_specs=[ANYWHERE if i in far else LOCAL for i in range(count)],
+        out_specs=spots or jax.tree.map(lambda _: LOCAL, outs),
         scratch_shapes=list(scratch),
+        compiler_params=pltpu.CompilerParams(vmem_limit_bytes=16 << 20),
         cost_estimate=pl.CostEstimate(
             flops=int(flops), bytes_accessed=1 << 20, transcendentals=1 << 17
         ),
@@ -163,6 +244,9 @@
     places = range(lax.axis_size("head"))
     other = lax.ppermute(own, "head", [(place, place ^ 1) for place in places])
     shape = jax.ShapeDtypeStruct
+    group = lax.axis_index("head") // 2
+    chosen = jnp.arange(beta.shape[1]) == group
+    strengths = jnp.sum(jnp.where(chosen[:, None], beta.T, 0.0), axis=0, keepdims=True)
     pack, solved, sides, coef = call(
         prepare,
         (
@@ -171,22 +255,43 @@
             shape((width, 2 * length), NARROW),
             shape((8, length), WIDE),
         ),
+        3,
         [pltpu.VMEM((3, width, length), NARROW)],
-    )(own, other, beta.T)
-    everyone = lax.all_gather(pack, "seq", tiled=True)
-    moved, local = call(
+    )(own, other, strengths)
+
+    def across(block):
+        return lax.ppermute(block, "seq", [(i, i ^ 1) for i in range(segments)])
+
+    mate = across(pack)
+    far = []
+    for chip in range(1, segments // 2):
+        pairs = [(i, (i + 2 * chip) % segments) for i in range(segments)]
+        far.append(lax.ppermute(pack, "seq", pairs))
+    moved, *state = call(
         own_segment,
-        (shape((length, heads * width), NARROW), shape((length, heads * length), WIDE)),
-    )(queries, solved, sides, coef)
+        (shape((length, heads * width), NARROW),)
+        + (shape((length, heads * width), WIDE),) * 3,
+        5,
+    )(queries, solved, sides, coef, pack)
+    blocks = []
+    for block in far:
+        blocks += [block, across(block)]
     return call(
         attend,
         shape((length, heads * width), NARROW),
+        6 + len(blocks),
         [
             pltpu.VMEM((width, (segments - 1) * length), NARROW),
-            pltpu.VMEM((segments * length, width), NARROW),
+            pltpu.VMEM(((segments - 1) * length, 2 * width), NARROW),
+            pltpu.VMEM((length, heads * width), NARROW),
+            pltpu.VMEM((1, width), WIDE),
+            pltpu.SemaphoreType.DMA((heads,)),
+            pltpu.SemaphoreType.DMA,
         ],
         flops=1e9,
-    )(moved, local, everyone, gain.reshape(1, -1))
+        spots=ANYWHERE,
+        far=(4,),
+    )(moved, *state, gain.reshape(1, -1), mate, *blocks)
 
 
 def solution(mesh):
@@ -198,6 +303,7 @@
         P("seq", None),
         P(),
     )
+
     return jax.shard_map(
         shards, mesh=mesh, in_specs=placed, out_specs=P("seq", "head"), check_vma=False
     )

time: 37.2 us -> 27.1 us (0.73)
  the two profiles are of different devices: /device:TPU:0 before, /device:TPU:15 now
where the time goes in v2:
time: 27.1 us; the launch traced here: 26.8 us
  starting transfers between devices  11.9 us (44%)
  Pallas kernels  9.88 us (36%)
  waiting for transfers between devices  2.74 us (10%)
  other arithmetic  1.57 us (6%)
  local copies, waits for them, and re-layouts  0.65 us (2%)
    ppermute x4, starting transfers between devices, across(): return lax.ppermute(block, 'seq', [(i, i ^ 1) for i in range(segments)])  7.83 us
    pallas_call x1, Pallas kernels, shards(): call(attend, shape((length, heads * width), NARROW), 6 + len(blocks), [pl...  4.08 us
    ppermute x3, starting transfers between devices, shards(): far.append(lax.ppermute(pack, 'seq', pairs))  3.83 us
    pallas_call x1, Pallas kernels, shards(): call(own_segment, (shape((length, heads * width), NARROW),) + (shape((len...  3.29 us
    pallas_call x1, Pallas kernels, shards(): call(prepare, (shape((width, 2 * length + width), NARROW), shape((2, leng...  2.51 us
    ppermute x1, waiting for transfers between devices, shards(): other = lax.ppermute(own, 'head', [(place, place ^ 1) for place in places])  1.92 us
    ppermute x3, waiting for transfers between devices, shards(): far.append(lax.ppermute(pack, 'seq', pairs))  0.82 us
    concatenate x1, other arithmetic, shards(): own = jnp.concatenate([keys.T, values.T, directions.T], axis=0)  0.8 us
  transfers between devices with their start and end apart: 8, of which 2 were waited for; matrix products, arithmetic and copies ran while one was open for 3% of the time, Pallas kernels for 12%

profile of v2, /device:TPU:15, one launch (start us, length us, event | category | flops | bytes accessed | tf_op | source)
XLA Modules:
  0.0 26.8 jit_solution(11937511826121326288)
XLA Ops:
  0.0 0.8 %pad_maximum_fusion.own_ref = bf16[192,128]{1,0:T(8,128)(2,1)S(1)} fusion(bf16[64,128]{1,0:T(8,128)(2,1)} %bitcast.7, bf16[64,128]{1,0:T(8,128)(2,1)} %bitcast.8, bf16[64,128]{1,0:T(8,128)(2,1)} %bitcast.9), kind=kLoop, calls=%fused_computation | loop fusion | flops 147456 | bytes 98304 | tf_op jit(solution)/shard_map/concatenate | solution.py:243
  0.8 0.3 collective-permute-start
  1.1 0.8 %select_reduce_fusion = f32[128]{0:T(128)S(1)} fusion(f32[128,2]{0,1:T(2,128)} %param.10, pred[2]{0:T(512)(128)(4,1)S(1)} %iota_compare_fusion), kind=kLoop, calls=%fused_computation.1 | loop fusion | flops 384 | bytes 1538 | tf_op jit(solution)/shard_map/reduce_sum | solution.py:249
  1.8 1.9 %collective-permute-done.other_ref = bf16[192,128]{1,0:T(8,128)(2,1)S(1)} collective-permute-done((bf16[192,128]{1,0:T(8,128)(2,1)S(1)}, bf16[192,128]{1,0:T(8,128)(2,1)S(1)}, u32[]{:S(2)}, u32[]{:S(2)}) %collective-permute-start) | collective-permute-done | bytes 49184 | tf_op jit(solution)/shard_map/ppermute | solution.py:245
  3.7 2.5 %shard_map.64 = (bf16[128,384]{1,0:T(8,128)(2,1)S(1)}, bf16[2,128,256]{2,1,0:T(8,128)(2,1)S(1)}, bf16[128,256]{1,0:T(8,128)(2,1)S(1)}, f32[8,128]{1,0:T(8,128)S(1)}) custom-call(bf16[192,128]{1,0:T(8,128)(2,1)S(1)} %pad_maximum_fusion.own_ref, bf16[192,128]{1,0:T(8,128)(2,1)S(1)} %collective-permute-done.other_ref, f32[1,128]{1,0:T(1,128)S(1)} %bitcast.5), custom_call_target="tpu_custom_call" | custom-call | flops 100000000 | bytes 1048576 | tf_op jit(solution)/shard_map/pallas_call | solution.py:250
  6.3 1.3 %collective-permute-start.2 = (bf16[128,384]{1,0:T(8,128)(2,1)S(1)}, bf16[128,384]{1,0:T(8,128)(2,1)S(1)}, u32[]{:S(2)}, u32[]{:S(2)}) collective-permute-start(bf16[128,384]{1,0:T(8,128)(2,1)S(1)} %get-tuple-element.16.pack_ref), channel_id=1, source_target_pairs={{0,8},{4,12},{8,16},{12,20},{16,24},{20,28},{24,0},{28,4},{1,9},{5... | collective-permute-start | bytes 294920 | tf_op jit(solution)/shard_map/ppermute | solution.py:269
  7.6 1.1 %collective-permute-start.4 = (bf16[128,384]{1,0:T(8,128)(2,1)S(1)}, bf16[128,384]{1,0:T(8,128)(2,1)S(1)}, u32[]{:S(2)}, u32[]{:S(2)}) collective-permute-start(bf16[128,384]{1,0:T(8,128)(2,1)S(1)} %get-tuple-element.16.pack_ref), channel_id=1, source_target_pairs={{0,16},{4,20},{8,24},{12,28},{16,0},{20,4},{24,8},{28,12},{1,17},{... | collective-permute-start | bytes 294920 | tf_op jit(solution)/shard_map/ppermute | solution.py:269
  8.7 1.4 %collective-permute-start.6 = (bf16[128,384]{1,0:T(8,128)(2,1)S(1)}, bf16[128,384]{1,0:T(8,128)(2,1)S(1)}, u32[]{:S(2)}, u32[]{:S(2)}) collective-permute-start(bf16[128,384]{1,0:T(8,128)(2,1)S(1)} %get-tuple-element.16.pack_ref), channel_id=1, source_target_pairs={{0,24},{4,28},{8,0},{12,4},{16,8},{20,12},{24,16},{28,20},{1,25},{... | collective-permute-start | bytes 294920 | tf_op jit(solution)/shard_map/ppermute | solution.py:269
  10.1 2.7 %collective-permute-start.1 = (bf16[128,384]{1,0:T(8,128)(2,1)S(1)}, bf16[128,384]{1,0:T(8,128)(2,1)S(1)}, u32[]{:S(2)}, u32[]{:S(2)}) collective-permute-start(bf16[128,384]{1,0:T(8,128)(2,1)S(1)} %get-tuple-element.16.pack_ref), channel_id=1, source_target_pairs={{0,4},{4,0},{8,12},{12,8},{16,20},{20,16},{24,28},{28,24},{1,5},{5... | collective-permute-start | bytes 294920 | tf_op jit(solution)/shard_map/ppermute | solution.py:263
  12.8 0.0 collective-permute-done.2.refs_6_
  12.8 1.0 %collective-permute-start.3 = (bf16[128,384]{1,0:T(8,128)(2,1)S(1)}, bf16[128,384]{1,0:T(8,128)(2,1)S(1)}, u32[]{:S(2)}, u32[]{:S(2)}) collective-permute-start(bf16[128,384]{1,0:T(8,128)(2,1)S(1)} %collective-permute-done.2.refs_6_), channel_id=1, source_target_pairs={{0,4},{4,0},{8,12},{12,8},{16,20},{20,16},{24,28},{28,24},{1,5},{5... | collective-permute-start | bytes 294920 | tf_op jit(solution)/shard_map/ppermute | solution.py:263
  13.8 0.0 collective-permute-done.4.refs_8_
  13.8 3.3 %collective-permute-start.5 = (bf16[128,384]{1,0:T(8,128)(2,1)S(1)}, bf16[128,384]{1,0:T(8,128)(2,1)S(1)}, u32[]{:S(2)}, u32[]{:S(2)}) collective-permute-start(bf16[128,384]{1,0:T(8,128)(2,1)S(1)} %collective-permute-done.4.refs_8_), channel_id=1, source_target_pairs={{0,4},{4,0},{8,12},{12,8},{16,20},{20,16},{24,28},{28,24},{1,5},{5... | collective-permute-start | bytes 294920 | tf_op jit(solution)/shard_map/ppermute | solution.py:263
  17.1 0.8 %collective-permute-done.6.refs_10_ = bf16[128,384]{1,0:T(8,128)(2,1)S(1)} collective-permute-done((bf16[128,384]{1,0:T(8,128)(2,1)S(1)}, bf16[128,384]{1,0:T(8,128)(2,1)S(1)}, u32[]{:S(2)}, u32[]{:S(2)}) %collective-permute-start.6) | collective-permute-done | bytes 98336 | tf_op jit(solution)/shard_map/ppermute | solution.py:269
  17.9 0.8 %collective-permute-start.7 = (bf16[128,384]{1,0:T(8,128)(2,1)S(1)}, bf16[128,384]{1,0:T(8,128)(2,1)S(1)}, u32[]{:S(2)}, u32[]{:S(2)}) collective-permute-start(bf16[128,384]{1,0:T(8,128)(2,1)S(1)} %collective-permute-done.6.refs_10_), channel_id=1, source_target_pairs={{0,4},{4,0},{8,12},{12,8},{16,20},{20,16},{24,28},{28,24},{1,5},{5... | collective-permute-start | bytes 294920 | tf_op jit(solution)/shard_map/ppermute | solution.py:263
  18.7 0.0 copy-done
  18.7 3.3 %shard_map.65 = (bf16[128,1024]{1,0:T(8,128)(2,1)S(1)}, f32[128,1024]{1,0:T(8,128)S(1)}, f32[128,1024]{1,0:T(8,128)S(1)}, f32[128,1024]{1,0:T(8,128)S(1)}) custom-call(bf16[128,1024]{1,0:T(8,128)(2,1)S(1)} %copy-done, bf16[2,128,256]{2,1,0:T(8,128)(2,1)S(1)} %get-tuple-element.13.solved_ref, bf16[128,256]{1,0:T(8,128)(2,1)S(1)} %get-tuple-element.14.sides_ref, ...), custom_call_target="tpu_custom_call" | custom-call | flops 100000000 | bytes 1048576 | tf_op jit(solution)/shard_map/pallas_call | solution.py:270
  22.0 0.0 collective-permute-done.1.refs_5_
  22.0 0.0 collective-permute-done.3.refs_7_
  22.1 0.0 collective-permute-done.5.refs_9_
  22.1 0.0 collective-permute-done.7.refs_11_
  22.1 0.0 copy-start.1
  22.1 0.6 %copy-done.1 = f32[128]{0:T(128)S(1)} copy-done((f32[128]{0:T(128)S(1)}, f32[128]{0:T(128)}, u32[]{:S(2)}) %copy-start.1) | copy-done | bytes 536
  22.7 4.1 %shard_map.66 = bf16[128,1024]{1,0:T(8,128)(2,1)} custom-call(bf16[128,1024]{1,0:T(8,128)(2,1)S(1)} %get-tuple-element.17.refs_0_, f32[128,1024]{1,0:T(8,128)S(1)} %get-tuple-element.18.refs_1_, f32[128,1024]{1,0:T(8,128)S(1)} %get-tuple-element.19.refs_2_, f32[128,1024]{1,0:T(8,128)S(1)} %get-tuple-element.20.refs_3_, f32[1,128]{1,0:T(1,128)S(1)} %bitcast.6, ...), custom_call_target="tpu_custom_call" | custom-call | flops 1000000000 | bytes 1048576 | tf_op jit(solution)/shard_map/pallas_call | solution.py:279
  (2 shorter events, 0.0 us)
Async XLA Ops:
  0.0 18.7 %copy-start = (bf16[128,1024]{1,0:T(8,128)(2,1)S(1)}, bf16[128,1024]{1,0:T(8,128)(2,1)}, u32[]{:S(2)}) copy-start(bf16[128,1024]{1,0:T(8,128)(2,1)} %queries_ref.1) | copy-start | bytes 786436
  0.8 2.9 %collective-permute-start = (bf16[192,128]{1,0:T(8,128)(2,1)S(1)}, bf16[192,128]{1,0:T(8,128)(2,1)S(1)}, u32[]{:S(2)}, u32[]{:S(2)}) collective-permute-start(bf16[192,128]{1,0:T(8,128)(2,1)S(1)} %pad_maximum_fusion.own_ref), channel_id=1, source_target_pairs={{0,1},{1,0},{2,3},{3,2},{4,5},{5,4},{6,7},{7,6},{8,9},{9,8},{10,11... | collective-permute-start | bytes 147464 | tf_op jit(solution)/shard_map/ppermute | solution.py:245
  6.3 6.5 %collective-permute-start.2 = (bf16[128,384]{1,0:T(8,128)(2,1)S(1)}, bf16[128,384]{1,0:T(8,128)(2,1)S(1)}, u32[]{:S(2)}, u32[]{:S(2)}) collective-permute-start(bf16[128,384]{1,0:T(8,128)(2,1)S(1)} %get-tuple-element.16.pack_ref), channel_id=1, source_target_pairs={{0,8},{4,12},{8,16},{12,20},{16,24},{20,28},{24,0},{28,4},{1,9},{5... | collective-permute-start | bytes 294920 | tf_op jit(solution)/shard_map/ppermute | solution.py:269
  7.6 6.2 %collective-permute-start.4 = (bf16[128,384]{1,0:T(8,128)(2,1)S(1)}, bf16[128,384]{1,0:T(8,128)(2,1)S(1)}, u32[]{:S(2)}, u32[]{:S(2)}) collective-permute-start(bf16[128,384]{1,0:T(8,128)(2,1)S(1)} %get-tuple-element.16.pack_ref), channel_id=1, source_target_pairs={{0,16},{4,20},{8,24},{12,28},{16,0},{20,4},{24,8},{28,12},{1,17},{... | collective-permute-start | bytes 294920 | tf_op jit(solution)/shard_map/ppermute | solution.py:269
  8.7 9.2 %collective-permute-start.6 = (bf16[128,384]{1,0:T(8,128)(2,1)S(1)}, bf16[128,384]{1,0:T(8,128)(2,1)S(1)}, u32[]{:S(2)}, u32[]{:S(2)}) collective-permute-start(bf16[128,384]{1,0:T(8,128)(2,1)S(1)} %get-tuple-element.16.pack_ref), channel_id=1, source_target_pairs={{0,24},{4,28},{8,0},{12,4},{16,8},{20,12},{24,16},{28,20},{1,25},{... | collective-permute-start | bytes 294920 | tf_op jit(solution)/shard_map/ppermute | solution.py:269
  10.1 11.9 %collective-permute-start.1 = (bf16[128,384]{1,0:T(8,128)(2,1)S(1)}, bf16[128,384]{1,0:T(8,128)(2,1)S(1)}, u32[]{:S(2)}, u32[]{:S(2)}) collective-permute-start(bf16[128,384]{1,0:T(8,128)(2,1)S(1)} %get-tuple-element.16.pack_ref), channel_id=1, source_target_pairs={{0,4},{4,0},{8,12},{12,8},{16,20},{20,16},{24,28},{28,24},{1,5},{5... | collective-permute-start | bytes 294920 | tf_op jit(solution)/shard_map/ppermute | solution.py:263
  12.8 9.3 %collective-permute-start.3 = (bf16[128,384]{1,0:T(8,128)(2,1)S(1)}, bf16[128,384]{1,0:T(8,128)(2,1)S(1)}, u32[]{:S(2)}, u32[]{:S(2)}) collective-permute-start(bf16[128,384]{1,0:T(8,128)(2,1)S(1)} %collective-permute-done.2.refs_6_), channel_id=1, source_target_pairs={{0,4},{4,0},{8,12},{12,8},{16,20},{20,16},{24,28},{28,24},{1,5},{5... | collective-permute-start | bytes 294920 | tf_op jit(solution)/shard_map/ppermute | solution.py:263
  13.8 8.3 %collective-permute-start.5 = (bf16[128,384]{1,0:T(8,128)(2,1)S(1)}, bf16[128,384]{1,0:T(8,128)(2,1)S(1)}, u32[]{:S(2)}, u32[]{:S(2)}) collective-permute-start(bf16[128,384]{1,0:T(8,128)(2,1)S(1)} %collective-permute-done.4.refs_8_), channel_id=1, source_target_pairs={{0,4},{4,0},{8,12},{12,8},{16,20},{20,16},{24,28},{28,24},{1,5},{5... | collective-permute-start | bytes 294920 | tf_op jit(solution)/shard_map/ppermute | solution.py:263
  17.9 4.2 %collective-permute-start.7 = (bf16[128,384]{1,0:T(8,128)(2,1)S(1)}, bf16[128,384]{1,0:T(8,128)(2,1)S(1)}, u32[]{:S(2)}, u32[]{:S(2)}) collective-permute-start(bf16[128,384]{1,0:T(8,128)(2,1)S(1)} %collective-permute-done.6.refs_10_), channel_id=1, source_target_pairs={{0,4},{4,0},{8,12},{12,8},{16,20},{20,16},{24,28},{28,24},{1,5},{5... | collective-permute-start | bytes 294920 | tf_op jit(solution)/shard_map/ppermute | solution.py:263
  22.1 0.7 %copy-start.1 = (f32[128]{0:T(128)S(1)}, f32[128]{0:T(128)}, u32[]{:S(2)}) copy-start(f32[128]{0:T(128)} %param.11) | copy-start | bytes 1540

commit v3 on v2

v3 whole, which is shorter than its diff:
```python
import math

import jax
import jax.numpy as jnp
from jax import lax
from jax.experimental import pallas as pl
from jax.experimental.pallas import tpu as pltpu
from jax.sharding import PartitionSpec as P


WIDE = jnp.float32
NARROW = jnp.bfloat16
MASKED = -1e30
OWN_PIECES, NEAR_PIECES, FAR_PIECES = 1,2,4


def halves(x):
    top = x.astype(NARROW)
    return top, (x - top.astype(WIDE)).astype(NARROW)


def dot(a, b):
    return jnp.dot(a, b, preferred_element_type=WIDE)


def dot3(a, b):
    a_top, a_low = a
    b_top, b_low = b
    return dot(
        jnp.concatenate([a_top, a_low, a_top], axis=1),
        jnp.concatenate([b_top, b_top, b_low], axis=0),
    )


def prepare(own_ref, other_ref, small_ref, pack_ref, solved_ref, sides_ref, coef_ref, full_ref):
    half, length = own_ref.shape[0] // 3, own_ref.shape[1]
    width = 2 * half
    place = lax.axis_index("head")
    parity = place % 2
    for part in range(3):
        rows = pl.ds(part * half, half)
        full_ref[part, pl.ds(parity * half, half), :] = own_ref[rows, :]
        full_ref[part, pl.ds((1 - parity) * half, half), :] = other_ref[rows, :]
    keys_t, values_t, dirs_t = full_ref[0], full_ref[1], full_ref[2]
    dirs_wide = dirs_t.astype(WIDE)
    dirs = dirs_wide.T.astype(NARROW)
    power = jnp.sum(dirs_wide * dirs_wide, axis=0, keepdims=True) + 1e-06
    coef = small_ref[:1, :] / power

    row = lax.broadcasted_iota(jnp.int32, (length, length), 0)
    col = lax.broadcasted_iota(jnp.int32, (length, length), 1)
    sides = jnp.concatenate([dirs_t, keys_t], axis=1)
    meets = dot(dirs, sides)
    below = jnp.where(row > col, meets[:, :length] * coef, 0.0)
    reach = jnp.where(row > col, meets[:, length:], 0.0)

    inverse = jnp.where(row == col, 1.0, 0.0) - jnp.where((row ^ col) == 1, below, 0.0)
    block = 2
    while block < length:
        joint = jnp.where((row // block) ^ (col // block) == 1, below, 0.0)
        parts = halves(inverse)
        inverse = inverse - dot3(parts, halves(dot3(halves(joint), parts)))
        block *= 2

    top, low = halves(inverse)
    reach_top, reach_low = halves(reach)
    right = jnp.concatenate([reach_top, dirs], axis=1)
    solved = dot(jnp.concatenate([top, low], axis=1), jnp.concatenate([right, right], axis=0))
    solved_reach = solved[:, :length] + dot(top, reach_low)
    solved = jnp.concatenate([solved_reach, solved[:, length:]], axis=1)
    solved_parts = halves(solved)
    change = dot3(halves(dirs_wide * coef), solved_parts)
    pack_ref[:, :length] = (keys_t.astype(WIDE) - change[:, :length]).astype(NARROW)
    row_w = lax.broadcasted_iota(jnp.int32, (width, width), 0)
    col_w = lax.broadcasted_iota(jnp.int32, (width, width), 1)
    unit = jnp.where(row_w == col_w, 1.0, 0.0)
    pack_ref[:, length : length + width] = (unit - change[:, length:]).astype(NARROW)
    pack_ref[:, length + width :] = values_t.astype(WIDE).T.astype(NARROW)
    solved_ref[0] = solved_parts[0]
    solved_ref[1] = solved_parts[1]
    sides_ref[...] = sides
    coef_ref[...] = jnp.broadcast_to(coef, coef_ref.shape)


def own_segment(
    queries_ref, solved_ref, sides_ref, coef_ref, pack_ref, moved_ref, peak_ref, sum_ref, mix_ref
):
    length = queries_ref.shape[0]
    width = sides_ref.shape[0]
    top, low = solved_ref[0], solved_ref[1]
    right = jnp.concatenate([top, top, low], axis=0)
    values = counted(pack_ref[:, length + width :])
    for part in pieces(moved_ref.shape[0], OWN_PIECES):
        heads = range(part.start // length, (part.start + part.size) // length)
        query = jnp.concatenate([queries_ref[:, pl.ds(h * width, width)] for h in heads], axis=0)
        row = lax.broadcasted_iota(jnp.int32, (part.size, length), 0) % length
        col = lax.broadcasted_iota(jnp.int32, (part.size, length), 1)
        past = row >= col
        plain = dot(query, sides_ref[...])
        met_top, met_low = halves(jnp.where(past, plain[:, :length] * coef_ref[:1, :], 0.0))
        change = dot(jnp.concatenate([met_top, met_low, met_top], axis=1), right)
        moved_ref[part, :] = (query.astype(WIDE) - change[:, length:]).astype(NARROW)
        scores = jnp.where(past, plain[:, length:] - change[:, :length], MASKED)
        peak = jnp.max(scores, axis=1, keepdims=True)
        mixed = dot(powers(scores, peak, width).astype(NARROW), values)
        peak_ref[part, :] = jnp.broadcast_to(peak, (part.size, width))
        mix_ref[part, :] = mixed[:, :width]
        sum_ref[part, :] = mixed[:, width:]


def counted(values):
    return jnp.concatenate([values, jnp.ones_like(values)], axis=1)


def powers(scores, peak, width):
    return jnp.exp2((scores - peak) * (width ** (-0.5) * math.log2(math.e)))


def carry(travel, block, length):
    both = dot(jnp.concatenate(halves(travel), axis=1), jnp.concatenate([block, block], axis=0))
    return both[:, :length].astype(NARROW), both[:, length:]


def gather(refs, core, keys_ref, values_ref, travel, length):
    width = keys_ref.shape[0]
    for slot, ref in enumerate(refs):
        if isinstance(ref, tuple):
            block = jnp.where(core == 1, ref[0][...], ref[1][...])
        else:
            block = ref[...]
        at = pl.ds(slot * length, length)
        values_ref[at, :] = counted(block[:, length + width :])
        block = block[:, : length + width]
        if travel is None:
            keys_ref[:, at] = block[:, :length]
            row = lax.broadcasted_iota(jnp.int32, (width, width), 0)
            col = lax.broadcasted_iota(jnp.int32, (width, width), 1)
            unit = jnp.where(row == col, 1.0, 0.0)
            travel = jnp.where(core == 1, block[:, length:].astype(WIDE), unit)
        else:
            keys_ref[:, at], travel = carry(travel, block, length)
    return travel


def take_in(query, keys, values, first, last, peak, total, mix):
    width = mix.shape[1]
    scores = dot(query, keys)
    column = lax.broadcasted_iota(jnp.int32, scores.shape, 1)
    scores = jnp.where((column >= first) & (column < last), scores, MASKED)
    above = jnp.maximum(peak, jnp.max(scores, axis=1, keepdims=True))
    fade = powers(peak, above, width)
    level = jnp.concatenate([above] * (scores.shape[1] // width), axis=1)
    mixed = dot(powers(scores, level, width).astype(NARROW), values)
    return above, total * fade + mixed[:, width:], mix * fade + mixed[:, :width]


def pieces(rows, count):
    size = rows // count
    return [pl.ds(start, size) for start in range(0, rows, size)]


def attend_near(
    moved_ref, peak_ref, sum_ref, mix_ref, mate_ref, straight_ref, crossed_ref,
    peak_out, sum_out, mix_out, travel_out, keys_ref, values_ref,
):
    width = keys_ref.shape[0]
    length = mate_ref.shape[1] - 2 * width
    place = lax.axis_index("seq")
    core, chip_place = place % 2, place // 2
    order = [mate_ref, (straight_ref, crossed_ref), (crossed_ref, straight_ref)]
    travel_out[...] = gather(order, core, keys_ref, values_ref, None, length)
    first = (1 - core) * length
    last = jnp.where(chip_place > 0, 3, 1) * length
    for part in pieces(moved_ref.shape[0], NEAR_PIECES):
        peak_out[part, :], sum_out[part, :], mix_out[part, :] = take_in(
            moved_ref[part, :], keys_ref[...], values_ref[...], first, last,
            peak_ref[part, :], sum_ref[part, :], mix_ref[part, :],
        )


def attend_far(*refs):
    moved_ref, peak_ref, sum_ref, mix_ref, travel_ref, small_ref = refs[:6]
    out_ref, keys_ref, values_ref, done_ref, sem = refs[-5:]
    far = refs[6:-5]
    length, width = out_ref.shape[0], keys_ref.shape[0]
    heads = out_ref.shape[1] // width
    place = lax.axis_index("seq")
    core, chip_place = place % 2, place // 2

    def out_copy(head):
        cols = pl.ds(head * width, width)
        return pltpu.make_async_copy(done_ref.at[:, cols], out_ref.at[:, cols], sem.at[head])

    def finish(part, total, mix):
        square = jnp.mean(mix * mix, axis=1, keepdims=True)
        strength = lax.rsqrt(square + 1e-06 * (total * total))
        normed = (mix * strength * small_ref[1:2, :]).astype(NARROW)
        for at in range(0, part.size, length):
            head = (part.start + at) // length
            done_ref[:, pl.ds(head * width, width)] = normed[at : at + length]
            out_copy(head).start()

    @pl.when(chip_place > 1)
    def _():
        order = []
        for straight, crossed in zip(far[::2], far[1::2]):
            order += [(straight, crossed), (crossed, straight)]
        gather(order, core, keys_ref, values_ref, travel_ref[...], length)
        last = 2 * (chip_place - 1) * length
        for part in pieces(moved_ref.shape[0], FAR_PIECES):
            _, total, mix = take_in(
                moved_ref[part, :], keys_ref[...], values_ref[...], 0, last,
                peak_ref[part, :], sum_ref[part, :], mix_ref[part, :],
            )
            finish(part, total, mix)

    @pl.when(chip_place <= 1)
    def _():
        for part in pieces(moved_ref.shape[0], heads):
            finish(part, sum_ref[part, :], mix_ref[part, :])

    for head in range(heads):
        out_copy(head).wait()


LOCAL = pl.BlockSpec(memory_space=pltpu.VMEM)
ANYWHERE = pl.BlockSpec(memory_space=pltpu.HBM)


def call(kernel, outs, count, scratch=(), flops=1e8, spots=None):
    return pl.pallas_call(
        kernel,
        out_shape=outs,
        in_specs=[LOCAL] * count,
        out_specs=spots or jax.tree.map(lambda _: LOCAL, outs),
        scratch_shapes=list(scratch),
        compiler_params=pltpu.CompilerParams(vmem_limit_bytes=16 << 20),
        cost_estimate=pl.CostEstimate(
            flops=int(flops), bytes_accessed=1 << 20, transcendentals=1 << 17
        ),
    )


def shards(queries, keys, values, directions, beta, gain):
    length, half = directions.shape
    width = 2 * half
    heads = queries.shape[1] // width
    segments = lax.axis_size("seq")
    own = jnp.concatenate([keys.T, values.T, directions.T], axis=0)
    places = range(lax.axis_size("head"))
    other = lax.ppermute(own, "head", [(place, place ^ 1) for place in places])
    shape = jax.ShapeDtypeStruct
    group = lax.axis_index("head") // 2
    chosen = jnp.arange(beta.shape[1]) == group
    strengths = jnp.sum(jnp.where(chosen[:, None], beta.T, 0.0), axis=0, keepdims=True)
    small = jnp.concatenate([strengths, gain.reshape(1, -1)], axis=0)
    pack, solved, sides, coef = call(
        prepare,
        (
            shape((width, 2 * length + width), NARROW),
            shape((2, length, length + width), NARROW),
            shape((width, 2 * length), NARROW),
            shape((8, length), WIDE),
        ),
        3,
        [pltpu.VMEM((3, width, length), NARROW)],
    )(own, other, small)

    def across(block):
        return lax.ppermute(block, "seq", [(i, i ^ 1) for i in range(segments)])

    mate = across(pack)
    chips = segments // 2
    far = []
    for chip in range(1, chips):
        pairs = [(i, (i + 2 * chip) % segments) for i in range(segments)]
        far.append(lax.ppermute(pack, "seq", pairs))
    state_shape = (shape((heads * length, width), WIDE),) * 3
    moved, *state = call(
        own_segment, (shape((heads * length, width), NARROW),) + state_shape, 5
    )(queries, solved, sides, coef, pack)

    def stores(count):
        return [
            pltpu.VMEM((width, count * length), NARROW),
            pltpu.VMEM((count * length, 2 * width), NARROW),
        ]

    crossed = across(far[0])
    *state, travel = call(
        attend_near, state_shape + (shape((width, width), WIDE),), 7, stores(3)
    )(moved, *state, mate, far[0], crossed)
    blocks = []
    for chip in range(2, chips):
        blocks += [far[chip - 1], across(far[chip - 1])]
    return call(
        attend_far,
        shape((length, heads * width), NARROW),
        6 + len(blocks),
        stores(2 * (chips - 2))
        + [pltpu.VMEM((length, heads * width), NARROW), pltpu.SemaphoreType.DMA((heads,))],
        flops=1e9,
        spots=ANYWHERE,
    )(moved, *state, travel, small, *blocks)


def solution(mesh):
    placed = (
        P("seq", "head"),
        P("seq", "head"),
        P("seq", "head"),
        P("seq", "head"),
        P("seq", None),
        P(),
    )

    return jax.shard_map(
        shards, mesh=mesh, in_specs=placed, out_specs=P("seq", "head"), check_vma=False
    )
```

time: 27.1 us -> 22.6 us (0.83)
  the two profiles are of different devices: /device:TPU:15 before, /device:TPU:24 now
where the time goes in v3:
time: 22.6 us; the launch traced here: 22.3 us
  waiting for transfers between devices  9.86 us (44%)
  Pallas kernels  7.07 us (31%)
  starting transfers between devices  4.41 us (20%)
  other arithmetic  0.9 us (4%)
    ppermute x3, waiting for transfers between devices, shards(): far.append(lax.ppermute(pack, 'seq', pairs))  7.36 us
    pallas_call x1, Pallas kernels, shards(): call(prepare, (shape((width, 2 * length + width), NARROW), shape((2, leng...  2.51 us
    ppermute x1, waiting for transfers between devices, shards(): other = lax.ppermute(own, 'head', [(place, place ^ 1) for place in places])  2.49 us
    pallas_call x1, Pallas kernels, shards(): call(attend_far, shape((length, heads * width), NARROW), 6 + len(blocks),...  2.41 us
    ppermute x3, starting transfers between devices, shards(): far.append(lax.ppermute(pack, 'seq', pairs))  2.41 us
    ppermute x1, starting transfers between devices, shards(): other = lax.ppermute(own, 'head', [(place, place ^ 1) for place in places])  1.49 us
    pallas_call x1, Pallas kernels, shards(): call(attend_near, state_shape + (shape((width, width), WIDE),), 7, stores...  1.14 us
    pallas_call x1, Pallas kernels, shards(): call(own_segment, (shape((heads * length, width), NARROW),) + state_shape...  1.01 us
  transfers between devices with their start and end apart: 8, of which 3 were waited for; matrix products, arithmetic and copies ran while one was open for 0% of the time, Pallas kernels for 10%

profile of v3, /device:TPU:24, one launch (start us, length us, event | category | flops | bytes accessed | tf_op | source)
XLA Modules:
  0.0 22.3 jit_solution(9283777627672497376)
XLA Ops:
  0.0 0.8 %pad_maximum_fusion.own_ref = bf16[192,128]{1,0:T(8,128)(2,1)S(1)} fusion(bf16[64,128]{1,0:T(8,128)(2,1)} %bitcast.5, bf16[64,128]{1,0:T(8,128)(2,1)} %bitcast.6, bf16[64,128]{1,0:T(8,128)(2,1)} %bitcast.7), kind=kLoop, calls=%fused_computation | loop fusion | flops 147456 | bytes 98304 | tf_op jit(solution)/shard_map/concatenate | solution.py:249
  0.8 1.5 %collective-permute-start = (bf16[192,128]{1,0:T(8,128)(2,1)S(1)}, bf16[192,128]{1,0:T(8,128)(2,1)S(1)}, u32[]{:S(2)}, u32[]{:S(2)}) collective-permute-start(bf16[192,128]{1,0:T(8,128)(2,1)S(1)} %pad_maximum_fusion.own_ref), channel_id=1, source_target_pairs={{0,1},{1,0},{2,3},{3,2},{4,5},{5,4},{6,7},{7,6},{8,9},{9,8},{10,11... | collective-permute-start | bytes 147464 | tf_op jit(solution)/shard_map/ppermute | solution.py:251
  2.3 0.0 copy-done.1
  2.3 0.1 select_reduce_fusion
  2.4 0.0 copy-done.2
  2.4 2.5 %collective-permute-done.other_ref = bf16[192,128]{1,0:T(8,128)(2,1)S(1)} collective-permute-done((bf16[192,128]{1,0:T(8,128)(2,1)S(1)}, bf16[192,128]{1,0:T(8,128)(2,1)S(1)}, u32[]{:S(2)}, u32[]{:S(2)}) %collective-permute-start) | collective-permute-done | bytes 49184 | tf_op jit(solution)/shard_map/ppermute | solution.py:251
  4.9 2.5 %shard_map.64 = (bf16[128,384]{1,0:T(8,128)(2,1)S(1)}, bf16[2,128,256]{2,1,0:T(8,128)(2,1)S(1)}, bf16[128,256]{1,0:T(8,128)(2,1)S(1)}, f32[8,128]{1,0:T(8,128)S(1)}) custom-call(bf16[192,128]{1,0:T(8,128)(2,1)S(1)} %pad_maximum_fusion.own_ref, bf16[192,128]{1,0:T(8,128)(2,1)S(1)} %collective-permute-done.other_ref, ...), custom_call_target="tpu_custom_call" | custom-call | flops 100000000 | bytes 1048576 | tf_op jit(solution)/shard_map/pallas_call | solution.py:257
  7.4 0.1 collective-permute-start.2
  7.5 1.9 %collective-permute-start.4 = (bf16[128,384]{1,0:T(8,128)(2,1)S(1)}, bf16[128,384]{1,0:T(8,128)(2,1)S(1)}, u32[]{:S(2)}, u32[]{:S(2)}) collective-permute-start(bf16[128,384]{1,0:T(8,128)(2,1)S(1)} %get-tuple-element.20.pack_ref), channel_id=1, source_target_pairs={{0,16},{4,20},{8,24},{12,28},{16,0},{20,4},{24,8},{28,12},{1,17},{... | collective-permute-start | bytes 294920 | tf_op jit(solution)/shard_map/ppermute | solution.py:277
  9.4 0.4 %collective-permute-start.6 = (bf16[128,384]{1,0:T(8,128)(2,1)S(1)}, bf16[128,384]{1,0:T(8,128)(2,1)S(1)}, u32[]{:S(2)}, u32[]{:S(2)}) collective-permute-start(bf16[128,384]{1,0:T(8,128)(2,1)S(1)} %get-tuple-element.20.pack_ref), channel_id=1, source_target_pairs={{0,24},{4,28},{8,0},{12,4},{16,8},{20,12},{24,16},{28,20},{1,25},{... | collective-permute-start | bytes 294920 | tf_op jit(solution)/shard_map/ppermute | solution.py:277
  9.8 0.0 collective-permute-start.1
  9.8 2.3 %collective-permute-done.2.straight_ref = bf16[128,384]{1,0:T(8,128)(2,1)S(1)} collective-permute-done((bf16[128,384]{1,0:T(8,128)(2,1)S(1)}, bf16[128,384]{1,0:T(8,128)(2,1)S(1)}, u32[]{:S(2)}, u32[]{:S(2)}) %collective-permute-start.2) | collective-permute-done | bytes 98336 | tf_op jit(solution)/shard_map/ppermute | solution.py:277
  12.1 0.0 collective-permute-start.3
  12.1 5.1 %collective-permute-done.4.refs_6_ = bf16[128,384]{1,0:T(8,128)(2,1)S(1)} collective-permute-done((bf16[128,384]{1,0:T(8,128)(2,1)S(1)}, bf16[128,384]{1,0:T(8,128)(2,1)S(1)}, u32[]{:S(2)}, u32[]{:S(2)}) %collective-permute-start.4) | collective-permute-done | bytes 98336 | tf_op jit(solution)/shard_map/ppermute | solution.py:277
  17.2 0.0 collective-permute-start.5
  17.2 0.0 collective-permute-done.6.refs_8_
  17.2 0.5 %collective-permute-start.7 = (bf16[128,384]{1,0:T(8,128)(2,1)S(1)}, bf16[128,384]{1,0:T(8,128)(2,1)S(1)}, u32[]{:S(2)}, u32[]{:S(2)}) collective-permute-start(bf16[128,384]{1,0:T(8,128)(2,1)S(1)} %collective-permute-done.6.refs_8_), channel_id=1, source_target_pairs={{0,4},{4,0},{8,12},{12,8},{16,20},{20,16},{24,28},{28,24},{1,5},{5... | collective-permute-start | bytes 294920 | tf_op jit(solution)/shard_map/ppermute | solution.py:270
  17.7 1.0 %shard_map.65 = (bf16[1024,128]{1,0:T(8,128)(2,1)S(1)}, f32[1024,128]{1,0:T(8,128)S(1)}, f32[1024,128]{1,0:T(8,128)S(1)}, f32[1024,128]{1,0:T(8,128)S(1)}) custom-call(bf16[128,1024]{1,0:T(8,128)(2,1)S(1)} %copy-done, bf16[2,128,256]{2,1,0:T(8,128)(2,1)S(1)} %get-tuple-element.17.solved_ref, bf16[128,256]{1,0:T(8,128)(2,1)S(1)} %get-tuple-element.18.sides_ref, ...), custom_call_target="tpu_custom_call" | custom-call | flops 100000000 | bytes 1048576 | tf_op jit(solution)/shard_map/pallas_call | solution.py:279
  18.7 0.0 collective-permute-done.1.mate_ref
  18.7 0.0 collective-permute-done.3.crossed_ref
  18.8 1.1 %shard_map.66 = (f32[1024,128]{1,0:T(8,128)S(1)}, f32[1024,128]{1,0:T(8,128)S(1)}, f32[1024,128]{1,0:T(8,128)S(1)}, f32[128,128]{1,0:T(8,128)S(1)}) custom-call(bf16[1024,128]{1,0:T(8,128)(2,1)S(1)} %get-tuple-element.21.moved_ref.refs_0_, f32[1024,128]{1,0:T(8,128)S(1)} %get-tuple-element.22.peak_ref, f32[1024,128]{1,0:T(8,128)S(1)} %get-tuple-element.23.sum_ref, ...), custom_call_target="tpu_custom_call" | custom-call | flops 100000000 | bytes 1048576 | tf_op jit(solution)/shard_map/pallas_call | solution.py:290
  19.9 0.0 collective-permute-done.5.refs_7_
  19.9 0.0 collective-permute-done.7.refs_9_
  19.9 2.4 %shard_map.67 = bf16[128,1024]{1,0:T(8,128)(2,1)} custom-call(bf16[1024,128]{1,0:T(8,128)(2,1)S(1)} %get-tuple-element.21.moved_ref.refs_0_, f32[1024,128]{1,0:T(8,128)S(1)} %get-tuple-element.25.refs_1_, f32[1024,128]{1,0:T(8,128)S(1)} %get-tuple-element.26.refs_2_, f32[1024,128]{1,0:T(8,128)S(1)} %get-tuple-element.27.refs_3_, ...), custom_call_target="tpu_custom_call" | custom-call | flops 1000000000 | bytes 1048576 | tf_op jit(solution)/shard_map/pallas_call | solution.py:296
  (6 shorter events, 0.0 us)
Async XLA Ops:
  0.0 2.3 %copy-start.1 = (f32[128,2]{0,1:T(2,128)S(1)}, f32[128,2]{0,1:T(2,128)}, u32[]{:S(2)}) copy-start(f32[128,2]{0,1:T(2,128)} %param.10) | copy-start | bytes 3076
  0.0 2.4 %copy-start.2 = (f32[128]{0:T(128)S(1)}, f32[128]{0:T(128)}, u32[]{:S(2)}) copy-start(f32[128]{0:T(128)} %param.11) | copy-start | bytes 1540
  0.0 17.7 %copy-start = (bf16[128,1024]{1,0:T(8,128)(2,1)S(1)}, bf16[128,1024]{1,0:T(8,128)(2,1)}, u32[]{:S(2)}) copy-start(bf16[128,1024]{1,0:T(8,128)(2,1)} %queries_ref.1) | copy-start | bytes 786436
  0.8 4.1 %collective-permute-start = (bf16[192,128]{1,0:T(8,128)(2,1)S(1)}, bf16[192,128]{1,0:T(8,128)(2,1)S(1)}, u32[]{:S(2)}, u32[]{:S(2)}) collective-permute-start(bf16[192,128]{1,0:T(8,128)(2,1)S(1)} %pad_maximum_fusion.own_ref), channel_id=1, source_target_pairs={{0,1},{1,0},{2,3},{3,2},{4,5},{5,4},{6,7},{7,6},{8,9},{9,8},{10,11... | collective-permute-start | bytes 147464 | tf_op jit(solution)/shard_map/ppermute | solution.py:251
  7.4 4.7 %collective-permute-start.2 = (bf16[128,384]{1,0:T(8,128)(2,1)S(1)}, bf16[128,384]{1,0:T(8,128)(2,1)S(1)}, u32[]{:S(2)}, u32[]{:S(2)}) collective-permute-start(bf16[128,384]{1,0:T(8,128)(2,1)S(1)} %get-tuple-element.20.pack_ref), channel_id=1, source_target_pairs={{0,8},{4,12},{8,16},{12,20},{16,24},{20,28},{24,0},{28,4},{1,9},{5... | collective-permute-start | bytes 294920 | tf_op jit(solution)/shard_map/ppermute | solution.py:277
  7.5 9.7 %collective-permute-start.4 = (bf16[128,384]{1,0:T(8,128)(2,1)S(1)}, bf16[128,384]{1,0:T(8,128)(2,1)S(1)}, u32[]{:S(2)}, u32[]{:S(2)}) collective-permute-start(bf16[128,384]{1,0:T(8,128)(2,1)S(1)} %get-tuple-element.20.pack_ref), channel_id=1, source_target_pairs={{0,16},{4,20},{8,24},{12,28},{16,0},{20,4},{24,8},{28,12},{1,17},{... | collective-permute-start | bytes 294920 | tf_op jit(solution)/shard_map/ppermute | solution.py:277
  9.4 7.8 %collective-permute-start.6 = (bf16[128,384]{1,0:T(8,128)(2,1)S(1)}, bf16[128,384]{1,0:T(8,128)(2,1)S(1)}, u32[]{:S(2)}, u32[]{:S(2)}) collective-permute-start(bf16[128,384]{1,0:T(8,128)(2,1)S(1)} %get-tuple-element.20.pack_ref), channel_id=1, source_target_pairs={{0,24},{4,28},{8,0},{12,4},{16,8},{20,12},{24,16},{28,20},{1,25},{... | collective-permute-start | bytes 294920 | tf_op jit(solution)/shard_map/ppermute | solution.py:277
  9.8 8.9 %collective-permute-start.1 = (bf16[128,384]{1,0:T(8,128)(2,1)S(1)}, bf16[128,384]{1,0:T(8,128)(2,1)S(1)}, u32[]{:S(2)}, u32[]{:S(2)}) collective-permute-start(bf16[128,384]{1,0:T(8,128)(2,1)S(1)} %get-tuple-element.20.pack_ref), channel_id=1, source_target_pairs={{0,4},{4,0},{8,12},{12,8},{16,20},{20,16},{24,28},{28,24},{1,5},{5... | collective-permute-start | bytes 294920 | tf_op jit(solution)/shard_map/ppermute | solution.py:270
  12.1 6.7 %collective-permute-start.3 = (bf16[128,384]{1,0:T(8,128)(2,1)S(1)}, bf16[128,384]{1,0:T(8,128)(2,1)S(1)}, u32[]{:S(2)}, u32[]{:S(2)}) collective-permute-start(bf16[128,384]{1,0:T(8,128)(2,1)S(1)} %collective-permute-done.2.straight_ref), channel_id=1, source_target_pairs={{0,4},{4,0},{8,12},{12,8},{16,20},{20,16},{24,28},{28,24},{1,5},{5... | collective-permute-start | bytes 294920 | tf_op jit(solution)/shard_map/ppermute | solution.py:270
  17.2 2.7 %collective-permute-start.5 = (bf16[128,384]{1,0:T(8,128)(2,1)S(1)}, bf16[128,384]{1,0:T(8,128)(2,1)S(1)}, u32[]{:S(2)}, u32[]{:S(2)}) collective-permute-start(bf16[128,384]{1,0:T(8,128)(2,1)S(1)} %collective-permute-done.4.refs_6_), channel_id=1, source_target_pairs={{0,4},{4,0},{8,12},{12,8},{16,20},{20,16},{24,28},{28,24},{1,5},{5... | collective-permute-start | bytes 294920 | tf_op jit(solution)/shard_map/ppermute | solution.py:270
  17.2 2.7 %collective-permute-start.7 = (bf16[128,384]{1,0:T(8,128)(2,1)S(1)}, bf16[128,384]{1,0:T(8,128)(2,1)S(1)}, u32[]{:S(2)}, u32[]{:S(2)}) collective-permute-start(bf16[128,384]{1,0:T(8,128)(2,1)S(1)} %collective-permute-done.6.refs_8_), channel_id=1, source_target_pairs={{0,4},{4,0},{8,12},{12,8},{16,20},{20,16},{24,28},{28,24},{1,5},{5... | collective-permute-start | bytes 294920 | tf_op jit(solution)/shard_map/ppermute | solution.py:270

commit v4 on v3

--- a/solution.py
+++ b/solution.py
@@ -11,7 +11,8 @@
 WIDE = jnp.float32
 NARROW = jnp.bfloat16
 MASKED = -1e30
-OWN_PIECES, NEAR_PIECES, FAR_PIECES = 1,2,4
+LAST_PIECES, LAST_GROUPS = 4, 2
+OWN_PIECES, NEAR_PIECES = 1, 2
 
 
 def halves(x):
@@ -32,44 +33,70 @@
     )
 
 
-def prepare(own_ref, other_ref, small_ref, pack_ref, solved_ref, sides_ref, coef_ref, full_ref):
-    half, length = own_ref.shape[0] // 3, own_ref.shape[1]
-    width = 2 * half
+def whole(full_ref, own, other, parity):
+    half = own.shape[0]
+    full_ref[pl.ds(parity * half, half), :] = own
+    full_ref[pl.ds((1 - parity) * half, half), :] = other
+    return full_ref[...]
+
+
+def invert(own_ref, other_ref, small_ref, inverse_ref, across_ref, dirs_ref, coef_ref, full_ref):
+    length = own_ref.shape[1]
     place = lax.axis_index("head")
     parity = place % 2
-    for part in range(3):
-        rows = pl.ds(part * half, half)
-        full_ref[part, pl.ds(parity * half, half), :] = own_ref[rows, :]
-        full_ref[part, pl.ds((1 - parity) * half, half), :] = other_ref[rows, :]
-    keys_t, values_t, dirs_t = full_ref[0], full_ref[1], full_ref[2]
+    dirs_t = whole(full_ref, own_ref[...], other_ref[...], parity)
+    across_ref[...] = dirs_t
     dirs_wide = dirs_t.astype(WIDE)
     dirs = dirs_wide.T.astype(NARROW)
+    dirs_ref[...] = dirs
     power = jnp.sum(dirs_wide * dirs_wide, axis=0, keepdims=True) + 1e-06
-    coef = small_ref[:1, :] / power
+    coef = small_ref[pl.ds(place // 2, 1), :] / power
+    coef_ref[...] = jnp.broadcast_to(coef, coef_ref.shape)
 
     row = lax.broadcasted_iota(jnp.int32, (length, length), 0)
     col = lax.broadcasted_iota(jnp.int32, (length, length), 1)
-    sides = jnp.concatenate([dirs_t, keys_t], axis=1)
-    meets = dot(dirs, sides)
-    below = jnp.where(row > col, meets[:, :length] * coef, 0.0)
-    reach = jnp.where(row > col, meets[:, length:], 0.0)
+    below = jnp.where(row > col, dot(dirs, dirs_t) * coef, 0.0)
 
     inverse = jnp.where(row == col, 1.0, 0.0) - jnp.where((row ^ col) == 1, below, 0.0)
     block = 2
     while block < length:
-        joint = jnp.where((row // block) ^ (col // block) == 1, below, 0.0)
+        joint = halves(jnp.where((row // block) ^ (col // block) == 1, below, 0.0))
         parts = halves(inverse)
-        inverse = inverse - dot3(parts, halves(dot3(halves(joint), parts)))
+        step = block if block % 8 == 0 else length
+        starts = range(step % length, length, 2 * step)
+        lower = [jnp.concatenate([p[s : s + step] for s in starts], axis=0) for p in parts]
+        change = dot3(halves(dot3(lower, joint)), parts)
+        if step == length:
+            inverse = inverse - change
+        else:
+            rows = []
+            for at, start in enumerate(starts):
+                rows.append(inverse[start - step : start])
+                rows.append(inverse[start : start + step] - change[at * step : (at + 1) * step])
+            inverse = jnp.concatenate(rows, axis=0)
         block *= 2
-
-    top, low = halves(inverse)
-    reach_top, reach_low = halves(reach)
+    inverse_ref[0], inverse_ref[1] = halves(inverse)
+
+
+def prepare(
+    own_ref, other_ref, inverse_ref, across_ref, dirs_ref, coef_ref,
+    pack_ref, solved_ref, sides_ref, full_ref,
+):
+    half, length = own_ref.shape[0] // 2, own_ref.shape[1]
+    width = 2 * half
+    parity = lax.axis_index("head") % 2
+    keys_t = whole(full_ref.at[0], own_ref[:half, :], other_ref[:half, :], parity)
+    values_t = whole(full_ref.at[1], own_ref[half:, :], other_ref[half:, :], parity)
+    dirs_t, dirs = across_ref[...], dirs_ref[...]
+    row = lax.broadcasted_iota(jnp.int32, (length, length), 0)
+    col = lax.broadcasted_iota(jnp.int32, (length, length), 1)
+    top, low = inverse_ref[0], inverse_ref[1]
+    reach_top, reach_low = halves(jnp.where(row > col, dot(dirs, keys_t), 0.0))
     right = jnp.concatenate([reach_top, dirs], axis=1)
     solved = dot(jnp.concatenate([top, low], axis=1), jnp.concatenate([right, right], axis=0))
     solved_reach = solved[:, :length] + dot(top, reach_low)
-    solved = jnp.concatenate([solved_reach, solved[:, length:]], axis=1)
-    solved_parts = halves(solved)
-    change = dot3(halves(dirs_wide * coef), solved_parts)
+    solved_parts = halves(jnp.concatenate([solved_reach, solved[:, length:]], axis=1))
+    change = dot3(halves(dirs_t.astype(WIDE) * coef_ref[:1, :]), solved_parts)
     pack_ref[:, :length] = (keys_t.astype(WIDE) - change[:, :length]).astype(NARROW)
     row_w = lax.broadcasted_iota(jnp.int32, (width, width), 0)
     col_w = lax.broadcasted_iota(jnp.int32, (width, width), 1)
@@ -78,8 +105,7 @@
     pack_ref[:, length + width :] = values_t.astype(WIDE).T.astype(NARROW)
     solved_ref[0] = solved_parts[0]
     solved_ref[1] = solved_parts[1]
-    sides_ref[...] = sides
-    coef_ref[...] = jnp.broadcast_to(coef, coef_ref.shape)
+    sides_ref[...] = jnp.concatenate([dirs_t, keys_t], axis=1)
 
 
 def own_segment(
@@ -142,11 +168,19 @@
     return travel
 
 
-def take_in(query, keys, values, first, last, peak, total, mix):
+def pairs_of(far):
+    order = []
+    for straight, crossed in zip(far[::2], far[1::2]):
+        order += [(straight, crossed), (crossed, straight)]
+    return order
+
+
+def take_in(query, keys, values, limits, peak, total, mix):
     width = mix.shape[1]
     scores = dot(query, keys)
-    column = lax.broadcasted_iota(jnp.int32, scores.shape, 1)
-    scores = jnp.where((column >= first) & (column < last), scores, MASKED)
+    if limits is not None:
+        column = lax.broadcasted_iota(jnp.int32, scores.shape, 1)
+        scores = jnp.where((column >= limits[0]) & (column < limits[1]), scores, MASKED)
     above = jnp.maximum(peak, jnp.max(scores, axis=1, keepdims=True))
     fade = powers(peak, above, width)
     level = jnp.concatenate([above] * (scores.shape[1] // width), axis=1)
@@ -167,18 +201,27 @@
     length = mate_ref.shape[1] - 2 * width
     place = lax.axis_index("seq")
     core, chip_place = place % 2, place // 2
-    order = [mate_ref, (straight_ref, crossed_ref), (crossed_ref, straight_ref)]
-    travel_out[...] = gather(order, core, keys_ref, values_ref, None, length)
-    first = (1 - core) * length
-    last = jnp.where(chip_place > 0, 3, 1) * length
-    for part in pieces(moved_ref.shape[0], NEAR_PIECES):
-        peak_out[part, :], sum_out[part, :], mix_out[part, :] = take_in(
-            moved_ref[part, :], keys_ref[...], values_ref[...], first, last,
-            peak_ref[part, :], sum_ref[part, :], mix_ref[part, :],
-        )
-
-
-def attend_far(*refs):
+
+    def absorb(span, limits):
+        for part in pieces(moved_ref.shape[0], NEAR_PIECES):
+            peak_out[part, :], sum_out[part, :], mix_out[part, :] = take_in(
+                moved_ref[part, :], keys_ref[:, span], values_ref[span, :], limits,
+                peak_ref[part, :], sum_ref[part, :], mix_ref[part, :],
+            )
+
+    @pl.when(chip_place > 0)
+    def _():
+        order = [mate_ref] + pairs_of([straight_ref, crossed_ref])
+        travel_out[...] = gather(order, core, keys_ref, values_ref, None, length)
+        absorb(pl.ds(0, 3 * length), ((1 - core) * length, 3 * length))
+
+    @pl.when((chip_place == 0) & (core == 1))
+    def _():
+        gather([mate_ref], core, keys_ref, values_ref, None, length)
+        absorb(pl.ds(0, length), None)
+
+
+def attend_last(*refs):
     moved_ref, peak_ref, sum_ref, mix_ref, travel_ref, small_ref = refs[:6]
     out_ref, keys_ref, values_ref, done_ref, sem = refs[-5:]
     far = refs[6:-5]
@@ -194,30 +237,35 @@
     def finish(part, total, mix):
         square = jnp.mean(mix * mix, axis=1, keepdims=True)
         strength = lax.rsqrt(square + 1e-06 * (total * total))
-        normed = (mix * strength * small_ref[1:2, :]).astype(NARROW)
+        normed = (mix * strength * small_ref[small_ref.shape[0] - 1 :, :]).astype(NARROW)
         for at in range(0, part.size, length):
             head = (part.start + at) // length
             done_ref[:, pl.ds(head * width, width)] = normed[at : at + length]
-            out_copy(head).start()
+
+    def run(states):
+        parts = pieces(moved_ref.shape[0], LAST_PIECES)
+        group = len(parts) // LAST_GROUPS
+        for at in range(0, len(parts), group):
+            for part in parts[at : at + group]:
+                finish(part, *states(part))
+            first = parts[at].start // length
+            for head in range(first, first + group * parts[at].size // length):
+                out_copy(head).start()
 
     @pl.when(chip_place > 1)
     def _():
-        order = []
-        for straight, crossed in zip(far[::2], far[1::2]):
-            order += [(straight, crossed), (crossed, straight)]
-        gather(order, core, keys_ref, values_ref, travel_ref[...], length)
-        last = 2 * (chip_place - 1) * length
-        for part in pieces(moved_ref.shape[0], FAR_PIECES):
-            _, total, mix = take_in(
-                moved_ref[part, :], keys_ref[...], values_ref[...], 0, last,
+        gather(pairs_of(far), core, keys_ref, values_ref, travel_ref[...], length)
+        limits = (0, 2 * (chip_place - 1) * length) if len(far) > 2 else None
+        run(
+            lambda part: take_in(
+                moved_ref[part, :], keys_ref[...], values_ref[...], limits,
                 peak_ref[part, :], sum_ref[part, :], mix_ref[part, :],
-            )
-            finish(part, total, mix)
-
-    @pl.when(chip_place <= 1)
+            )[1:]
+        )
+
+    @pl.when(jnp.logical_not(chip_place > 1))
     def _():
-        for part in pieces(moved_ref.shape[0], heads):
-            finish(part, sum_ref[part, :], mix_ref[part, :])
+        run(lambda part: (sum_ref[part, :], mix_ref[part, :]))
 
     for head in range(heads):
         out_copy(head).wait()
@@ -227,13 +275,14 @@
 ANYWHERE = pl.BlockSpec(memory_space=pltpu.HBM)
 
 
-def call(kernel, outs, count, scratch=(), flops=1e8, spots=None):
+def call(kernel, outs, count, scratch=(), flops=1e8, spots=None, aliases=None):
     return pl.pallas_call(
         kernel,
         out_shape=outs,
         in_specs=[LOCAL] * count,
         out_specs=spots or jax.tree.map(lambda _: LOCAL, outs),
         scratch_shapes=list(scratch),
+        input_output_aliases=aliases or {},
         compiler_params=pltpu.CompilerParams(vmem_limit_bytes=16 << 20),
         cost_estimate=pl.CostEstimate(
             flops=int(flops), bytes_accessed=1 << 20, transcendentals=1 << 17
@@ -246,28 +295,36 @@
     width = 2 * half
     heads = queries.shape[1] // width
     segments = lax.axis_size("seq")
-    own = jnp.concatenate([keys.T, values.T, directions.T], axis=0)
     places = range(lax.axis_size("head"))
-    other = lax.ppermute(own, "head", [(place, place ^ 1) for place in places])
+
+    def partner(block):
+        return lax.ppermute(block, "head", [(place, place ^ 1) for place in places])
+
+    other_dirs = partner(directions.T)
+    own = jnp.concatenate([keys.T, values.T], axis=0)
+    other = partner(own)
     shape = jax.ShapeDtypeStruct
-    group = lax.axis_index("head") // 2
-    chosen = jnp.arange(beta.shape[1]) == group
-    strengths = jnp.sum(jnp.where(chosen[:, None], beta.T, 0.0), axis=0, keepdims=True)
-    small = jnp.concatenate([strengths, gain.reshape(1, -1)], axis=0)
-    pack, solved, sides, coef = call(
+    small = jnp.concatenate([beta.T, gain.reshape(1, -1)], axis=0)
+    square = shape((width, length), NARROW)
+    inverse, dirs_t, dirs, coef = call(
+        invert,
+        (shape((2, length, length), NARROW), square, square, shape((8, length), WIDE)),
+        3,
+        [pltpu.VMEM((width, length), NARROW)],
+    )(directions.T, other_dirs, small)
+    pack, solved, sides = call(
         prepare,
         (
             shape((width, 2 * length + width), NARROW),
             shape((2, length, length + width), NARROW),
             shape((width, 2 * length), NARROW),
-            shape((8, length), WIDE),
         ),
-        3,
-        [pltpu.VMEM((3, width, length), NARROW)],
-    )(own, other, small)
-
-    def across(block):
-        return lax.ppermute(block, "seq", [(i, i ^ 1) for i in range(segments)])
+        6,
+        [pltpu.VMEM((2, width, length), NARROW)],
+    )(own, other, inverse, dirs_t, dirs, coef)
+
+    def across(block, first=0):
+        return lax.ppermute(block, "seq", [(i, i ^ 1) for i in range(2 * first, segments)])
 
     mate = across(pack)
     chips = segments // 2
@@ -287,14 +344,16 @@
         ]
 
     crossed = across(far[0])
-    *state, travel = call(
-        attend_near, state_shape + (shape((width, width), WIDE),), 7, stores(3)
-    )(moved, *state, mate, far[0], crossed)
+    states = state_shape + (shape((width, width), WIDE),)
+    in_place = {1: 0, 2: 1, 3: 2}
+    *state, travel = call(attend_near, states, 7, stores(3), aliases=in_place)(
+        moved, *state, mate, far[0], crossed
+    )
     blocks = []
     for chip in range(2, chips):
         blocks += [far[chip - 1], across(far[chip - 1])]
     return call(
-        attend_far,
+        attend_last,
         shape((length, heads * width), NARROW),
         6 + len(blocks),
         stores(2 * (chips - 2))

time: 22.6 us -> 22 us (0.973)
  waiting for transfers between devices: 9.86 us -> 8.01 us
  local copies, waits for them, and re-layouts: 0.01 us -> 0.69 us
  starting transfers between devices: 4.41 us -> 4.96 us
    pallas_call x1, Pallas kernels: 2.51 us -> 0.5 us  [shards(): call(prepare, (shape((width, 2 * length + width), NARROW), shape((2, leng...]
    pallas_call x2 -> x3, Pallas kernels: 3.55 us -> 5.54 us  [the longest x1 2.46 us: shards(): call(attend_last, shape((length, heads * width), NARROW), 6 + len(blocks)...]
    ppermute x5 -> x6, waiting for transfers between devices: 2.5 us -> 0.92 us  [the longest x2 0.91 us: partner(): return lax.ppermute(block, 'head', [(place, place ^ 1) for place in places])]
    unnamed x6 -> x8, local copies, waits for them, and re-layouts: 0.01 us -> 0.69 us
    ppermute x5 -> x6, starting transfers between devices: 2.01 us -> 2.54 us  [the longest x2 2.03 us: partner(): return lax.ppermute(block, 'head', [(place, place ^ 1) for place in places])]
    ppermute x3, waiting for transfers between devices: 7.36 us -> 7.09 us  [shards(): far.append(lax.ppermute(pack, 'seq', pairs))]
  transfers between devices with their start and end apart: 8 -> 9, of which waited for: 3 -> 4; matrix products, arithmetic and copies ran while one was open for 0% -> 4% of each run, Pallas kernels for 10% -> 19%
where the time goes in v4:
time: 22 us; the launch traced here: 21.5 us
  waiting for transfers between devices  8.01 us (36%)
  Pallas kernels  7.05 us (32%)
  starting transfers between devices  4.96 us (23%)
  other arithmetic  0.76 us (3%)
  local copies, waits for them, and re-layouts  0.69 us (3%)
    ppermute x3, waiting for transfers between devices, shards(): far.append(lax.ppermute(pack, 'seq', pairs))  7.09 us
    pallas_call x1, Pallas kernels, shards(): call(attend_last, shape((length, heads * width), NARROW), 6 + len(blocks)...  2.46 us
    ppermute x3, starting transfers between devices, shards(): far.append(lax.ppermute(pack, 'seq', pairs))  2.42 us
    ppermute x2, starting transfers between devices, partner(): return lax.ppermute(block, 'head', [(place, place ^ 1) for place in places])  2.03 us
    pallas_call x1, Pallas kernels, shards(): call(invert, (shape((2, length, length), NARROW), square, square, shape((...  1.75 us
    pallas_call x1, Pallas kernels, shards(): call(attend_near, states, 7, stores(3), aliases=in_place)  1.32 us
    pallas_call x1, Pallas kernels, shards(): call(own_segment, (shape((heads * length, width), NARROW),) + state_shape...  1.01 us
    ppermute x2, waiting for transfers between devices, partner(): return lax.ppermute(block, 'head', [(place, place ^ 1) for place in places])  0.91 us
  transfers between devices with their start and end apart: 9, of which 4 were waited for; matrix products, arithmetic and copies ran while one was open for 4% of the time, Pallas kernels for 19%

profile of v4, /device:TPU:24, one launch (start us, length us, event | category | flops | bytes accessed | tf_op | source)
XLA Modules:
  0.0 21.5 jit_solution(3471834661364218965)
XLA Ops:
  0.0 1.5 %collective-permute-start.1 = (bf16[64,128]{1,0:T(8,128)(2,1)}, bf16[64,128]{1,0:T(8,128)(2,1)S(1)}, u32[]{:S(2)}, u32[]{:S(2)}) collective-permute-start(bf16[64,128]{1,0:T(8,128)(2,1)} %bitcast.5), channel_id=1, source_target_pairs={{0,1},{1,0},{2,3},{3,2},{4,5},{5,4},{6,7},{7,6},{8,9},{9,8},{10,11... | collective-permute-start | bytes 49160 | tf_op jit(solution)/shard_map/ppermute | solution.py:301
  1.5 0.7 %pad_maximum_fusion.own_ref = bf16[128,128]{1,0:T(8,128)(2,1)S(1)} fusion(bf16[64,128]{1,0:T(8,128)(2,1)} %bitcast.7, bf16[64,128]{1,0:T(8,128)(2,1)} %bitcast.8), kind=kLoop, calls=%fused_computation | loop fusion | flops 65536 | bytes 65536 | tf_op jit(solution)/shard_map/concatenate | solution.py:304
  2.2 0.5 %collective-permute-start = (bf16[128,128]{1,0:T(8,128)(2,1)S(1)}, bf16[128,128]{1,0:T(8,128)(2,1)S(1)}, u32[]{:S(2)}, u32[]{:S(2)}) collective-permute-start(bf16[128,128]{1,0:T(8,128)(2,1)S(1)} %pad_maximum_fusion.own_ref), channel_id=1, source_target_pairs={{0,1},{1,0},{2,3},{3,2},{4,5},{5,4},{6,7},{7,6},{8,9},{9,8},{10,11... | collective-permute-start | bytes 98312 | tf_op jit(solution)/shard_map/ppermute | solution.py:301
  2.8 0.7 %copy-done.2 = f32[128,2]{0,1:T(2,128)S(1)} copy-done((f32[128,2]{0,1:T(2,128)S(1)}, f32[128,2]{0,1:T(2,128)}, u32[]{:S(2)}) %copy-start.2) | copy-done | bytes 1048
  3.5 0.5 %collective-permute-done.1.other_ref = bf16[64,128]{1,0:T(8,128)(2,1)S(1)} collective-permute-done((bf16[64,128]{1,0:T(8,128)(2,1)}, bf16[64,128]{1,0:T(8,128)(2,1)S(1)}, u32[]{:S(2)}, u32[]{:S(2)}) %collective-permute-start.1) | collective-permute-done | bytes 16416 | tf_op jit(solution)/shard_map/ppermute | solution.py:301
  4.0 1.8 %shard_map.64 = (bf16[2,128,128]{2,1,0:T(8,128)(2,1)S(1)}, bf16[128,128]{1,0:T(8,128)(2,1)S(1)}, bf16[128,128]{1,0:T(8,128)(2,1)S(1)}, f32[8,128]{1,0:T(8,128)S(1)}) custom-call(bf16[64,128]{1,0:T(8,128)(2,1)S(1)} %bitcast.6, bf16[64,128]{1,0:T(8,128)(2,1)S(1)} %collective-permute-done.1.other_ref, f32[3,128]{1,0:T(4,128)S(1)} %pad_maximum_fusion.1.small_ref.refs_5_), custom_call_target="tpu_custom_call" | custom-call | flops 100000000 | bytes 1048576 | tf_op jit(solution)/shard_map/pallas_call | solution.py:309
  5.7 0.0 copy-start
  5.7 0.4 %collective-permute-done.other_ref = bf16[128,128]{1,0:T(8,128)(2,1)S(1)} collective-permute-done((bf16[128,128]{1,0:T(8,128)(2,1)S(1)}, bf16[128,128]{1,0:T(8,128)(2,1)S(1)}, u32[]{:S(2)}, u32[]{:S(2)}) %collective-permute-start) | collective-permute-done | bytes 32800 | tf_op jit(solution)/shard_map/ppermute | solution.py:301
  6.2 0.5 %shard_map.65 = (bf16[128,384]{1,0:T(8,128)(2,1)S(1)}, bf16[2,128,256]{2,1,0:T(8,128)(2,1)S(1)}, bf16[128,256]{1,0:T(8,128)(2,1)S(1)}) custom-call(bf16[128,128]{1,0:T(8,128)(2,1)S(1)} %pad_maximum_fusion.own_ref, bf16[128,128]{1,0:T(8,128)(2,1)S(1)} %collective-permute-done.other_ref, bf16[2,128,128]{2,1,0:T(8,128)(2,1)S(1)} %get-tuple-element.20.inverse_ref, ...), custom_call_target="tpu_custom_call" | custom-call | flops 100000000 | bytes 1048576 | tf_op jit(solution)/shard_map/pallas_call | solution.py:315
  6.7 0.3 %collective-permute-start.3 = (bf16[128,384]{1,0:T(8,128)(2,1)S(1)}, bf16[128,384]{1,0:T(8,128)(2,1)S(1)}, u32[]{:S(2)}, u32[]{:S(2)}) collective-permute-start(bf16[128,384]{1,0:T(8,128)(2,1)S(1)} %get-tuple-element.26.pack_ref), channel_id=1, source_target_pairs={{0,8},{4,12},{8,16},{12,20},{16,24},{20,28},{24,0},{28,4},{1,9},{5... | collective-permute-start | bytes 294920 | tf_op jit(solution)/shard_map/ppermute | solution.py:334
  6.9 1.7 %collective-permute-start.5 = (bf16[128,384]{1,0:T(8,128)(2,1)S(1)}, bf16[128,384]{1,0:T(8,128)(2,1)S(1)}, u32[]{:S(2)}, u32[]{:S(2)}) collective-permute-start(bf16[128,384]{1,0:T(8,128)(2,1)S(1)} %get-tuple-element.26.pack_ref), channel_id=1, source_target_pairs={{0,16},{4,20},{8,24},{12,28},{16,0},{20,4},{24,8},{28,12},{1,17},{... | collective-permute-start | bytes 294920 | tf_op jit(solution)/shard_map/ppermute | solution.py:334
  8.6 0.5 %collective-permute-start.7 = (bf16[128,384]{1,0:T(8,128)(2,1)S(1)}, bf16[128,384]{1,0:T(8,128)(2,1)S(1)}, u32[]{:S(2)}, u32[]{:S(2)}) collective-permute-start(bf16[128,384]{1,0:T(8,128)(2,1)S(1)} %get-tuple-element.26.pack_ref), channel_id=1, source_target_pairs={{0,24},{4,28},{8,0},{12,4},{16,8},{20,12},{24,16},{28,20},{1,25},{... | collective-permute-start | bytes 294920 | tf_op jit(solution)/shard_map/ppermute | solution.py:334
  9.1 0.0 collective-permute-start.2
  9.1 2.2 %collective-permute-done.3.straight_ref = bf16[128,384]{1,0:T(8,128)(2,1)S(1)} collective-permute-done((bf16[128,384]{1,0:T(8,128)(2,1)S(1)}, bf16[128,384]{1,0:T(8,128)(2,1)S(1)}, u32[]{:S(2)}, u32[]{:S(2)}) %collective-permute-start.3) | collective-permute-done | bytes 98336 | tf_op jit(solution)/shard_map/ppermute | solution.py:334
  11.3 0.0 collective-permute-start.4
  11.3 4.8 %collective-permute-done.5.refs_6_ = bf16[128,384]{1,0:T(8,128)(2,1)S(1)} collective-permute-done((bf16[128,384]{1,0:T(8,128)(2,1)S(1)}, bf16[128,384]{1,0:T(8,128)(2,1)S(1)}, u32[]{:S(2)}, u32[]{:S(2)}) %collective-permute-start.5) | collective-permute-done | bytes 98336 | tf_op jit(solution)/shard_map/ppermute | solution.py:334
  16.2 0.0 collective-permute-start.6
  16.2 0.0 collective-permute-done.7.refs_8_
  16.2 0.5 %collective-permute-start.8 = (bf16[128,384]{1,0:T(8,128)(2,1)S(1)}, bf16[128,384]{1,0:T(8,128)(2,1)S(1)}, u32[]{:S(2)}, u32[]{:S(2)}) collective-permute-start(bf16[128,384]{1,0:T(8,128)(2,1)S(1)} %collective-permute-done.7.refs_8_), channel_id=1, source_target_pairs={{0,4},{4,0},{8,12},{12,8},{16,20},{20,16},{24,28},{28,24},{1,5},{5... | collective-permute-start | bytes 294920 | tf_op jit(solution)/shard_map/ppermute | solution.py:327
  16.7 1.0 %shard_map.66 = (bf16[1024,128]{1,0:T(8,128)(2,1)S(1)}, f32[1024,128]{1,0:T(8,128)S(1)}, f32[1024,128]{1,0:T(8,128)S(1)}, f32[1024,128]{1,0:T(8,128)S(1)}) custom-call(bf16[128,1024]{1,0:T(8,128)(2,1)S(1)} %copy-done, bf16[2,128,256]{2,1,0:T(8,128)(2,1)S(1)} %get-tuple-element.24.solved_ref, bf16[128,256]{1,0:T(8,128)(2,1)S(1)} %get-tuple-element.25.sides_ref, ...), custom_call_target="tpu_custom_call" | custom-call | flops 100000000 | bytes 1048576 | tf_op jit(solution)/shard_map/pallas_call | solution.py:336
  17.7 0.0 collective-permute-done.2.mate_ref
  17.7 1.3 %shard_map.67 = (f32[1024,128]{1,0:T(8,128)S(1)}, f32[1024,128]{1,0:T(8,128)S(1)}, f32[1024,128]{1,0:T(8,128)S(1)}, f32[128,128]{1,0:T(8,128)S(1)}) custom-call(bf16[1024,128]{1,0:T(8,128)(2,1)S(1)} %get-tuple-element.27.moved_ref.refs_0_, f32[1024,128]{1,0:T(8,128)S(1)} %get-tuple-element.28.peak_ref, ...), custom_call_target="tpu_custom_call", output_to_operand_aliasing={{0}: (1, {}), {1}: (2, {}), {2}: (3, {})} | custom-call | flops 100000000 | bytes 1048576 | tf_op jit(solution)/shard_map/pallas_call | solution.py:349
  19.1 0.0 collective-permute-done.6.refs_7_
  19.1 2.5 %shard_map.68 = bf16[128,1024]{1,0:T(8,128)(2,1)} custom-call(bf16[1024,128]{1,0:T(8,128)(2,1)S(1)} %get-tuple-element.27.moved_ref.refs_0_, f32[1024,128]{1,0:T(8,128)S(1)} %get-tuple-element.31.refs_1_, f32[1024,128]{1,0:T(8,128)S(1)} %get-tuple-element.32.refs_2_, f32[1024,128]{1,0:T(8,128)S(1)} %get-tuple-element.33.refs_3_, ...), custom_call_target="tpu_custom_call" | custom-call | flops 1000000000 | bytes 1048576 | tf_op jit(solution)/shard_map/pallas_call | solution.py:355
  (9 shorter events, 0.0 us)
Async XLA Ops:
  0.0 3.9 %collective-permute-start.1 = (bf16[64,128]{1,0:T(8,128)(2,1)}, bf16[64,128]{1,0:T(8,128)(2,1)S(1)}, u32[]{:S(2)}, u32[]{:S(2)}) collective-permute-start(bf16[64,128]{1,0:T(8,128)(2,1)} %bitcast.5), channel_id=1, source_target_pairs={{0,1},{1,0},{2,3},{3,2},{4,5},{5,4},{6,7},{7,6},{8,9},{9,8},{10,11... | collective-permute-start | bytes 49160 | tf_op jit(solution)/shard_map/ppermute | solution.py:301
  1.5 2.5 %copy-start.1 = (bf16[128,64]{0,1:T(8,128)(2,1)S(1)}, bf16[128,64]{0,1:T(8,128)(2,1)}, u32[]{:S(2)}) copy-start(bf16[128,64]{0,1:T(8,128)(2,1)} %param.9) | copy-start | bytes 49156
  2.2 3.9 %collective-permute-start = (bf16[128,128]{1,0:T(8,128)(2,1)S(1)}, bf16[128,128]{1,0:T(8,128)(2,1)S(1)}, u32[]{:S(2)}, u32[]{:S(2)}) collective-permute-start(bf16[128,128]{1,0:T(8,128)(2,1)S(1)} %pad_maximum_fusion.own_ref), channel_id=1, source_target_pairs={{0,1},{1,0},{2,3},{3,2},{4,5},{5,4},{6,7},{7,6},{8,9},{9,8},{10,11... | collective-permute-start | bytes 98312 | tf_op jit(solution)/shard_map/ppermute | solution.py:301
  2.8 0.7 %copy-start.2 = (f32[128,2]{0,1:T(2,128)S(1)}, f32[128,2]{0,1:T(2,128)}, u32[]{:S(2)}) copy-start(f32[128,2]{0,1:T(2,128)} %param.10) | copy-start | bytes 3076
  2.8 0.7 %copy-start.3 = (f32[128]{0:T(128)S(1)}, f32[128]{0:T(128)}, u32[]{:S(2)}) copy-start(f32[128]{0:T(128)} %param.11) | copy-start | bytes 1540
  5.7 11.0 %copy-start = (bf16[128,1024]{1,0:T(8,128)(2,1)S(1)}, bf16[128,1024]{1,0:T(8,128)(2,1)}, u32[]{:S(2)}) copy-start(bf16[128,1024]{1,0:T(8,128)(2,1)} %queries_ref.1) | copy-start | bytes 786436
  6.7 4.7 %collective-permute-start.3 = (bf16[128,384]{1,0:T(8,128)(2,1)S(1)}, bf16[128,384]{1,0:T(8,128)(2,1)S(1)}, u32[]{:S(2)}, u32[]{:S(2)}) collective-permute-start(bf16[128,384]{1,0:T(8,128)(2,1)S(1)} %get-tuple-element.26.pack_ref), channel_id=1, source_target_pairs={{0,8},{4,12},{8,16},{12,20},{16,24},{20,28},{24,0},{28,4},{1,9},{5... | collective-permute-start | bytes 294920 | tf_op jit(solution)/shard_map/ppermute | solution.py:334
  6.9 9.2 %collective-permute-start.5 = (bf16[128,384]{1,0:T(8,128)(2,1)S(1)}, bf16[128,384]{1,0:T(8,128)(2,1)S(1)}, u32[]{:S(2)}, u32[]{:S(2)}) collective-permute-start(bf16[128,384]{1,0:T(8,128)(2,1)S(1)} %get-tuple-element.26.pack_ref), channel_id=1, source_target_pairs={{0,16},{4,20},{8,24},{12,28},{16,0},{20,4},{24,8},{28,12},{1,17},{... | collective-permute-start | bytes 294920 | tf_op jit(solution)/shard_map/ppermute | solution.py:334
  8.6 7.6 %collective-permute-start.7 = (bf16[128,384]{1,0:T(8,128)(2,1)S(1)}, bf16[128,384]{1,0:T(8,128)(2,1)S(1)}, u32[]{:S(2)}, u32[]{:S(2)}) collective-permute-start(bf16[128,384]{1,0:T(8,128)(2,1)S(1)} %get-tuple-element.26.pack_ref), channel_id=1, source_target_pairs={{0,24},{4,28},{8,0},{12,4},{16,8},{20,12},{24,16},{28,20},{1,25},{... | collective-permute-start | bytes 294920 | tf_op jit(solution)/shard_map/ppermute | solution.py:334
  9.1 8.6 %collective-permute-start.2 = (bf16[128,384]{1,0:T(8,128)(2,1)S(1)}, bf16[128,384]{1,0:T(8,128)(2,1)S(1)}, u32[]{:S(2)}, u32[]{:S(2)}) collective-permute-start(bf16[128,384]{1,0:T(8,128)(2,1)S(1)} %get-tuple-element.26.pack_ref), channel_id=1, source_target_pairs={{0,4},{4,0},{8,12},{12,8},{16,20},{20,16},{24,28},{28,24},{1,5},{5... | collective-permute-start | bytes 294920 | tf_op jit(solution)/shard_map/ppermute | solution.py:327
  11.3 6.4 %collective-permute-start.4 = (bf16[128,384]{1,0:T(8,128)(2,1)S(1)}, bf16[128,384]{1,0:T(8,128)(2,1)S(1)}, u32[]{:S(2)}, u32[]{:S(2)}) collective-permute-start(bf16[128,384]{1,0:T(8,128)(2,1)S(1)} %collective-permute-done.3.straight_ref), channel_id=1, source_target_pairs={{0,4},{4,0},{8,12},{12,8},{16,20},{20,16},{24,28},{28,24},{1,5},{5... | collective-permute-start | bytes 294920 | tf_op jit(solution)/shard_map/ppermute | solution.py:327
  16.2 2.9 %collective-permute-start.6 = (bf16[128,384]{1,0:T(8,128)(2,1)S(1)}, bf16[128,384]{1,0:T(8,128)(2,1)S(1)}, u32[]{:S(2)}, u32[]{:S(2)}) collective-permute-start(bf16[128,384]{1,0:T(8,128)(2,1)S(1)} %collective-permute-done.5.refs_6_), channel_id=1, source_target_pairs={{0,4},{4,0},{8,12},{12,8},{16,20},{20,16},{24,28},{28,24},{1,5},{5... | collective-permute-start | bytes 294920 | tf_op jit(solution)/shard_map/ppermute | solution.py:327
  16.2 2.9 %collective-permute-start.8 = (bf16[128,384]{1,0:T(8,128)(2,1)S(1)}, bf16[128,384]{1,0:T(8,128)(2,1)S(1)}, u32[]{:S(2)}, u32[]{:S(2)}) collective-permute-start(bf16[128,384]{1,0:T(8,128)(2,1)S(1)} %collective-permute-done.7.refs_8_), channel_id=1, source_target_pairs={{0,4},{4,0},{8,12},{12,8},{16,20},{20,16},{24,28},{28,24},{1,5},{5... | collective-permute-start | bytes 294920 | tf_op jit(solution)/shard_map/ppermute | solution.py:327

commit v5 on v4

--- a/solution.py
+++ b/solution.py
@@ -12,6 +12,7 @@
 NARROW = jnp.bfloat16
 MASKED = -1e30
 LAST_PIECES, LAST_GROUPS = 4, 2
+SETTLE_PIECES, SETTLE_GROUPS = 4, 2
 OWN_PIECES, NEAR_PIECES = 1, 2
 
 
@@ -57,8 +58,12 @@
     col = lax.broadcasted_iota(jnp.int32, (length, length), 1)
     below = jnp.where(row > col, dot(dirs, dirs_t) * coef, 0.0)
 
-    inverse = jnp.where(row == col, 1.0, 0.0) - jnp.where((row ^ col) == 1, below, 0.0)
-    block = 2
+    pair = jnp.where((row ^ col) == 1, -below, 0.0)
+    joint = jnp.where((row // 2) ^ (col // 2) == 1, below, 0.0)
+    joint = joint + jnp.sum(pair, axis=1, keepdims=True) * pltpu.roll(joint, 1, 0)
+    joint = joint + pltpu.roll(joint, length - 1, 1) * jnp.sum(pair, axis=0, keepdims=True)
+    inverse = jnp.where(row == col, 1.0, 0.0) + pair - joint
+    block = 4
     while block < length:
         joint = halves(jnp.where((row // block) ^ (col // block) == 1, below, 0.0))
         parts = halves(inverse)
@@ -193,93 +198,119 @@
     return [pl.ds(start, size) for start in range(0, rows, size)]
 
 
-def attend_near(
-    moved_ref, peak_ref, sum_ref, mix_ref, mate_ref, straight_ref, crossed_ref,
-    peak_out, sum_out, mix_out, travel_out, keys_ref, values_ref,
-):
-    width = keys_ref.shape[0]
-    length = mate_ref.shape[1] - 2 * width
-    place = lax.axis_index("seq")
-    core, chip_place = place % 2, place // 2
-
-    def absorb(span, limits):
-        for part in pieces(moved_ref.shape[0], NEAR_PIECES):
-            peak_out[part, :], sum_out[part, :], mix_out[part, :] = take_in(
-                moved_ref[part, :], keys_ref[:, span], values_ref[span, :], limits,
-                peak_ref[part, :], sum_ref[part, :], mix_ref[part, :],
-            )
-
-    @pl.when(chip_place > 0)
-    def _():
-        order = [mate_ref] + pairs_of([straight_ref, crossed_ref])
-        travel_out[...] = gather(order, core, keys_ref, values_ref, None, length)
-        absorb(pl.ds(0, 3 * length), ((1 - core) * length, 3 * length))
-
-    @pl.when((chip_place == 0) & (core == 1))
-    def _():
-        gather([mate_ref], core, keys_ref, values_ref, None, length)
-        absorb(pl.ds(0, length), None)
-
-
-def attend_last(*refs):
-    moved_ref, peak_ref, sum_ref, mix_ref, travel_ref, small_ref = refs[:6]
-    out_ref, keys_ref, values_ref, done_ref, sem = refs[-5:]
-    far = refs[6:-5]
-    length, width = out_ref.shape[0], keys_ref.shape[0]
-    heads = out_ref.shape[1] // width
-    place = lax.axis_index("seq")
-    core, chip_place = place % 2, place // 2
+def settle(out_ref, done_ref, sem, gain, parts, groups, states):
+    length, width = out_ref.shape[0], gain.shape[1]
 
     def out_copy(head):
         cols = pl.ds(head * width, width)
         return pltpu.make_async_copy(done_ref.at[:, cols], out_ref.at[:, cols], sem.at[head])
 
-    def finish(part, total, mix):
-        square = jnp.mean(mix * mix, axis=1, keepdims=True)
-        strength = lax.rsqrt(square + 1e-06 * (total * total))
-        normed = (mix * strength * small_ref[small_ref.shape[0] - 1 :, :]).astype(NARROW)
-        for at in range(0, part.size, length):
-            head = (part.start + at) // length
-            done_ref[:, pl.ds(head * width, width)] = normed[at : at + length]
-
-    def run(states):
+    group = len(parts) // groups
+    for at in range(0, len(parts), group):
+        for part in parts[at : at + group]:
+            total, mix = states(part)
+            square = jnp.mean(mix * mix, axis=1, keepdims=True)
+            strength = lax.rsqrt(square + 1e-06 * (total * total))
+            normed = (mix * strength * gain).astype(NARROW)
+            for start in range(0, part.size, length):
+                head = (part.start + start) // length
+                done_ref[:, pl.ds(head * width, width)] = normed[start : start + length]
+        first = parts[at].start // length
+        for head in range(first, first + group * parts[at].size // length):
+            out_copy(head).start()
+    for head in range(out_ref.shape[1] // width):
+        out_copy(head).wait()
+
+
+def update(moved_ref, olds, news, keys, values, limits):
+    for part in pieces(moved_ref.shape[0], NEAR_PIECES):
+        fresh = take_in(
+            moved_ref[part, :], keys, values, limits, *(old[part, :] for old in olds)
+        )
+        for new, value in zip(news, fresh):
+            new[part, :] = value
+
+
+def attend_near(
+    moved_ref, peak_ref, sum_ref, mix_ref, small_ref, mate_ref, straight_ref, crossed_ref,
+    peak_out, sum_out, mix_out, travel_out, out_ref, keys_ref, values_ref, done_ref, sem,
+):
+    length = out_ref.shape[0]
+    place = lax.axis_index("seq")
+    core, chip_place = place % 2, place // 2
+    olds, news = (peak_ref, sum_ref, mix_ref), (peak_out, sum_out, mix_out)
+
+    @pl.when(chip_place > 0)
+    def _():
+        order = [mate_ref] + pairs_of([straight_ref, crossed_ref])
+        travel_out[...] = gather(order, core, keys_ref, values_ref, None, length)
+        limits = ((1 - core) * length, 3 * length)
+        update(moved_ref, olds, news, keys_ref[...], values_ref[...], limits)
+
+    @pl.when((chip_place == 0) & (core == 1))
+    def _():
+        span = pl.ds(0, length)
+        gather([mate_ref], core, keys_ref, values_ref, None, length)
+        update(moved_ref, olds, news, keys_ref[:, span], values_ref[span, :], None)
+
+    @pl.when(chip_place == 0)
+    def _():
+        parts = pieces(moved_ref.shape[0], SETTLE_PIECES)
+        states = lambda part: (sum_out[part, :], mix_out[part, :])
+        settle(out_ref, done_ref, sem, small_ref[small_ref.shape[0] - 1 :, :], parts, SETTLE_GROUPS, states)
+
+
+def attend_next(
+    moved_ref, peak_ref, sum_ref, mix_ref, travel_ref, out_in, small_ref, straight_ref, crossed_ref,
+    peak_out, sum_out, mix_out, travel_out, out_ref, keys_ref, values_ref, done_ref, sem,
+):
+    length = out_ref.shape[0]
+    place = lax.axis_index("seq")
+    chip_place = place // 2
+    olds, news = (peak_ref, sum_ref, mix_ref), (peak_out, sum_out, mix_out)
+
+    @pl.when(chip_place > 1)
+    def _():
+        order = pairs_of([straight_ref, crossed_ref])
+        travel_out[...] = gather(order, place % 2, keys_ref, values_ref, travel_ref[...], length)
+        update(moved_ref, olds, news, keys_ref[...], values_ref[...], None)
+
+    @pl.when((chip_place == 1) | (chip_place == 2))
+    def _():
+        parts = pieces(moved_ref.shape[0], SETTLE_PIECES)
+        states = lambda part: (sum_out[part, :], mix_out[part, :])
+        settle(out_ref, done_ref, sem, small_ref[small_ref.shape[0] - 1 :, :], parts, SETTLE_GROUPS, states)
+
+
+def attend_last(*refs):
+    moved_ref, peak_ref, sum_ref, mix_ref, travel_ref, _, small_ref = refs[:7]
+    out_ref, keys_ref, values_ref, done_ref, sem = refs[-5:]
+    far = refs[7:-5]
+    length = out_ref.shape[0]
+    place = lax.axis_index("seq")
+    core, chip_place = place % 2, place // 2
+
+    @pl.when(chip_place > 2)
+    def _():
+        gather(pairs_of(far), core, keys_ref, values_ref, travel_ref[...], length)
+        limits = (0, 2 * (chip_place - 2) * length) if len(far) > 2 else None
         parts = pieces(moved_ref.shape[0], LAST_PIECES)
-        group = len(parts) // LAST_GROUPS
-        for at in range(0, len(parts), group):
-            for part in parts[at : at + group]:
-                finish(part, *states(part))
-            first = parts[at].start // length
-            for head in range(first, first + group * parts[at].size // length):
-                out_copy(head).start()
-
-    @pl.when(chip_place > 1)
-    def _():
-        gather(pairs_of(far), core, keys_ref, values_ref, travel_ref[...], length)
-        limits = (0, 2 * (chip_place - 1) * length) if len(far) > 2 else None
-        run(
-            lambda part: take_in(
-                moved_ref[part, :], keys_ref[...], values_ref[...], limits,
-                peak_ref[part, :], sum_ref[part, :], mix_ref[part, :],
-            )[1:]
-        )
-
-    @pl.when(jnp.logical_not(chip_place > 1))
-    def _():
-        run(lambda part: (sum_ref[part, :], mix_ref[part, :]))
-
-    for head in range(heads):
-        out_copy(head).wait()
+        states = lambda part: take_in(
+            moved_ref[part, :], keys_ref[...], values_ref[...], limits,
+            peak_ref[part, :], sum_ref[part, :], mix_ref[part, :],
+        )[1:]
+        settle(out_ref, done_ref, sem, small_ref[small_ref.shape[0] - 1 :, :], parts, LAST_GROUPS, states)
 
 
 LOCAL = pl.BlockSpec(memory_space=pltpu.VMEM)
 ANYWHERE = pl.BlockSpec(memory_space=pltpu.HBM)
 
 
-def call(kernel, outs, count, scratch=(), flops=1e8, spots=None, aliases=None):
+def call(kernel, outs, count, scratch=(), flops=1e8, spots=None, aliases=None, places=None):
     return pl.pallas_call(
         kernel,
         out_shape=outs,
-        in_specs=[LOCAL] * count,
+        in_specs=places or [LOCAL] * count,
         out_specs=spots or jax.tree.map(lambda _: LOCAL, outs),
         scratch_shapes=list(scratch),
         input_output_aliases=aliases or {},
@@ -344,23 +375,38 @@
         ]
 
     crossed = across(far[0])
-    states = state_shape + (shape((width, width), WIDE),)
+    states = state_shape + (shape((width, width), WIDE), shape((length, heads * width), NARROW))
+    spots = (LOCAL,) * 4 + (ANYWHERE,)
+    ends = [pltpu.VMEM((length, heads * width), NARROW), pltpu.SemaphoreType.DMA((heads,))]
     in_place = {1: 0, 2: 1, 3: 2}
-    *state, travel = call(attend_near, states, 7, stores(3), aliases=in_place)(
-        moved, *state, mate, far[0], crossed
-    )
+    *state, travel, out = call(
+        attend_near, states, 8, stores(3) + ends, spots=spots, aliases=in_place
+    )(moved, *state, small, mate, far[0], crossed)
+    places = [ANYWHERE if at == 5 else LOCAL for at in range(9)]
+    crossed = across(far[1])
+    *state, travel, out = call(
+        attend_next,
+        states,
+        9,
+        stores(2) + ends,
+        spots=spots,
+        aliases={**in_place, 4: 3, 5: 4},
+        places=places,
+    )(moved, *state, travel, out, small, far[1], crossed)
     blocks = []
-    for chip in range(2, chips):
+    for chip in range(3, chips):
         blocks += [far[chip - 1], across(far[chip - 1])]
+    count = 7 + len(blocks)
     return call(
         attend_last,
         shape((length, heads * width), NARROW),
-        6 + len(blocks),
-        stores(2 * (chips - 2))
-        + [pltpu.VMEM((length, heads * width), NARROW), pltpu.SemaphoreType.DMA((heads,))],
+        count,
+        stores(2 * (chips - 3)) + ends,
         flops=1e9,
         spots=ANYWHERE,
-    )(moved, *state, travel, small, *blocks)
+        aliases={5: 0},
+        places=[ANYWHERE if at == 5 else LOCAL for at in range(count)],
+    )(moved, *state, travel, out, small, *blocks)
 
 
 def solution(mesh):

time: 22 us -> 22.6 us (1.027)
  Pallas kernels: 7.05 us -> 7.59 us
    pallas_call x2 -> x3, Pallas kernels: 3.78 us -> 4.46 us  [the longest x1 1.81 us: shards(): call(attend_last, shape((length, heads * width), NARROW), count, stores(2...]
  transfers between devices with their start and end apart: 9 -> 9, of which waited for: 4 -> 4; matrix products, arithmetic and copies ran while one was open for 4% -> 3% of each run, Pallas kernels for 19% -> 24%
where the time goes in v5:
time: 22.6 us; the launch traced here: 22.2 us
  waiting for transfers between devices  8.14 us (36%)
  Pallas kernels  7.59 us (34%)
  starting transfers between devices  4.96 us (22%)
  other arithmetic  0.76 us (3%)
  local copies, waits for them, and re-layouts  0.69 us (3%)
    ppermute x3, waiting for transfers between devices, shards(): far.append(lax.ppermute(pack, 'seq', pairs))  7.09 us
    ppermute x3, starting transfers between devices, shards(): far.append(lax.ppermute(pack, 'seq', pairs))  2.41 us
    ppermute x2, starting transfers between devices, partner(): return lax.ppermute(block, 'head', [(place, place ^ 1) for place in places])  2.03 us
    pallas_call x1, Pallas kernels, shards(): call(attend_last, shape((length, heads * width), NARROW), count, stores(2...  1.81 us
    pallas_call x1, Pallas kernels, shards(): call(invert, (shape((2, length, length), NARROW), square, square, shape((...  1.62 us
    pallas_call x1, Pallas kernels, shards(): call(attend_near, states, 8, stores(3) + ends, spots=spots, aliases=in_pl...  1.39 us
    pallas_call x1, Pallas kernels, shards(): call(attend_next, states, 9, stores(2) + ends, spots=spots, aliases={**in...  1.25 us
    ppermute x2, waiting for transfers between devices, partner(): return lax.ppermute(block, 'head', [(place, place ^ 1) for place in places])  1.04 us
  transfers between devices with their start and end apart: 9, of which 4 were waited for; matrix products, arithmetic and copies ran while one was open for 3% of the time, Pallas kernels for 24%

profile of v5, /device:TPU:24, one launch (start us, length us, event | category | flops | bytes accessed | tf_op | source)
XLA Modules:
  0.0 22.2 jit_solution(11784231570631460710)
XLA Ops:
  0.0 1.5 %collective-permute-start.1 = (bf16[64,128]{1,0:T(8,128)(2,1)}, bf16[64,128]{1,0:T(8,128)(2,1)S(1)}, u32[]{:S(2)}, u32[]{:S(2)}) collective-permute-start(bf16[64,128]{1,0:T(8,128)(2,1)} %bitcast.5), channel_id=1, source_target_pairs={{0,1},{1,0},{2,3},{3,2},{4,5},{5,4},{6,7},{7,6},{8,9},{9,8},{10,11... | collective-permute-start | bytes 49160 | tf_op jit(solution)/shard_map/ppermute | solution.py:332
  1.5 0.7 %pad_maximum_fusion.own_ref = bf16[128,128]{1,0:T(8,128)(2,1)S(1)} fusion(bf16[64,128]{1,0:T(8,128)(2,1)} %bitcast.7, bf16[64,128]{1,0:T(8,128)(2,1)} %bitcast.8), kind=kLoop, calls=%fused_computation | loop fusion | flops 65536 | bytes 65536 | tf_op jit(solution)/shard_map/concatenate | solution.py:335
  2.2 0.5 %collective-permute-start = (bf16[128,128]{1,0:T(8,128)(2,1)S(1)}, bf16[128,128]{1,0:T(8,128)(2,1)S(1)}, u32[]{:S(2)}, u32[]{:S(2)}) collective-permute-start(bf16[128,128]{1,0:T(8,128)(2,1)S(1)} %pad_maximum_fusion.own_ref), channel_id=1, source_target_pairs={{0,1},{1,0},{2,3},{3,2},{4,5},{5,4},{6,7},{7,6},{8,9},{9,8},{10,11... | collective-permute-start | bytes 98312 | tf_op jit(solution)/shard_map/ppermute | solution.py:332
  2.8 0.7 %copy-done.2 = f32[128,2]{0,1:T(2,128)S(1)} copy-done((f32[128,2]{0,1:T(2,128)S(1)}, f32[128,2]{0,1:T(2,128)}, u32[]{:S(2)}) %copy-start.2) | copy-done | bytes 1048
  3.5 0.5 %collective-permute-done.1.other_ref = bf16[64,128]{1,0:T(8,128)(2,1)S(1)} collective-permute-done((bf16[64,128]{1,0:T(8,128)(2,1)}, bf16[64,128]{1,0:T(8,128)(2,1)S(1)}, u32[]{:S(2)}, u32[]{:S(2)}) %collective-permute-start.1) | collective-permute-done | bytes 16416 | tf_op jit(solution)/shard_map/ppermute | solution.py:332
  4.0 1.6 %shard_map.64 = (bf16[2,128,128]{2,1,0:T(8,128)(2,1)S(1)}, bf16[128,128]{1,0:T(8,128)(2,1)S(1)}, bf16[128,128]{1,0:T(8,128)(2,1)S(1)}, f32[8,128]{1,0:T(8,128)S(1)}) custom-call(bf16[64,128]{1,0:T(8,128)(2,1)S(1)} %bitcast.6, bf16[64,128]{1,0:T(8,128)(2,1)S(1)} %collective-permute-done.1.other_ref, f32[3,128]{1,0:T(4,128)S(1)} %pad_maximum_fusion.1.small_ref.refs_6_), custom_call_target="tpu_custom_call" | custom-call | flops 100000000 | bytes 1048576 | tf_op jit(solution)/shard_map/pallas_call | solution.py:340
  5.6 0.0 copy-start
  5.6 0.6 %collective-permute-done.other_ref = bf16[128,128]{1,0:T(8,128)(2,1)S(1)} collective-permute-done((bf16[128,128]{1,0:T(8,128)(2,1)S(1)}, bf16[128,128]{1,0:T(8,128)(2,1)S(1)}, u32[]{:S(2)}, u32[]{:S(2)}) %collective-permute-start) | collective-permute-done | bytes 32800 | tf_op jit(solution)/shard_map/ppermute | solution.py:332
  6.2 0.5 %shard_map.65 = (bf16[128,384]{1,0:T(8,128)(2,1)S(1)}, bf16[2,128,256]{2,1,0:T(8,128)(2,1)S(1)}, bf16[128,256]{1,0:T(8,128)(2,1)S(1)}) custom-call(bf16[128,128]{1,0:T(8,128)(2,1)S(1)} %pad_maximum_fusion.own_ref, bf16[128,128]{1,0:T(8,128)(2,1)S(1)} %collective-permute-done.other_ref, bf16[2,128,128]{2,1,0:T(8,128)(2,1)S(1)} %get-tuple-element.26.inverse_ref, ...), custom_call_target="tpu_custom_call" | custom-call | flops 100000000 | bytes 1048576 | tf_op jit(solution)/shard_map/pallas_call | solution.py:346
  6.7 0.3 %collective-permute-start.3 = (bf16[128,384]{1,0:T(8,128)(2,1)S(1)}, bf16[128,384]{1,0:T(8,128)(2,1)S(1)}, u32[]{:S(2)}, u32[]{:S(2)}) collective-permute-start(bf16[128,384]{1,0:T(8,128)(2,1)S(1)} %get-tuple-element.32.pack_ref), channel_id=1, source_target_pairs={{0,8},{4,12},{8,16},{12,20},{16,24},{20,28},{24,0},{28,4},{1,9},{5... | collective-permute-start | bytes 294920 | tf_op jit(solution)/shard_map/ppermute | solution.py:365
  6.9 1.7 %collective-permute-start.5 = (bf16[128,384]{1,0:T(8,128)(2,1)S(1)}, bf16[128,384]{1,0:T(8,128)(2,1)S(1)}, u32[]{:S(2)}, u32[]{:S(2)}) collective-permute-start(bf16[128,384]{1,0:T(8,128)(2,1)S(1)} %get-tuple-element.32.pack_ref), channel_id=1, source_target_pairs={{0,16},{4,20},{8,24},{12,28},{16,0},{20,4},{24,8},{28,12},{1,17},{... | collective-permute-start | bytes 294920 | tf_op jit(solution)/shard_map/ppermute | solution.py:365
  8.6 0.5 %collective-permute-start.7 = (bf16[128,384]{1,0:T(8,128)(2,1)S(1)}, bf16[128,384]{1,0:T(8,128)(2,1)S(1)}, u32[]{:S(2)}, u32[]{:S(2)}) collective-permute-start(bf16[128,384]{1,0:T(8,128)(2,1)S(1)} %get-tuple-element.32.pack_ref), channel_id=1, source_target_pairs={{0,24},{4,28},{8,0},{12,4},{16,8},{20,12},{24,16},{28,20},{1,25},{... | collective-permute-start | bytes 294920 | tf_op jit(solution)/shard_map/ppermute | solution.py:365
  9.1 0.0 collective-permute-start.2
  9.1 2.2 %collective-permute-done.3.straight_ref = bf16[128,384]{1,0:T(8,128)(2,1)S(1)} collective-permute-done((bf16[128,384]{1,0:T(8,128)(2,1)S(1)}, bf16[128,384]{1,0:T(8,128)(2,1)S(1)}, u32[]{:S(2)}, u32[]{:S(2)}) %collective-permute-start.3) | collective-permute-done | bytes 98336 | tf_op jit(solution)/shard_map/ppermute | solution.py:365
  11.3 0.0 collective-permute-start.4
  11.3 4.8 %collective-permute-done.5.straight_ref = bf16[128,384]{1,0:T(8,128)(2,1)S(1)} collective-permute-done((bf16[128,384]{1,0:T(8,128)(2,1)S(1)}, bf16[128,384]{1,0:T(8,128)(2,1)S(1)}, u32[]{:S(2)}, u32[]{:S(2)}) %collective-permute-start.5) | collective-permute-done | bytes 98336 | tf_op jit(solution)/shard_map/ppermute | solution.py:365
  16.2 0.0 collective-permute-start.6
  16.2 0.0 collective-permute-done.7.refs_7_
  16.2 0.5 %collective-permute-start.8 = (bf16[128,384]{1,0:T(8,128)(2,1)S(1)}, bf16[128,384]{1,0:T(8,128)(2,1)S(1)}, u32[]{:S(2)}, u32[]{:S(2)}) collective-permute-start(bf16[128,384]{1,0:T(8,128)(2,1)S(1)} %collective-permute-done.7.refs_7_), channel_id=1, source_target_pairs={{0,4},{4,0},{8,12},{12,8},{16,20},{20,16},{24,28},{28,24},{1,5},{5... | collective-permute-start | bytes 294920 | tf_op jit(solution)/shard_map/ppermute | solution.py:358
  16.7 1.0 %shard_map.66 = (bf16[1024,128]{1,0:T(8,128)(2,1)S(1)}, f32[1024,128]{1,0:T(8,128)S(1)}, f32[1024,128]{1,0:T(8,128)S(1)}, f32[1024,128]{1,0:T(8,128)S(1)}) custom-call(bf16[128,1024]{1,0:T(8,128)(2,1)S(1)} %copy-done, bf16[2,128,256]{2,1,0:T(8,128)(2,1)S(1)} %get-tuple-element.30.solved_ref, bf16[128,256]{1,0:T(8,128)(2,1)S(1)} %get-tuple-element.31.sides_ref, ...), custom_call_target="tpu_custom_call" | custom-call | flops 100000000 | bytes 1048576 | tf_op jit(solution)/shard_map/pallas_call | solution.py:367
  17.7 0.0 collective-permute-done.2.mate_ref
  17.7 1.4 %shard_map.67 = (f32[1024,128]{1,0:T(8,128)S(1)}, f32[1024,128]{1,0:T(8,128)S(1)}, f32[1024,128]{1,0:T(8,128)S(1)}, f32[128,128]{1,0:T(8,128)S(1)}, bf16[128,1024]{1,0:T(8,128)(2,1)}) custom-call(bf16[1024,128]{1,0:T(8,128)(2,1)S(1)} %get-tuple-element.33.moved_ref.refs_0_, ...), custom_call_target="tpu_custom_call", output_to_operand_aliasing={{0}: (1, {}), {1}: (2, {}), {2}: (3, {})} | custom-call | flops 100000000 | bytes 1048576 | tf_op jit(solution)/shard_map/pallas_call | solution.py:382
  19.1 1.3 %shard_map.68 = (f32[1024,128]{1,0:T(8,128)S(1)}, f32[1024,128]{1,0:T(8,128)S(1)}, f32[1024,128]{1,0:T(8,128)S(1)}, f32[128,128]{1,0:T(8,128)S(1)}, bf16[128,1024]{1,0:T(8,128)(2,1)}) custom-call(bf16[1024,128]{1,0:T(8,128)(2,1)S(1)} %get-tuple-element.33.moved_ref.refs_0_, ...), custom_call_target="tpu_custom_call", output_to_operand_aliasing={{0}: (1, {}), {1}: (2, {}), {2}: (3, {}), {3}: (4, {}), {4}... | custom-call | flops 100000000 | bytes 1048576 | tf_op jit(solution)/shard_map/pallas_call | solution.py:387
  20.4 1.8 %shard_map.69 = bf16[128,1024]{1,0:T(8,128)(2,1)} custom-call(bf16[1024,128]{1,0:T(8,128)(2,1)S(1)} %get-tuple-element.33.moved_ref.refs_0_, f32[1024,128]{1,0:T(8,128)S(1)} %get-tuple-element.42.refs_1_, f32[1024,128]{1,0:T(8,128)S(1)} %get-tuple-element.43.refs_2_, f32[1024,128]{1,0:T(8,128)S(1)} %get-tuple-element.44.refs_3_, ...), custom_call_target="tpu_custom_call", output_to_operand_aliasing={{}: (5, {})} | custom-call | flops 1000000000 | bytes 1048576 | tf_op jit(solution)/shard_map/pallas_call | solution.py:400
  (10 shorter events, 0.0 us)
Async XLA Ops:
  0.0 3.9 %collective-permute-start.1 = (bf16[64,128]{1,0:T(8,128)(2,1)}, bf16[64,128]{1,0:T(8,128)(2,1)S(1)}, u32[]{:S(2)}, u32[]{:S(2)}) collective-permute-start(bf16[64,128]{1,0:T(8,128)(2,1)} %bitcast.5), channel_id=1, source_target_pairs={{0,1},{1,0},{2,3},{3,2},{4,5},{5,4},{6,7},{7,6},{8,9},{9,8},{10,11... | collective-permute-start | bytes 49160 | tf_op jit(solution)/shard_map/ppermute | solution.py:332
  1.5 2.5 %copy-start.1 = (bf16[128,64]{0,1:T(8,128)(2,1)S(1)}, bf16[128,64]{0,1:T(8,128)(2,1)}, u32[]{:S(2)}) copy-start(bf16[128,64]{0,1:T(8,128)(2,1)} %param.9) | copy-start | bytes 49156
  2.2 3.9 %collective-permute-start = (bf16[128,128]{1,0:T(8,128)(2,1)S(1)}, bf16[128,128]{1,0:T(8,128)(2,1)S(1)}, u32[]{:S(2)}, u32[]{:S(2)}) collective-permute-start(bf16[128,128]{1,0:T(8,128)(2,1)S(1)} %pad_maximum_fusion.own_ref), channel_id=1, source_target_pairs={{0,1},{1,0},{2,3},{3,2},{4,5},{5,4},{6,7},{7,6},{8,9},{9,8},{10,11... | collective-permute-start | bytes 98312 | tf_op jit(solution)/shard_map/ppermute | solution.py:332
  2.8 0.7 %copy-start.2 = (f32[128,2]{0,1:T(2,128)S(1)}, f32[128,2]{0,1:T(2,128)}, u32[]{:S(2)}) copy-start(f32[128,2]{0,1:T(2,128)} %param.10) | copy-start | bytes 3076
  2.8 0.7 %copy-start.3 = (f32[128]{0:T(128)S(1)}, f32[128]{0:T(128)}, u32[]{:S(2)}) copy-start(f32[128]{0:T(128)} %param.11) | copy-start | bytes 1540
  5.6 11.1 %copy-start = (bf16[128,1024]{1,0:T(8,128)(2,1)S(1)}, bf16[128,1024]{1,0:T(8,128)(2,1)}, u32[]{:S(2)}) copy-start(bf16[128,1024]{1,0:T(8,128)(2,1)} %queries_ref.1) | copy-start | bytes 786436
  6.7 4.7 %collective-permute-start.3 = (bf16[128,384]{1,0:T(8,128)(2,1)S(1)}, bf16[128,384]{1,0:T(8,128)(2,1)S(1)}, u32[]{:S(2)}, u32[]{:S(2)}) collective-permute-start(bf16[128,384]{1,0:T(8,128)(2,1)S(1)} %get-tuple-element.32.pack_ref), channel_id=1, source_target_pairs={{0,8},{4,12},{8,16},{12,20},{16,24},{20,28},{24,0},{28,4},{1,9},{5... | collective-permute-start | bytes 294920 | tf_op jit(solution)/shard_map/ppermute | solution.py:365
  6.9 9.2 %collective-permute-start.5 = (bf16[128,384]{1,0:T(8,128)(2,1)S(1)}, bf16[128,384]{1,0:T(8,128)(2,1)S(1)}, u32[]{:S(2)}, u32[]{:S(2)}) collective-permute-start(bf16[128,384]{1,0:T(8,128)(2,1)S(1)} %get-tuple-element.32.pack_ref), channel_id=1, source_target_pairs={{0,16},{4,20},{8,24},{12,28},{16,0},{20,4},{24,8},{28,12},{1,17},{... | collective-permute-start | bytes 294920 | tf_op jit(solution)/shard_map/ppermute | solution.py:365
  8.6 7.5 %collective-permute-start.7 = (bf16[128,384]{1,0:T(8,128)(2,1)S(1)}, bf16[128,384]{1,0:T(8,128)(2,1)S(1)}, u32[]{:S(2)}, u32[]{:S(2)}) collective-permute-start(bf16[128,384]{1,0:T(8,128)(2,1)S(1)} %get-tuple-element.32.pack_ref), channel_id=1, source_target_pairs={{0,24},{4,28},{8,0},{12,4},{16,8},{20,12},{24,16},{28,20},{1,25},{... | collective-permute-start | bytes 294920 | tf_op jit(solution)/shard_map/ppermute | solution.py:365
  9.1 8.6 %collective-permute-start.2 = (bf16[128,384]{1,0:T(8,128)(2,1)S(1)}, bf16[128,384]{1,0:T(8,128)(2,1)S(1)}, u32[]{:S(2)}, u32[]{:S(2)}) collective-permute-start(bf16[128,384]{1,0:T(8,128)(2,1)S(1)} %get-tuple-element.32.pack_ref), channel_id=1, source_target_pairs={{0,4},{4,0},{8,12},{12,8},{16,20},{20,16},{24,28},{28,24},{1,5},{5... | collective-permute-start | bytes 294920 | tf_op jit(solution)/shard_map/ppermute | solution.py:358
  11.3 6.4 %collective-permute-start.4 = (bf16[128,384]{1,0:T(8,128)(2,1)S(1)}, bf16[128,384]{1,0:T(8,128)(2,1)S(1)}, u32[]{:S(2)}, u32[]{:S(2)}) collective-permute-start(bf16[128,384]{1,0:T(8,128)(2,1)S(1)} %collective-permute-done.3.straight_ref), channel_id=1, source_target_pairs={{0,4},{4,0},{8,12},{12,8},{16,20},{20,16},{24,28},{28,24},{1,5},{5... | collective-permute-start | bytes 294920 | tf_op jit(solution)/shard_map/ppermute | solution.py:358
  16.2 3.0 %collective-permute-start.6 = (bf16[128,384]{1,0:T(8,128)(2,1)S(1)}, bf16[128,384]{1,0:T(8,128)(2,1)S(1)}, u32[]{:S(2)}, u32[]{:S(2)}) collective-permute-start(bf16[128,384]{1,0:T(8,128)(2,1)S(1)} %collective-permute-done.5.straight_ref), channel_id=1, source_target_pairs={{0,4},{4,0},{8,12},{12,8},{16,20},{20,16},{24,28},{28,24},{1,5},{5... | collective-permute-start | bytes 294920 | tf_op jit(solution)/shard_map/ppermute | solution.py:358
  16.2 4.2 %collective-permute-start.8 = (bf16[128,384]{1,0:T(8,128)(2,1)S(1)}, bf16[128,384]{1,0:T(8,128)(2,1)S(1)}, u32[]{:S(2)}, u32[]{:S(2)}) collective-permute-start(bf16[128,384]{1,0:T(8,128)(2,1)S(1)} %collective-permute-done.7.refs_7_), channel_id=1, source_target_pairs={{0,4},{4,0},{8,12},{12,8},{16,20},{20,16},{24,28},{28,24},{1,5},{5... | collective-permute-start | bytes 294920 | tf_op jit(solution)/shard_map/ppermute | solution.py:358

commit v6 on v5

--- a/solution.py
+++ b/solution.py
@@ -231,6 +231,15 @@
             new[part, :] = value
 
 
+def ready(pack_ref, mate_ref, ready_ref):
+    width = pack_ref.shape[0]
+    length = pack_ref.shape[1] - 2 * width
+    keys = pack_ref[:, :length]
+    through = dot(mate_ref[:, pl.ds(length, width)], keys).astype(NARROW)
+    ready_ref[:, :length] = jnp.where(lax.axis_index("seq") % 2 == 0, through, keys)
+    ready_ref[:, length:] = pack_ref[:, length + width :]
+
+
 def attend_near(
     moved_ref, peak_ref, sum_ref, mix_ref, small_ref, mate_ref, straight_ref, crossed_ref,
     peak_out, sum_out, mix_out, travel_out, out_ref, keys_ref, values_ref, done_ref, sem,
@@ -292,8 +301,16 @@
 
     @pl.when(chip_place > 2)
     def _():
-        gather(pairs_of(far), core, keys_ref, values_ref, travel_ref[...], length)
-        limits = (0, 2 * (chip_place - 2) * length) if len(far) > 2 else None
+        order = pairs_of(far[:-2])
+        travel = gather(order, core, keys_ref, values_ref, travel_ref[...], length)
+        straight, crossed = far[-2][...], far[-1][...]
+        pair = [jnp.where(core == 1, straight, crossed), jnp.where(core == 1, crossed, straight)]
+        keys = jnp.concatenate([block[:, :length] for block in pair], axis=1)
+        keys = dot(jnp.concatenate(halves(travel), axis=1), jnp.concatenate([keys, keys], axis=0))
+        keys_ref[:, pl.ds(len(order) * length, 2 * length)] = keys.astype(NARROW)
+        for slot, block in enumerate(pair, len(order)):
+            values_ref[pl.ds(slot * length, length), :] = counted(block[:, length:])
+        limits = (0, 2 * (chip_place - 2) * length) if order else None
         parts = pieces(moved_ref.shape[0], LAST_PIECES)
         states = lambda part: take_in(
             moved_ref[part, :], keys_ref[...], values_ref[...], limits,
@@ -362,7 +379,10 @@
     far = []
     for chip in range(1, chips):
         pairs = [(i, (i + 2 * chip) % segments) for i in range(segments)]
-        far.append(lax.ppermute(pack, "seq", pairs))
+        block = pack
+        if chip == chips - 1:
+            block = call(ready, shape((width, length + width), NARROW), 2)(pack, mate)
+        far.append(lax.ppermute(block, "seq", pairs))
     state_shape = (shape((heads * length, width), WIDE),) * 3
     moved, *state = call(
         own_segment, (shape((heads * length, width), NARROW),) + state_shape, 5

time: 22.6 us -> 24 us (1.062)
  waiting for transfers between devices: 8.14 us -> 9.15 us
    ppermute x3, waiting for transfers between devices: 7.09 us -> 8.08 us  [shards(): far.append(lax.ppermute(block, 'seq', pairs))]
  transfers between devices with their start and end apart: 9 -> 9, of which waited for: 4 -> 4; matrix products, arithmetic and copies ran while one was open for 3% -> 3% of each run, Pallas kernels for 24% -> 23%
where the time goes in v6:
time: 24 us; the launch traced here: 23.6 us
  waiting for transfers between devices  9.15 us (38%)
  Pallas kernels  7.79 us (32%)
  starting transfers between devices  5.08 us (21%)
  other arithmetic  0.76 us (3%)
  local copies, waits for them, and re-layouts  0.69 us (3%)
    ppermute x3, waiting for transfers between devices, shards(): far.append(lax.ppermute(block, 'seq', pairs))  8.08 us
    ppermute x3, starting transfers between devices, shards(): far.append(lax.ppermute(block, 'seq', pairs))  2.47 us
    ppermute x2, starting transfers between devices, partner(): return lax.ppermute(block, 'head', [(place, place ^ 1) for place in places])  2.03 us
    pallas_call x1, Pallas kernels, shards(): call(attend_last, shape((length, heads * width), NARROW), count, stores(2...  1.87 us
    pallas_call x1, Pallas kernels, shards(): call(invert, (shape((2, length, length), NARROW), square, square, shape((...  1.62 us
    pallas_call x1, Pallas kernels, shards(): call(attend_near, states, 8, stores(3) + ends, spots=spots, aliases=in_pl...  1.39 us
    pallas_call x1, Pallas kernels, shards(): call(attend_next, states, 9, stores(2) + ends, spots=spots, aliases={**in...  1.25 us
    ppermute x2, waiting for transfers between devices, partner(): return lax.ppermute(block, 'head', [(place, place ^ 1) for place in places])  1.06 us
  transfers between devices with their start and end apart: 9, of which 4 were waited for; matrix products, arithmetic and copies ran while one was open for 3% of the time, Pallas kernels for 23%

profile of v6, /device:TPU:24, one launch (start us, length us, event | category | flops | bytes accessed | tf_op | source)
XLA Modules:
  0.0 23.6 jit_solution(16501564503523635182)
XLA Ops:
  0.0 1.5 %collective-permute-start.1 = (bf16[64,128]{1,0:T(8,128)(2,1)}, bf16[64,128]{1,0:T(8,128)(2,1)S(1)}, u32[]{:S(2)}, u32[]{:S(2)}) collective-permute-start(bf16[64,128]{1,0:T(8,128)(2,1)} %bitcast.5), channel_id=1, source_target_pairs={{0,1},{1,0},{2,3},{3,2},{4,5},{5,4},{6,7},{7,6},{8,9},{9,8},{10,11... | collective-permute-start | bytes 49160 | tf_op jit(solution)/shard_map/ppermute | solution.py:349
  1.5 0.7 %pad_maximum_fusion.own_ref = bf16[128,128]{1,0:T(8,128)(2,1)S(1)} fusion(bf16[64,128]{1,0:T(8,128)(2,1)} %bitcast.7, bf16[64,128]{1,0:T(8,128)(2,1)} %bitcast.8), kind=kLoop, calls=%fused_computation | loop fusion | flops 65536 | bytes 65536 | tf_op jit(solution)/shard_map/concatenate | solution.py:352
  2.2 0.5 %collective-permute-start = (bf16[128,128]{1,0:T(8,128)(2,1)S(1)}, bf16[128,128]{1,0:T(8,128)(2,1)S(1)}, u32[]{:S(2)}, u32[]{:S(2)}) collective-permute-start(bf16[128,128]{1,0:T(8,128)(2,1)S(1)} %pad_maximum_fusion.own_ref), channel_id=1, source_target_pairs={{0,1},{1,0},{2,3},{3,2},{4,5},{5,4},{6,7},{7,6},{8,9},{9,8},{10,11... | collective-permute-start | bytes 98312 | tf_op jit(solution)/shard_map/ppermute | solution.py:349
  2.8 0.7 %copy-done.2 = f32[128,2]{0,1:T(2,128)S(1)} copy-done((f32[128,2]{0,1:T(2,128)S(1)}, f32[128,2]{0,1:T(2,128)}, u32[]{:S(2)}) %copy-start.2) | copy-done | bytes 1048
  3.5 0.5 %collective-permute-done.1.other_ref = bf16[64,128]{1,0:T(8,128)(2,1)S(1)} collective-permute-done((bf16[64,128]{1,0:T(8,128)(2,1)}, bf16[64,128]{1,0:T(8,128)(2,1)S(1)}, u32[]{:S(2)}, u32[]{:S(2)}) %collective-permute-start.1) | collective-permute-done | bytes 16416 | tf_op jit(solution)/shard_map/ppermute | solution.py:349
  4.0 1.6 %shard_map.64 = (bf16[2,128,128]{2,1,0:T(8,128)(2,1)S(1)}, bf16[128,128]{1,0:T(8,128)(2,1)S(1)}, bf16[128,128]{1,0:T(8,128)(2,1)S(1)}, f32[8,128]{1,0:T(8,128)S(1)}) custom-call(bf16[64,128]{1,0:T(8,128)(2,1)S(1)} %bitcast.6, bf16[64,128]{1,0:T(8,128)(2,1)S(1)} %collective-permute-done.1.other_ref, f32[3,128]{1,0:T(4,128)S(1)} %pad_maximum_fusion.1.small_ref.refs_6_), custom_call_target="tpu_custom_call" | custom-call | flops 100000000 | bytes 1048576 | tf_op jit(solution)/shard_map/pallas_call | solution.py:357
  5.6 0.6 %collective-permute-done.other_ref = bf16[128,128]{1,0:T(8,128)(2,1)S(1)} collective-permute-done((bf16[128,128]{1,0:T(8,128)(2,1)S(1)}, bf16[128,128]{1,0:T(8,128)(2,1)S(1)}, u32[]{:S(2)}, u32[]{:S(2)}) %collective-permute-start) | collective-permute-done | bytes 32800 | tf_op jit(solution)/shard_map/ppermute | solution.py:349
  6.2 0.5 %shard_map.65 = (bf16[128,384]{1,0:T(8,128)(2,1)S(1)}, bf16[2,128,256]{2,1,0:T(8,128)(2,1)S(1)}, bf16[128,256]{1,0:T(8,128)(2,1)S(1)}) custom-call(bf16[128,128]{1,0:T(8,128)(2,1)S(1)} %pad_maximum_fusion.own_ref, bf16[128,128]{1,0:T(8,128)(2,1)S(1)} %collective-permute-done.other_ref, bf16[2,128,128]{2,1,0:T(8,128)(2,1)S(1)} %get-tuple-element.26.inverse_ref, ...), custom_call_target="tpu_custom_call" | custom-call | flops 100000000 | bytes 1048576 | tf_op jit(solution)/shard_map/pallas_call | solution.py:363
  6.7 0.0 copy-start
  6.7 0.1 collective-permute-start.2
  6.8 0.3 %collective-permute-start.3 = (bf16[128,384]{1,0:T(8,128)(2,1)S(1)}, bf16[128,384]{1,0:T(8,128)(2,1)S(1)}, u32[]{:S(2)}, u32[]{:S(2)}) collective-permute-start(bf16[128,384]{1,0:T(8,128)(2,1)S(1)} %get-tuple-element.32.pack_ref), channel_id=1, source_target_pairs={{0,8},{4,12},{8,16},{12,20},{16,24},{20,28},{24,0},{28,4},{1,9},{5... | collective-permute-start | bytes 294920 | tf_op jit(solution)/shard_map/ppermute | solution.py:385
  7.0 1.7 %collective-permute-start.5 = (bf16[128,384]{1,0:T(8,128)(2,1)S(1)}, bf16[128,384]{1,0:T(8,128)(2,1)S(1)}, u32[]{:S(2)}, u32[]{:S(2)}) collective-permute-start(bf16[128,384]{1,0:T(8,128)(2,1)S(1)} %get-tuple-element.32.pack_ref), channel_id=1, source_target_pairs={{0,16},{4,20},{8,24},{12,28},{16,0},{20,4},{24,8},{28,12},{1,17},{... | collective-permute-start | bytes 294920 | tf_op jit(solution)/shard_map/ppermute | solution.py:385
  8.7 0.1 shard_map.69
  8.9 0.5 %collective-permute-start.7 = (bf16[128,256]{1,0:T(8,128)(2,1)S(1)}, bf16[128,256]{1,0:T(8,128)(2,1)S(1)}, u32[]{:S(2)}, u32[]{:S(2)}) collective-permute-start(bf16[128,256]{1,0:T(8,128)(2,1)S(1)} %shard_map.69), channel_id=1, source_target_pairs={{0,24},{4,28},{8,0},{12,4},{16,8},{20,12},{24,16},{28,20},{1,25},{... | collective-permute-start | bytes 196616 | tf_op jit(solution)/shard_map/ppermute | solution.py:385
  9.4 2.9 %collective-permute-done.3.straight_ref = bf16[128,384]{1,0:T(8,128)(2,1)S(1)} collective-permute-done((bf16[128,384]{1,0:T(8,128)(2,1)S(1)}, bf16[128,384]{1,0:T(8,128)(2,1)S(1)}, u32[]{:S(2)}, u32[]{:S(2)}) %collective-permute-start.3) | collective-permute-done | bytes 98336 | tf_op jit(solution)/shard_map/ppermute | solution.py:385
  12.3 0.0 collective-permute-start.4
  12.3 5.1 %collective-permute-done.5.straight_ref = bf16[128,384]{1,0:T(8,128)(2,1)S(1)} collective-permute-done((bf16[128,384]{1,0:T(8,128)(2,1)S(1)}, bf16[128,384]{1,0:T(8,128)(2,1)S(1)}, u32[]{:S(2)}, u32[]{:S(2)}) %collective-permute-start.5) | collective-permute-done | bytes 98336 | tf_op jit(solution)/shard_map/ppermute | solution.py:385
  17.5 0.0 collective-permute-start.6
  17.5 0.0 collective-permute-done.7.refs_7_
  17.5 0.5 %collective-permute-start.8 = (bf16[128,256]{1,0:T(8,128)(2,1)S(1)}, bf16[128,256]{1,0:T(8,128)(2,1)S(1)}, u32[]{:S(2)}, u32[]{:S(2)}) collective-permute-start(bf16[128,256]{1,0:T(8,128)(2,1)S(1)} %collective-permute-done.7.refs_7_), channel_id=1, source_target_pairs={{0,4},{4,0},{8,12},{12,8},{16,20},{20,16},{24,28},{28,24},{1,5},{5... | collective-permute-start | bytes 196616 | tf_op jit(solution)/shard_map/ppermute | solution.py:375
  18.0 1.0 %shard_map.66 = (bf16[1024,128]{1,0:T(8,128)(2,1)S(1)}, f32[1024,128]{1,0:T(8,128)S(1)}, f32[1024,128]{1,0:T(8,128)S(1)}, f32[1024,128]{1,0:T(8,128)S(1)}) custom-call(bf16[128,1024]{1,0:T(8,128)(2,1)S(1)} %copy-done, bf16[2,128,256]{2,1,0:T(8,128)(2,1)S(1)} %get-tuple-element.30.solved_ref, bf16[128,256]{1,0:T(8,128)(2,1)S(1)} %get-tuple-element.31.sides_ref, ...), custom_call_target="tpu_custom_call" | custom-call | flops 100000000 | bytes 1048576 | tf_op jit(solution)/shard_map/pallas_call | solution.py:387
  19.0 1.4 %shard_map.67 = (f32[1024,128]{1,0:T(8,128)S(1)}, f32[1024,128]{1,0:T(8,128)S(1)}, f32[1024,128]{1,0:T(8,128)S(1)}, f32[128,128]{1,0:T(8,128)S(1)}, bf16[128,1024]{1,0:T(8,128)(2,1)}) custom-call(bf16[1024,128]{1,0:T(8,128)(2,1)S(1)} %get-tuple-element.33.moved_ref.refs_0_, ...), custom_call_target="tpu_custom_call", output_to_operand_aliasing={{0}: (1, {}), {1}: (2, {}), {2}: (3, {})} | custom-call | flops 100000000 | bytes 1048576 | tf_op jit(solution)/shard_map/pallas_call | solution.py:402
  20.4 1.3 %shard_map.68 = (f32[1024,128]{1,0:T(8,128)S(1)}, f32[1024,128]{1,0:T(8,128)S(1)}, f32[1024,128]{1,0:T(8,128)S(1)}, f32[128,128]{1,0:T(8,128)S(1)}, bf16[128,1024]{1,0:T(8,128)(2,1)}) custom-call(bf16[1024,128]{1,0:T(8,128)(2,1)S(1)} %get-tuple-element.33.moved_ref.refs_0_, ...), custom_call_target="tpu_custom_call", output_to_operand_aliasing={{0}: (1, {}), {1}: (2, {}), {2}: (3, {}), {3}: (4, {}), {4}... | custom-call | flops 100000000 | bytes 1048576 | tf_op jit(solution)/shard_map/pallas_call | solution.py:407
  21.7 1.9 %shard_map.70 = bf16[128,1024]{1,0:T(8,128)(2,1)} custom-call(bf16[1024,128]{1,0:T(8,128)(2,1)S(1)} %get-tuple-element.33.moved_ref.refs_0_, f32[1024,128]{1,0:T(8,128)S(1)} %get-tuple-element.42.refs_1_, f32[1024,128]{1,0:T(8,128)S(1)} %get-tuple-element.43.refs_2_, f32[1024,128]{1,0:T(8,128)S(1)} %get-tuple-element.44.refs_3_, ...), custom_call_target="tpu_custom_call", output_to_operand_aliasing={{}: (5, {})} | custom-call | flops 1000000000 | bytes 1048576 | tf_op jit(solution)/shard_map/pallas_call | solution.py:420
  (11 shorter events, 0.0 us)
Async XLA Ops:
  0.0 3.9 %collective-permute-start.1 = (bf16[64,128]{1,0:T(8,128)(2,1)}, bf16[64,128]{1,0:T(8,128)(2,1)S(1)}, u32[]{:S(2)}, u32[]{:S(2)}) collective-permute-start(bf16[64,128]{1,0:T(8,128)(2,1)} %bitcast.5), channel_id=1, source_target_pairs={{0,1},{1,0},{2,3},{3,2},{4,5},{5,4},{6,7},{7,6},{8,9},{9,8},{10,11... | collective-permute-start | bytes 49160 | tf_op jit(solution)/shard_map/ppermute | solution.py:349
  1.5 2.5 %copy-start.1 = (bf16[128,64]{0,1:T(8,128)(2,1)S(1)}, bf16[128,64]{0,1:T(8,128)(2,1)}, u32[]{:S(2)}) copy-start(bf16[128,64]{0,1:T(8,128)(2,1)} %param.9) | copy-start | bytes 49156
  2.2 3.9 %collective-permute-start = (bf16[128,128]{1,0:T(8,128)(2,1)S(1)}, bf16[128,128]{1,0:T(8,128)(2,1)S(1)}, u32[]{:S(2)}, u32[]{:S(2)}) collective-permute-start(bf16[128,128]{1,0:T(8,128)(2,1)S(1)} %pad_maximum_fusion.own_ref), channel_id=1, source_target_pairs={{0,1},{1,0},{2,3},{3,2},{4,5},{5,4},{6,7},{7,6},{8,9},{9,8},{10,11... | collective-permute-start | bytes 98312 | tf_op jit(solution)/shard_map/ppermute | solution.py:349
  2.8 0.7 %copy-start.2 = (f32[128,2]{0,1:T(2,128)S(1)}, f32[128,2]{0,1:T(2,128)}, u32[]{:S(2)}) copy-start(f32[128,2]{0,1:T(2,128)} %param.10) | copy-start | bytes 3076
  2.8 0.7 %copy-start.3 = (f32[128]{0:T(128)S(1)}, f32[128]{0:T(128)}, u32[]{:S(2)}) copy-start(f32[128]{0:T(128)} %param.11) | copy-start | bytes 1540
  6.7 11.3 %copy-start = (bf16[128,1024]{1,0:T(8,128)(2,1)S(1)}, bf16[128,1024]{1,0:T(8,128)(2,1)}, u32[]{:S(2)}) copy-start(bf16[128,1024]{1,0:T(8,128)(2,1)} %queries_ref.1) | copy-start | bytes 786436
  6.7 2.0 %collective-permute-start.2 = (bf16[128,384]{1,0:T(8,128)(2,1)S(1)}, bf16[128,384]{1,0:T(8,128)(2,1)S(1)}, u32[]{:S(2)}, u32[]{:S(2)}) collective-permute-start(bf16[128,384]{1,0:T(8,128)(2,1)S(1)} %get-tuple-element.32.pack_ref), channel_id=1, source_target_pairs={{0,4},{4,0},{8,12},{12,8},{16,20},{20,16},{24,28},{28,24},{1,5},{5... | collective-permute-start | bytes 294920 | tf_op jit(solution)/shard_map/ppermute | solution.py:375
  6.8 5.6 %collective-permute-start.3 = (bf16[128,384]{1,0:T(8,128)(2,1)S(1)}, bf16[128,384]{1,0:T(8,128)(2,1)S(1)}, u32[]{:S(2)}, u32[]{:S(2)}) collective-permute-start(bf16[128,384]{1,0:T(8,128)(2,1)S(1)} %get-tuple-element.32.pack_ref), channel_id=1, source_target_pairs={{0,8},{4,12},{8,16},{12,20},{16,24},{20,28},{24,0},{28,4},{1,9},{5... | collective-permute-start | bytes 294920 | tf_op jit(solution)/shard_map/ppermute | solution.py:385
  7.0 10.4 %collective-permute-start.5 = (bf16[128,384]{1,0:T(8,128)(2,1)S(1)}, bf16[128,384]{1,0:T(8,128)(2,1)S(1)}, u32[]{:S(2)}, u32[]{:S(2)}) collective-permute-start(bf16[128,384]{1,0:T(8,128)(2,1)S(1)} %get-tuple-element.32.pack_ref), channel_id=1, source_target_pairs={{0,16},{4,20},{8,24},{12,28},{16,0},{20,4},{24,8},{28,12},{1,17},{... | collective-permute-start | bytes 294920 | tf_op jit(solution)/shard_map/ppermute | solution.py:385
  8.9 8.6 %collective-permute-start.7 = (bf16[128,256]{1,0:T(8,128)(2,1)S(1)}, bf16[128,256]{1,0:T(8,128)(2,1)S(1)}, u32[]{:S(2)}, u32[]{:S(2)}) collective-permute-start(bf16[128,256]{1,0:T(8,128)(2,1)S(1)} %shard_map.69), channel_id=1, source_target_pairs={{0,24},{4,28},{8,0},{12,4},{16,8},{20,12},{24,16},{28,20},{1,25},{... | collective-permute-start | bytes 196616 | tf_op jit(solution)/shard_map/ppermute | solution.py:385
  12.3 6.7 %collective-permute-start.4 = (bf16[128,384]{1,0:T(8,128)(2,1)S(1)}, bf16[128,384]{1,0:T(8,128)(2,1)S(1)}, u32[]{:S(2)}, u32[]{:S(2)}) collective-permute-start(bf16[128,384]{1,0:T(8,128)(2,1)S(1)} %collective-permute-done.3.straight_ref), channel_id=1, source_target_pairs={{0,4},{4,0},{8,12},{12,8},{16,20},{20,16},{24,28},{28,24},{1,5},{5... | collective-permute-start | bytes 294920 | tf_op jit(solution)/shard_map/ppermute | solution.py:375
  17.5 2.9 %collective-permute-start.6 = (bf16[128,384]{1,0:T(8,128)(2,1)S(1)}, bf16[128,384]{1,0:T(8,128)(2,1)S(1)}, u32[]{:S(2)}, u32[]{:S(2)}) collective-permute-start(bf16[128,384]{1,0:T(8,128)(2,1)S(1)} %collective-permute-done.5.straight_ref), channel_id=1, source_target_pairs={{0,4},{4,0},{8,12},{12,8},{16,20},{20,16},{24,28},{28,24},{1,5},{5... | collective-permute-start | bytes 294920 | tf_op jit(solution)/shard_map/ppermute | solution.py:375
  17.5 4.2 %collective-permute-start.8 = (bf16[128,256]{1,0:T(8,128)(2,1)S(1)}, bf16[128,256]{1,0:T(8,128)(2,1)S(1)}, u32[]{:S(2)}, u32[]{:S(2)}) collective-permute-start(bf16[128,256]{1,0:T(8,128)(2,1)S(1)} %collective-permute-done.7.refs_7_), channel_id=1, source_target_pairs={{0,4},{4,0},{8,12},{12,8},{16,20},{20,16},{24,28},{28,24},{1,5},{5... | collective-permute-start | bytes 196616 | tf_op jit(solution)/shard_map/ppermute | solution.py:375

commit v7 on v6

--- a/solution.py
+++ b/solution.py
@@ -11,7 +11,7 @@
 WIDE = jnp.float32
 NARROW = jnp.bfloat16
 MASKED = -1e30
-LAST_PIECES, LAST_GROUPS = 4, 2
+LAST_PIECES, LAST_GROUPS = 8, 2
 SETTLE_PIECES, SETTLE_GROUPS = 4, 2
 OWN_PIECES, NEAR_PIECES = 1, 2
 
@@ -41,7 +41,10 @@
     return full_ref[...]
 
 
-def invert(own_ref, other_ref, small_ref, inverse_ref, across_ref, dirs_ref, coef_ref, full_ref):
+def invert(
+    own_ref, other_ref, small_ref,
+    inverse_ref, across_ref, dirs_ref, coef_ref, spread_ref, transform_ref, full_ref,
+):
     length = own_ref.shape[1]
     place = lax.axis_index("head")
     parity = place % 2
@@ -80,11 +83,21 @@
                 rows.append(inverse[start : start + step] - change[at * step : (at + 1) * step])
             inverse = jnp.concatenate(rows, axis=0)
         block *= 2
-    inverse_ref[0], inverse_ref[1] = halves(inverse)
+    top, low = halves(inverse)
+    inverse_ref[0], inverse_ref[1] = top, low
+    spread = halves(
+        dot(jnp.concatenate([top, low], axis=1), jnp.concatenate([dirs, dirs], axis=0))
+    )
+    spread_ref[0], spread_ref[1] = spread
+    width = dirs_t.shape[0]
+    row_w = lax.broadcasted_iota(jnp.int32, (width, width), 0)
+    col_w = lax.broadcasted_iota(jnp.int32, (width, width), 1)
+    unit = jnp.where(row_w == col_w, 1.0, 0.0)
+    transform_ref[...] = (unit - dot3(halves(dirs_wide * coef), spread)).astype(NARROW)
 
 
 def prepare(
-    own_ref, other_ref, inverse_ref, across_ref, dirs_ref, coef_ref,
+    own_ref, other_ref, inverse_ref, across_ref, dirs_ref, coef_ref, spread_ref, transform_ref,
     pack_ref, solved_ref, sides_ref, full_ref,
 ):
     half, length = own_ref.shape[0] // 2, own_ref.shape[1]
@@ -96,20 +109,14 @@
     row = lax.broadcasted_iota(jnp.int32, (length, length), 0)
     col = lax.broadcasted_iota(jnp.int32, (length, length), 1)
     top, low = inverse_ref[0], inverse_ref[1]
-    reach_top, reach_low = halves(jnp.where(row > col, dot(dirs, keys_t), 0.0))
-    right = jnp.concatenate([reach_top, dirs], axis=1)
-    solved = dot(jnp.concatenate([top, low], axis=1), jnp.concatenate([right, right], axis=0))
-    solved_reach = solved[:, :length] + dot(top, reach_low)
-    solved_parts = halves(jnp.concatenate([solved_reach, solved[:, length:]], axis=1))
-    change = dot3(halves(dirs_t.astype(WIDE) * coef_ref[:1, :]), solved_parts)
-    pack_ref[:, :length] = (keys_t.astype(WIDE) - change[:, :length]).astype(NARROW)
-    row_w = lax.broadcasted_iota(jnp.int32, (width, width), 0)
-    col_w = lax.broadcasted_iota(jnp.int32, (width, width), 1)
-    unit = jnp.where(row_w == col_w, 1.0, 0.0)
-    pack_ref[:, length : length + width] = (unit - change[:, length:]).astype(NARROW)
+    reach = halves(jnp.where(row > col, dot(dirs, keys_t), 0.0))
+    solved = halves(dot3((top, low), reach))
+    change = dot3(halves(dirs_t.astype(WIDE) * coef_ref[:1, :]), solved)
+    pack_ref[:, :length] = (keys_t.astype(WIDE) - change).astype(NARROW)
+    pack_ref[:, length : length + width] = transform_ref[...]
     pack_ref[:, length + width :] = values_t.astype(WIDE).T.astype(NARROW)
-    solved_ref[0] = solved_parts[0]
-    solved_ref[1] = solved_parts[1]
+    for at in range(2):
+        solved_ref[at] = jnp.concatenate([solved[at], spread_ref[at]], axis=1)
     sides_ref[...] = jnp.concatenate([dirs_t, keys_t], axis=1)
 
 
@@ -262,7 +269,7 @@
         gather([mate_ref], core, keys_ref, values_ref, None, length)
         update(moved_ref, olds, news, keys_ref[:, span], values_ref[span, :], None)
 
-    @pl.when(chip_place == 0)
+    @pl.when((chip_place == 0) & (core == 0))
     def _():
         parts = pieces(moved_ref.shape[0], SETTLE_PIECES)
         states = lambda part: (sum_out[part, :], mix_out[part, :])
@@ -284,7 +291,7 @@
         travel_out[...] = gather(order, place % 2, keys_ref, values_ref, travel_ref[...], length)
         update(moved_ref, olds, news, keys_ref[...], values_ref[...], None)
 
-    @pl.when((chip_place == 1) | (chip_place == 2))
+    @pl.when((place > 0) & (chip_place <= 2))
     def _():
         parts = pieces(moved_ref.shape[0], SETTLE_PIECES)
         states = lambda part: (sum_out[part, :], mix_out[part, :])
@@ -354,9 +361,16 @@
     shape = jax.ShapeDtypeStruct
     small = jnp.concatenate([beta.T, gain.reshape(1, -1)], axis=0)
     square = shape((width, length), NARROW)
-    inverse, dirs_t, dirs, coef = call(
+    inverse, dirs_t, dirs, coef, spread, transform = call(
         invert,
-        (shape((2, length, length), NARROW), square, square, shape((8, length), WIDE)),
+        (
+            shape((2, length, length), NARROW),
+            square,
+            square,
+            shape((8, length), WIDE),
+            shape((2, length, width), NARROW),
+            shape((width, width), NARROW),
+        ),
         3,
         [pltpu.VMEM((width, length), NARROW)],
     )(directions.T, other_dirs, small)
@@ -367,12 +381,12 @@
             shape((2, length, length + width), NARROW),
             shape((width, 2 * length), NARROW),
         ),
-        6,
+        8,
         [pltpu.VMEM((2, width, length), NARROW)],
-    )(own, other, inverse, dirs_t, dirs, coef)
-
-    def across(block, first=0):
-        return lax.ppermute(block, "seq", [(i, i ^ 1) for i in range(2 * first, segments)])
+    )(own, other, inverse, dirs_t, dirs, coef, spread, transform)
+
+    def across(block):
+        return lax.ppermute(block, "seq", [(i, i ^ 1) for i in range(segments)])
 
     mate = across(pack)
     chips = segments // 2

time: 24 us -> 23.8 us (level)
  waiting for transfers between devices: 9.15 us -> 8.88 us
    pallas_call x1, Pallas kernels: 1.62 us -> 1.89 us  [shards(): call(invert, (shape((2, length, length), NARROW), square, square, shape((...]
    ppermute x2, waiting for transfers between devices: 1.06 us -> 0.78 us  [partner(): return lax.ppermute(block, 'head', [(place, place ^ 1) for place in places])]
  transfers between devices with their start and end apart: 9 -> 9, of which waited for: 4 -> 4; matrix products, arithmetic and copies ran while one was open for 3% -> 3% of each run, Pallas kernels for 23% -> 24%
where the time goes in v7:
time: 23.8 us; the launch traced here: 23.4 us
  waiting for transfers between devices  8.88 us (37%)
  Pallas kernels  7.87 us (33%)
  starting transfers between devices  5.07 us (21%)
  other arithmetic  0.76 us (3%)
  local copies, waits for them, and re-layouts  0.69 us (3%)
    ppermute x3, waiting for transfers between devices, shards(): far.append(lax.ppermute(block, 'seq', pairs))  8.09 us
    ppermute x3, starting transfers between devices, shards(): far.append(lax.ppermute(block, 'seq', pairs))  2.46 us
    ppermute x2, starting transfers between devices, partner(): return lax.ppermute(block, 'head', [(place, place ^ 1) for place in places])  2.03 us
    pallas_call x1, Pallas kernels, shards(): call(invert, (shape((2, length, length), NARROW), square, square, shape((...  1.89 us
    pallas_call x1, Pallas kernels, shards(): call(attend_last, shape((length, heads * width), NARROW), count, stores(2...  1.71 us
    pallas_call x1, Pallas kernels, shards(): call(attend_near, states, 8, stores(3) + ends, spots=spots, aliases=in_pl...  1.39 us
    pallas_call x1, Pallas kernels, shards(): call(attend_next, states, 9, stores(2) + ends, spots=spots, aliases={**in...  1.25 us
    pallas_call x1, Pallas kernels, shards(): call(own_segment, (shape((heads * length, width), NARROW),) + state_shape...  1.01 us
  transfers between devices with their start and end apart: 9, of which 4 were waited for; matrix products, arithmetic and copies ran while one was open for 3% of the time, Pallas kernels for 24%

profile of v7, /device:TPU:24, one launch (start us, length us, event | category | flops | bytes accessed | tf_op | source)
XLA Modules:
  0.0 23.4 jit_solution(1974700422410264553)
XLA Ops:
  0.0 1.5 %collective-permute-start.1 = (bf16[64,128]{1,0:T(8,128)(2,1)}, bf16[64,128]{1,0:T(8,128)(2,1)S(1)}, u32[]{:S(2)}, u32[]{:S(2)}) collective-permute-start(bf16[64,128]{1,0:T(8,128)(2,1)} %bitcast.5), channel_id=1, source_target_pairs={{0,1},{1,0},{2,3},{3,2},{4,5},{5,4},{6,7},{7,6},{8,9},{9,8},{10,11... | collective-permute-start | bytes 49160 | tf_op jit(solution)/shard_map/ppermute | solution.py:356
  1.5 0.7 %pad_maximum_fusion.own_ref = bf16[128,128]{1,0:T(8,128)(2,1)S(1)} fusion(bf16[64,128]{1,0:T(8,128)(2,1)} %bitcast.7, bf16[64,128]{1,0:T(8,128)(2,1)} %bitcast.8), kind=kLoop, calls=%fused_computation | loop fusion | flops 65536 | bytes 65536 | tf_op jit(solution)/shard_map/concatenate | solution.py:359
  2.2 0.5 %collective-permute-start = (bf16[128,128]{1,0:T(8,128)(2,1)S(1)}, bf16[128,128]{1,0:T(8,128)(2,1)S(1)}, u32[]{:S(2)}, u32[]{:S(2)}) collective-permute-start(bf16[128,128]{1,0:T(8,128)(2,1)S(1)} %pad_maximum_fusion.own_ref), channel_id=1, source_target_pairs={{0,1},{1,0},{2,3},{3,2},{4,5},{5,4},{6,7},{7,6},{8,9},{9,8},{10,11... | collective-permute-start | bytes 98312 | tf_op jit(solution)/shard_map/ppermute | solution.py:356
  2.8 0.7 %copy-done.2 = f32[128,2]{0,1:T(2,128)S(1)} copy-done((f32[128,2]{0,1:T(2,128)S(1)}, f32[128,2]{0,1:T(2,128)}, u32[]{:S(2)}) %copy-start.2) | copy-done | bytes 1048
  3.5 0.5 %collective-permute-done.1.other_ref = bf16[64,128]{1,0:T(8,128)(2,1)S(1)} collective-permute-done((bf16[64,128]{1,0:T(8,128)(2,1)}, bf16[64,128]{1,0:T(8,128)(2,1)S(1)}, u32[]{:S(2)}, u32[]{:S(2)}) %collective-permute-start.1) | collective-permute-done | bytes 16416 | tf_op jit(solution)/shard_map/ppermute | solution.py:356
  4.0 1.9 %shard_map.64 = (bf16[2,128,128]{2,1,0:T(8,128)(2,1)S(1)}, bf16[128,128]{1,0:T(8,128)(2,1)S(1)}, bf16[128,128]{1,0:T(8,128)(2,1)S(1)}, f32[8,128]{1,0:T(8,128)S(...) custom-call(bf16[64,128]{1,0:T(8,128)(2,1)S(1)} %bitcast.6, ...), custom_call_target="tpu_custom_call" | custom-call | flops 100000000 | bytes 1048576 | tf_op jit(solution)/shard_map/pallas_call | solution.py:364
  5.9 0.3 %collective-permute-done.other_ref = bf16[128,128]{1,0:T(8,128)(2,1)S(1)} collective-permute-done((bf16[128,128]{1,0:T(8,128)(2,1)S(1)}, bf16[128,128]{1,0:T(8,128)(2,1)S(1)}, u32[]{:S(2)}, u32[]{:S(2)}) %collective-permute-start) | collective-permute-done | bytes 32800 | tf_op jit(solution)/shard_map/ppermute | solution.py:356
  6.2 0.5 %shard_map.65 = (bf16[128,384]{1,0:T(8,128)(2,1)S(1)}, bf16[2,128,256]{2,1,0:T(8,128)(2,1)S(1)}, bf16[128,256]{1,0:T(8,128)(2,1)S(1)}) custom-call(bf16[128,128]{1,0:T(8,128)(2,1)S(1)} %pad_maximum_fusion.own_ref, bf16[128,128]{1,0:T(8,128)(2,1)S(1)} %collective-permute-done.other_ref, bf16[2,128,128]{2,1,0:T(8,128)(2,1)S(1)} %get-tuple-element.28.inverse_ref, ...), custom_call_target="tpu_custom_call" | custom-call | flops 100000000 | bytes 1048576 | tf_op jit(solution)/shard_map/pallas_call | solution.py:377
  6.6 0.0 copy-start
  6.7 0.1 collective-permute-start.2
  6.7 0.3 %collective-permute-start.3 = (bf16[128,384]{1,0:T(8,128)(2,1)S(1)}, bf16[128,384]{1,0:T(8,128)(2,1)S(1)}, u32[]{:S(2)}, u32[]{:S(2)}) collective-permute-start(bf16[128,384]{1,0:T(8,128)(2,1)S(1)} %get-tuple-element.36.pack_ref), channel_id=1, source_target_pairs={{0,8},{4,12},{8,16},{12,20},{16,24},{20,28},{24,0},{28,4},{1,9},{5... | collective-permute-start | bytes 294920 | tf_op jit(solution)/shard_map/ppermute | solution.py:399
  7.0 1.7 %collective-permute-start.5 = (bf16[128,384]{1,0:T(8,128)(2,1)S(1)}, bf16[128,384]{1,0:T(8,128)(2,1)S(1)}, u32[]{:S(2)}, u32[]{:S(2)}) collective-permute-start(bf16[128,384]{1,0:T(8,128)(2,1)S(1)} %get-tuple-element.36.pack_ref), channel_id=1, source_target_pairs={{0,16},{4,20},{8,24},{12,28},{16,0},{20,4},{24,8},{28,12},{1,17},{... | collective-permute-start | bytes 294920 | tf_op jit(solution)/shard_map/ppermute | solution.py:399
  8.7 0.0 collective-permute-done.2.mate_ref
  8.7 0.1 shard_map.69
  8.8 0.5 %collective-permute-start.7 = (bf16[128,256]{1,0:T(8,128)(2,1)S(1)}, bf16[128,256]{1,0:T(8,128)(2,1)S(1)}, u32[]{:S(2)}, u32[]{:S(2)}) collective-permute-start(bf16[128,256]{1,0:T(8,128)(2,1)S(1)} %shard_map.69), channel_id=1, source_target_pairs={{0,24},{4,28},{8,0},{12,4},{16,8},{20,12},{24,16},{28,20},{1,25},{... | collective-permute-start | bytes 196616 | tf_op jit(solution)/shard_map/ppermute | solution.py:399
  9.3 2.9 %collective-permute-done.3.straight_ref = bf16[128,384]{1,0:T(8,128)(2,1)S(1)} collective-permute-done((bf16[128,384]{1,0:T(8,128)(2,1)S(1)}, bf16[128,384]{1,0:T(8,128)(2,1)S(1)}, u32[]{:S(2)}, u32[]{:S(2)}) %collective-permute-start.3) | collective-permute-done | bytes 98336 | tf_op jit(solution)/shard_map/ppermute | solution.py:399
  12.3 0.0 collective-permute-start.4
  12.3 5.1 %collective-permute-done.5.straight_ref = bf16[128,384]{1,0:T(8,128)(2,1)S(1)} collective-permute-done((bf16[128,384]{1,0:T(8,128)(2,1)S(1)}, bf16[128,384]{1,0:T(8,128)(2,1)S(1)}, u32[]{:S(2)}, u32[]{:S(2)}) %collective-permute-start.5) | collective-permute-done | bytes 98336 | tf_op jit(solution)/shard_map/ppermute | solution.py:399
  17.4 0.5 %collective-permute-start.8 = (bf16[128,256]{1,0:T(8,128)(2,1)S(1)}, bf16[128,256]{1,0:T(8,128)(2,1)S(1)}, u32[]{:S(2)}, u32[]{:S(2)}) collective-permute-start(bf16[128,256]{1,0:T(8,128)(2,1)S(1)} %collective-permute-done.7.refs_7_), channel_id=1, source_target_pairs={{0,4},{4,0},{8,12},{12,8},{16,20},{20,16},{24,28},{28,24},{1,5},{5... | collective-permute-start | bytes 196616 | tf_op jit(solution)/shard_map/ppermute | solution.py:389
  17.9 1.0 %shard_map.66 = (bf16[1024,128]{1,0:T(8,128)(2,1)S(1)}, f32[1024,128]{1,0:T(8,128)S(1)}, f32[1024,128]{1,0:T(8,128)S(1)}, f32[1024,128]{1,0:T(8,128)S(1)}) custom-call(bf16[128,1024]{1,0:T(8,128)(2,1)S(1)} %copy-done, bf16[2,128,256]{2,1,0:T(8,128)(2,1)S(1)} %get-tuple-element.34.solved_ref, bf16[128,256]{1,0:T(8,128)(2,1)S(1)} %get-tuple-element.35.sides_ref, ...), custom_call_target="tpu_custom_call" | custom-call | flops 100000000 | bytes 1048576 | tf_op jit(solution)/shard_map/pallas_call | solution.py:401
  19.0 0.0 collective-permute-done.4.crossed_ref
  19.0 1.4 %shard_map.67 = (f32[1024,128]{1,0:T(8,128)S(1)}, f32[1024,128]{1,0:T(8,128)S(1)}, f32[1024,128]{1,0:T(8,128)S(1)}, f32[128,128]{1,0:T(8,128)S(1)}, bf16[128,1024]{1,0:T(8,128)(2,1)}) custom-call(bf16[1024,128]{1,0:T(8,128)(2,1)S(1)} %get-tuple-element.37.moved_ref.refs_0_, ...), custom_call_target="tpu_custom_call", output_to_operand_aliasing={{0}: (1, {}), {1}: (2, {}), {2}: (3, {})} | custom-call | flops 100000000 | bytes 1048576 | tf_op jit(solution)/shard_map/pallas_call | solution.py:416
  20.4 1.3 %shard_map.68 = (f32[1024,128]{1,0:T(8,128)S(1)}, f32[1024,128]{1,0:T(8,128)S(1)}, f32[1024,128]{1,0:T(8,128)S(1)}, f32[128,128]{1,0:T(8,128)S(1)}, bf16[128,1024]{1,0:T(8,128)(2,1)}) custom-call(bf16[1024,128]{1,0:T(8,128)(2,1)S(1)} %get-tuple-element.37.moved_ref.refs_0_, ...), custom_call_target="tpu_custom_call", output_to_operand_aliasing={{0}: (1, {}), {1}: (2, {}), {2}: (3, {}), {3}: (4, {}), {4}... | custom-call | flops 100000000 | bytes 1048576 | tf_op jit(solution)/shard_map/pallas_call | solution.py:421
  21.7 1.7 %shard_map.70 = bf16[128,1024]{1,0:T(8,128)(2,1)} custom-call(bf16[1024,128]{1,0:T(8,128)(2,1)S(1)} %get-tuple-element.37.moved_ref.refs_0_, f32[1024,128]{1,0:T(8,128)S(1)} %get-tuple-element.46.refs_1_, f32[1024,128]{1,0:T(8,128)S(1)} %get-tuple-element.47.refs_2_, f32[1024,128]{1,0:T(8,128)S(1)} %get-tuple-element.48.refs_3_, ...), custom_call_target="tpu_custom_call", output_to_operand_aliasing={{}: (5, {})} | custom-call | flops 1000000000 | bytes 1048576 | tf_op jit(solution)/shard_map/pallas_call | solution.py:434
  (11 shorter events, 0.0 us)
Async XLA Ops:
  0.0 3.9 %collective-permute-start.1 = (bf16[64,128]{1,0:T(8,128)(2,1)}, bf16[64,128]{1,0:T(8,128)(2,1)S(1)}, u32[]{:S(2)}, u32[]{:S(2)}) collective-permute-start(bf16[64,128]{1,0:T(8,128)(2,1)} %bitcast.5), channel_id=1, source_target_pairs={{0,1},{1,0},{2,3},{3,2},{4,5},{5,4},{6,7},{7,6},{8,9},{9,8},{10,11... | collective-permute-start | bytes 49160 | tf_op jit(solution)/shard_map/ppermute | solution.py:356
  1.5 2.5 %copy-start.1 = (bf16[128,64]{0,1:T(8,128)(2,1)S(1)}, bf16[128,64]{0,1:T(8,128)(2,1)}, u32[]{:S(2)}) copy-start(bf16[128,64]{0,1:T(8,128)(2,1)} %param.9) | copy-start | bytes 49156
  2.2 3.9 %collective-permute-start = (bf16[128,128]{1,0:T(8,128)(2,1)S(1)}, bf16[128,128]{1,0:T(8,128)(2,1)S(1)}, u32[]{:S(2)}, u32[]{:S(2)}) collective-permute-start(bf16[128,128]{1,0:T(8,128)(2,1)S(1)} %pad_maximum_fusion.own_ref), channel_id=1, source_target_pairs={{0,1},{1,0},{2,3},{3,2},{4,5},{5,4},{6,7},{7,6},{8,9},{9,8},{10,11... | collective-permute-start | bytes 98312 | tf_op jit(solution)/shard_map/ppermute | solution.py:356
  2.8 0.7 %copy-start.2 = (f32[128,2]{0,1:T(2,128)S(1)}, f32[128,2]{0,1:T(2,128)}, u32[]{:S(2)}) copy-start(f32[128,2]{0,1:T(2,128)} %param.10) | copy-start | bytes 3076
  2.8 0.7 %copy-start.3 = (f32[128]{0:T(128)S(1)}, f32[128]{0:T(128)}, u32[]{:S(2)}) copy-start(f32[128]{0:T(128)} %param.11) | copy-start | bytes 1540
  6.6 11.3 %copy-start = (bf16[128,1024]{1,0:T(8,128)(2,1)S(1)}, bf16[128,1024]{1,0:T(8,128)(2,1)}, u32[]{:S(2)}) copy-start(bf16[128,1024]{1,0:T(8,128)(2,1)} %queries_ref.1) | copy-start | bytes 786436
  6.7 2.0 %collective-permute-start.2 = (bf16[128,384]{1,0:T(8,128)(2,1)S(1)}, bf16[128,384]{1,0:T(8,128)(2,1)S(1)}, u32[]{:S(2)}, u32[]{:S(2)}) collective-permute-start(bf16[128,384]{1,0:T(8,128)(2,1)S(1)} %get-tuple-element.36.pack_ref), channel_id=1, source_target_pairs={{0,4},{4,0},{8,12},{12,8},{16,20},{20,16},{24,28},{28,24},{1,5},{5... | collective-permute-start | bytes 294920 | tf_op jit(solution)/shard_map/ppermute | solution.py:389
  6.7 5.6 %collective-permute-start.3 = (bf16[128,384]{1,0:T(8,128)(2,1)S(1)}, bf16[128,384]{1,0:T(8,128)(2,1)S(1)}, u32[]{:S(2)}, u32[]{:S(2)}) collective-permute-start(bf16[128,384]{1,0:T(8,128)(2,1)S(1)} %get-tuple-element.36.pack_ref), channel_id=1, source_target_pairs={{0,8},{4,12},{8,16},{12,20},{16,24},{20,28},{24,0},{28,4},{1,9},{5... | collective-permute-start | bytes 294920 | tf_op jit(solution)/shard_map/ppermute | solution.py:399
  7.0 10.4 %collective-permute-start.5 = (bf16[128,384]{1,0:T(8,128)(2,1)S(1)}, bf16[128,384]{1,0:T(8,128)(2,1)S(1)}, u32[]{:S(2)}, u32[]{:S(2)}) collective-permute-start(bf16[128,384]{1,0:T(8,128)(2,1)S(1)} %get-tuple-element.36.pack_ref), channel_id=1, source_target_pairs={{0,16},{4,20},{8,24},{12,28},{16,0},{20,4},{24,8},{28,12},{1,17},{... | collective-permute-start | bytes 294920 | tf_op jit(solution)/shard_map/ppermute | solution.py:399
  8.8 8.6 %collective-permute-start.7 = (bf16[128,256]{1,0:T(8,128)(2,1)S(1)}, bf16[128,256]{1,0:T(8,128)(2,1)S(1)}, u32[]{:S(2)}, u32[]{:S(2)}) collective-permute-start(bf16[128,256]{1,0:T(8,128)(2,1)S(1)} %shard_map.69), channel_id=1, source_target_pairs={{0,24},{4,28},{8,0},{12,4},{16,8},{20,12},{24,16},{28,20},{1,25},{... | collective-permute-start | bytes 196616 | tf_op jit(solution)/shard_map/ppermute | solution.py:399
  12.3 6.7 %collective-permute-start.4 = (bf16[128,384]{1,0:T(8,128)(2,1)S(1)}, bf16[128,384]{1,0:T(8,128)(2,1)S(1)}, u32[]{:S(2)}, u32[]{:S(2)}) collective-permute-start(bf16[128,384]{1,0:T(8,128)(2,1)S(1)} %collective-permute-done.3.straight_ref), channel_id=1, source_target_pairs={{0,4},{4,0},{8,12},{12,8},{16,20},{20,16},{24,28},{28,24},{1,5},{5... | collective-permute-start | bytes 294920 | tf_op jit(solution)/shard_map/ppermute | solution.py:389
  17.4 2.9 %collective-permute-start.6 = (bf16[128,384]{1,0:T(8,128)(2,1)S(1)}, bf16[128,384]{1,0:T(8,128)(2,1)S(1)}, u32[]{:S(2)}, u32[]{:S(2)}) collective-permute-start(bf16[128,384]{1,0:T(8,128)(2,1)S(1)} %collective-permute-done.5.straight_ref), channel_id=1, source_target_pairs={{0,4},{4,0},{8,12},{12,8},{16,20},{20,16},{24,28},{28,24},{1,5},{5... | collective-permute-start | bytes 294920 | tf_op jit(solution)/shard_map/ppermute | solution.py:389
  17.4 4.2 %collective-permute-start.8 = (bf16[128,256]{1,0:T(8,128)(2,1)S(1)}, bf16[128,256]{1,0:T(8,128)(2,1)S(1)}, u32[]{:S(2)}, u32[]{:S(2)}) collective-permute-start(bf16[128,256]{1,0:T(8,128)(2,1)S(1)} %collective-permute-done.7.refs_7_), channel_id=1, source_target_pairs={{0,4},{4,0},{8,12},{12,8},{16,20},{20,16},{24,28},{28,24},{1,5},{5... | collective-permute-start | bytes 196616 | tf_op jit(solution)/shard_map/ppermute | solution.py:389

commit v8 on v6

--- a/solution.py
+++ b/solution.py
@@ -11,8 +11,8 @@
 WIDE = jnp.float32
 NARROW = jnp.bfloat16
 MASKED = -1e30
-LAST_PIECES, LAST_GROUPS = 4, 2
-SETTLE_PIECES, SETTLE_GROUPS = 4, 2
+LAST_PIECES, LAST_GROUPS = 8, 4
+SETTLE_PIECES, SETTLE_GROUPS = 8, 4
 OWN_PIECES, NEAR_PIECES = 1, 2
 
 
@@ -262,7 +262,7 @@
         gather([mate_ref], core, keys_ref, values_ref, None, length)
         update(moved_ref, olds, news, keys_ref[:, span], values_ref[span, :], None)
 
-    @pl.when(chip_place == 0)
+    @pl.when((chip_place == 0) & (core == 0))
     def _():
         parts = pieces(moved_ref.shape[0], SETTLE_PIECES)
         states = lambda part: (sum_out[part, :], mix_out[part, :])
@@ -284,7 +284,7 @@
         travel_out[...] = gather(order, place % 2, keys_ref, values_ref, travel_ref[...], length)
         update(moved_ref, olds, news, keys_ref[...], values_ref[...], None)
 
-    @pl.when((chip_place == 1) | (chip_place == 2))
+    @pl.when((place > 0) & (chip_place <= 2))
     def _():
         parts = pieces(moved_ref.shape[0], SETTLE_PIECES)
         states = lambda part: (sum_out[part, :], mix_out[part, :])
@@ -371,8 +371,8 @@
         [pltpu.VMEM((2, width, length), NARROW)],
     )(own, other, inverse, dirs_t, dirs, coef)
 
-    def across(block, first=0):
-        return lax.ppermute(block, "seq", [(i, i ^ 1) for i in range(2 * first, segments)])
+    def across(block):
+        return lax.ppermute(block, "seq", [(i, i ^ 1) for i in range(segments)])
 
     mate = across(pack)
     chips = segments // 2

time: 24 us -> 23.8 us (level)
  no operation moved by 1% of the time
where the time goes in v8:
time: 23.8 us; the launch traced here: 23.4 us
  waiting for transfers between devices  9.15 us (38%)
  Pallas kernels  7.59 us (32%)
  starting transfers between devices  5.08 us (21%)
  other arithmetic  0.76 us (3%)
  local copies, waits for them, and re-layouts  0.69 us (3%)
    ppermute x3, waiting for transfers between devices, shards(): far.append(lax.ppermute(block, 'seq', pairs))  8.08 us
    ppermute x3, starting transfers between devices, shards(): far.append(lax.ppermute(block, 'seq', pairs))  2.47 us
    ppermute x2, starting transfers between devices, partner(): return lax.ppermute(block, 'head', [(place, place ^ 1) for place in places])  2.03 us
    pallas_call x1, Pallas kernels, shards(): call(attend_last, shape((length, heads * width), NARROW), count, stores(2...  1.68 us
    pallas_call x1, Pallas kernels, shards(): call(invert, (shape((2, length, length), NARROW), square, square, shape((...  1.62 us
    pallas_call x1, Pallas kernels, shards(): call(attend_near, states, 8, stores(3) + ends, spots=spots, aliases=in_pl...  1.39 us
    pallas_call x1, Pallas kernels, shards(): call(attend_next, states, 9, stores(2) + ends, spots=spots, aliases={**in...  1.25 us
    ppermute x2, waiting for transfers between devices, partner(): return lax.ppermute(block, 'head', [(place, place ^ 1) for place in places])  1.06 us
  transfers between devices with their start and end apart: 9, of which 4 were waited for; matrix products, arithmetic and copies ran while one was open for 3% of the time, Pallas kernels for 23%

profile of v8, /device:TPU:24, one launch (start us, length us, event | category | flops | bytes accessed | tf_op | source)
XLA Modules:
  0.0 23.4 jit_solution(17038322089918478885)
XLA Ops:
  0.0 1.5 %collective-permute-start.1 = (bf16[64,128]{1,0:T(8,128)(2,1)}, bf16[64,128]{1,0:T(8,128)(2,1)S(1)}, u32[]{:S(2)}, u32[]{:S(2)}) collective-permute-start(bf16[64,128]{1,0:T(8,128)(2,1)} %bitcast.5), channel_id=1, source_target_pairs={{0,1},{1,0},{2,3},{3,2},{4,5},{5,4},{6,7},{7,6},{8,9},{9,8},{10,11... | collective-permute-start | bytes 49160 | tf_op jit(solution)/shard_map/ppermute | solution.py:349
  1.5 0.7 %pad_maximum_fusion.own_ref = bf16[128,128]{1,0:T(8,128)(2,1)S(1)} fusion(bf16[64,128]{1,0:T(8,128)(2,1)} %bitcast.7, bf16[64,128]{1,0:T(8,128)(2,1)} %bitcast.8), kind=kLoop, calls=%fused_computation | loop fusion | flops 65536 | bytes 65536 | tf_op jit(solution)/shard_map/concatenate | solution.py:352
  2.2 0.5 %collective-permute-start = (bf16[128,128]{1,0:T(8,128)(2,1)S(1)}, bf16[128,128]{1,0:T(8,128)(2,1)S(1)}, u32[]{:S(2)}, u32[]{:S(2)}) collective-permute-start(bf16[128,128]{1,0:T(8,128)(2,1)S(1)} %pad_maximum_fusion.own_ref), channel_id=1, source_target_pairs={{0,1},{1,0},{2,3},{3,2},{4,5},{5,4},{6,7},{7,6},{8,9},{9,8},{10,11... | collective-permute-start | bytes 98312 | tf_op jit(solution)/shard_map/ppermute | solution.py:349
  2.8 0.7 %copy-done.2 = f32[128,2]{0,1:T(2,128)S(1)} copy-done((f32[128,2]{0,1:T(2,128)S(1)}, f32[128,2]{0,1:T(2,128)}, u32[]{:S(2)}) %copy-start.2) | copy-done | bytes 1048
  3.5 0.5 %collective-permute-done.1.other_ref = bf16[64,128]{1,0:T(8,128)(2,1)S(1)} collective-permute-done((bf16[64,128]{1,0:T(8,128)(2,1)}, bf16[64,128]{1,0:T(8,128)(2,1)S(1)}, u32[]{:S(2)}, u32[]{:S(2)}) %collective-permute-start.1) | collective-permute-done | bytes 16416 | tf_op jit(solution)/shard_map/ppermute | solution.py:349
  4.0 1.6 %shard_map.64 = (bf16[2,128,128]{2,1,0:T(8,128)(2,1)S(1)}, bf16[128,128]{1,0:T(8,128)(2,1)S(1)}, bf16[128,128]{1,0:T(8,128)(2,1)S(1)}, f32[8,128]{1,0:T(8,128)S(1)}) custom-call(bf16[64,128]{1,0:T(8,128)(2,1)S(1)} %bitcast.6, bf16[64,128]{1,0:T(8,128)(2,1)S(1)} %collective-permute-done.1.other_ref, f32[3,128]{1,0:T(4,128)S(1)} %pad_maximum_fusion.1.small_ref.refs_6_), custom_call_target="tpu_custom_call" | custom-call | flops 100000000 | bytes 1048576 | tf_op jit(solution)/shard_map/pallas_call | solution.py:357
  5.6 0.6 %collective-permute-done.other_ref = bf16[128,128]{1,0:T(8,128)(2,1)S(1)} collective-permute-done((bf16[128,128]{1,0:T(8,128)(2,1)S(1)}, bf16[128,128]{1,0:T(8,128)(2,1)S(1)}, u32[]{:S(2)}, u32[]{:S(2)}) %collective-permute-start) | collective-permute-done | bytes 32800 | tf_op jit(solution)/shard_map/ppermute | solution.py:349
  6.2 0.5 %shard_map.65 = (bf16[128,384]{1,0:T(8,128)(2,1)S(1)}, bf16[2,128,256]{2,1,0:T(8,128)(2,1)S(1)}, bf16[128,256]{1,0:T(8,128)(2,1)S(1)}) custom-call(bf16[128,128]{1,0:T(8,128)(2,1)S(1)} %pad_maximum_fusion.own_ref, bf16[128,128]{1,0:T(8,128)(2,1)S(1)} %collective-permute-done.other_ref, bf16[2,128,128]{2,1,0:T(8,128)(2,1)S(1)} %get-tuple-element.26.inverse_ref, ...), custom_call_target="tpu_custom_call" | custom-call | flops 100000000 | bytes 1048576 | tf_op jit(solution)/shard_map/pallas_call | solution.py:363
  6.7 0.0 copy-start
  6.7 0.1 collective-permute-start.2
  6.8 0.3 %collective-permute-start.3 = (bf16[128,384]{1,0:T(8,128)(2,1)S(1)}, bf16[128,384]{1,0:T(8,128)(2,1)S(1)}, u32[]{:S(2)}, u32[]{:S(2)}) collective-permute-start(bf16[128,384]{1,0:T(8,128)(2,1)S(1)} %get-tuple-element.32.pack_ref), channel_id=1, source_target_pairs={{0,8},{4,12},{8,16},{12,20},{16,24},{20,28},{24,0},{28,4},{1,9},{5... | collective-permute-start | bytes 294920 | tf_op jit(solution)/shard_map/ppermute | solution.py:385
  7.0 1.7 %collective-permute-start.5 = (bf16[128,384]{1,0:T(8,128)(2,1)S(1)}, bf16[128,384]{1,0:T(8,128)(2,1)S(1)}, u32[]{:S(2)}, u32[]{:S(2)}) collective-permute-start(bf16[128,384]{1,0:T(8,128)(2,1)S(1)} %get-tuple-element.32.pack_ref), channel_id=1, source_target_pairs={{0,16},{4,20},{8,24},{12,28},{16,0},{20,4},{24,8},{28,12},{1,17},{... | collective-permute-start | bytes 294920 | tf_op jit(solution)/shard_map/ppermute | solution.py:385
  8.7 0.1 shard_map.69
  8.9 0.5 %collective-permute-start.7 = (bf16[128,256]{1,0:T(8,128)(2,1)S(1)}, bf16[128,256]{1,0:T(8,128)(2,1)S(1)}, u32[]{:S(2)}, u32[]{:S(2)}) collective-permute-start(bf16[128,256]{1,0:T(8,128)(2,1)S(1)} %shard_map.69), channel_id=1, source_target_pairs={{0,24},{4,28},{8,0},{12,4},{16,8},{20,12},{24,16},{28,20},{1,25},{... | collective-permute-start | bytes 196616 | tf_op jit(solution)/shard_map/ppermute | solution.py:385
  9.4 2.9 %collective-permute-done.3.straight_ref = bf16[128,384]{1,0:T(8,128)(2,1)S(1)} collective-permute-done((bf16[128,384]{1,0:T(8,128)(2,1)S(1)}, bf16[128,384]{1,0:T(8,128)(2,1)S(1)}, u32[]{:S(2)}, u32[]{:S(2)}) %collective-permute-start.3) | collective-permute-done | bytes 98336 | tf_op jit(solution)/shard_map/ppermute | solution.py:385
  12.3 0.0 collective-permute-start.4
  12.3 5.1 %collective-permute-done.5.straight_ref = bf16[128,384]{1,0:T(8,128)(2,1)S(1)} collective-permute-done((bf16[128,384]{1,0:T(8,128)(2,1)S(1)}, bf16[128,384]{1,0:T(8,128)(2,1)S(1)}, u32[]{:S(2)}, u32[]{:S(2)}) %collective-permute-start.5) | collective-permute-done | bytes 98336 | tf_op jit(solution)/shard_map/ppermute | solution.py:385
  17.5 0.0 collective-permute-start.6
  17.5 0.0 collective-permute-done.7.refs_7_
  17.5 0.5 %collective-permute-start.8 = (bf16[128,256]{1,0:T(8,128)(2,1)S(1)}, bf16[128,256]{1,0:T(8,128)(2,1)S(1)}, u32[]{:S(2)}, u32[]{:S(2)}) collective-permute-start(bf16[128,256]{1,0:T(8,128)(2,1)S(1)} %collective-permute-done.7.refs_7_), channel_id=1, source_target_pairs={{0,4},{4,0},{8,12},{12,8},{16,20},{20,16},{24,28},{28,24},{1,5},{5... | collective-permute-start | bytes 196616 | tf_op jit(solution)/shard_map/ppermute | solution.py:375
  18.0 1.0 %shard_map.66 = (bf16[1024,128]{1,0:T(8,128)(2,1)S(1)}, f32[1024,128]{1,0:T(8,128)S(1)}, f32[1024,128]{1,0:T(8,128)S(1)}, f32[1024,128]{1,0:T(8,128)S(1)}) custom-call(bf16[128,1024]{1,0:T(8,128)(2,1)S(1)} %copy-done, bf16[2,128,256]{2,1,0:T(8,128)(2,1)S(1)} %get-tuple-element.30.solved_ref, bf16[128,256]{1,0:T(8,128)(2,1)S(1)} %get-tuple-element.31.sides_ref, ...), custom_call_target="tpu_custom_call" | custom-call | flops 100000000 | bytes 1048576 | tf_op jit(solution)/shard_map/pallas_call | solution.py:387
  19.0 1.4 %shard_map.67 = (f32[1024,128]{1,0:T(8,128)S(1)}, f32[1024,128]{1,0:T(8,128)S(1)}, f32[1024,128]{1,0:T(8,128)S(1)}, f32[128,128]{1,0:T(8,128)S(1)}, bf16[128,1024]{1,0:T(8,128)(2,1)}) custom-call(bf16[1024,128]{1,0:T(8,128)(2,1)S(1)} %get-tuple-element.33.moved_ref.refs_0_, ...), custom_call_target="tpu_custom_call", output_to_operand_aliasing={{0}: (1, {}), {1}: (2, {}), {2}: (3, {})} | custom-call | flops 100000000 | bytes 1048576 | tf_op jit(solution)/shard_map/pallas_call | solution.py:402
  20.4 1.3 %shard_map.68 = (f32[1024,128]{1,0:T(8,128)S(1)}, f32[1024,128]{1,0:T(8,128)S(1)}, f32[1024,128]{1,0:T(8,128)S(1)}, f32[128,128]{1,0:T(8,128)S(1)}, bf16[128,1024]{1,0:T(8,128)(2,1)}) custom-call(bf16[1024,128]{1,0:T(8,128)(2,1)S(1)} %get-tuple-element.33.moved_ref.refs_0_, ...), custom_call_target="tpu_custom_call", output_to_operand_aliasing={{0}: (1, {}), {1}: (2, {}), {2}: (3, {}), {3}: (4, {}), {4}... | custom-call | flops 100000000 | bytes 1048576 | tf_op jit(solution)/shard_map/pallas_call | solution.py:407
  21.7 1.7 %shard_map.70 = bf16[128,1024]{1,0:T(8,128)(2,1)} custom-call(bf16[1024,128]{1,0:T(8,128)(2,1)S(1)} %get-tuple-element.33.moved_ref.refs_0_, f32[1024,128]{1,0:T(8,128)S(1)} %get-tuple-element.42.refs_1_, f32[1024,128]{1,0:T(8,128)S(1)} %get-tuple-element.43.refs_2_, f32[1024,128]{1,0:T(8,128)S(1)} %get-tuple-element.44.refs_3_, ...), custom_call_target="tpu_custom_call", output_to_operand_aliasing={{}: (5, {})} | custom-call | flops 1000000000 | bytes 1048576 | tf_op jit(solution)/shard_map/pallas_call | solution.py:420
  (11 shorter events, 0.0 us)
Async XLA Ops:
  0.0 3.9 %collective-permute-start.1 = (bf16[64,128]{1,0:T(8,128)(2,1)}, bf16[64,128]{1,0:T(8,128)(2,1)S(1)}, u32[]{:S(2)}, u32[]{:S(2)}) collective-permute-start(bf16[64,128]{1,0:T(8,128)(2,1)} %bitcast.5), channel_id=1, source_target_pairs={{0,1},{1,0},{2,3},{3,2},{4,5},{5,4},{6,7},{7,6},{8,9},{9,8},{10,11... | collective-permute-start | bytes 49160 | tf_op jit(solution)/shard_map/ppermute | solution.py:349
  1.5 2.5 %copy-start.1 = (bf16[128,64]{0,1:T(8,128)(2,1)S(1)}, bf16[128,64]{0,1:T(8,128)(2,1)}, u32[]{:S(2)}) copy-start(bf16[128,64]{0,1:T(8,128)(2,1)} %param.9) | copy-start | bytes 49156
  2.2 3.9 %collective-permute-start = (bf16[128,128]{1,0:T(8,128)(2,1)S(1)}, bf16[128,128]{1,0:T(8,128)(2,1)S(1)}, u32[]{:S(2)}, u32[]{:S(2)}) collective-permute-start(bf16[128,128]{1,0:T(8,128)(2,1)S(1)} %pad_maximum_fusion.own_ref), channel_id=1, source_target_pairs={{0,1},{1,0},{2,3},{3,2},{4,5},{5,4},{6,7},{7,6},{8,9},{9,8},{10,11... | collective-permute-start | bytes 98312 | tf_op jit(solution)/shard_map/ppermute | solution.py:349
  2.8 0.7 %copy-start.2 = (f32[128,2]{0,1:T(2,128)S(1)}, f32[128,2]{0,1:T(2,128)}, u32[]{:S(2)}) copy-start(f32[128,2]{0,1:T(2,128)} %param.10) | copy-start | bytes 3076
  2.8 0.7 %copy-start.3 = (f32[128]{0:T(128)S(1)}, f32[128]{0:T(128)}, u32[]{:S(2)}) copy-start(f32[128]{0:T(128)} %param.11) | copy-start | bytes 1540
  6.7 11.3 %copy-start = (bf16[128,1024]{1,0:T(8,128)(2,1)S(1)}, bf16[128,1024]{1,0:T(8,128)(2,1)}, u32[]{:S(2)}) copy-start(bf16[128,1024]{1,0:T(8,128)(2,1)} %queries_ref.1) | copy-start | bytes 786436
  6.7 2.0 %collective-permute-start.2 = (bf16[128,384]{1,0:T(8,128)(2,1)S(1)}, bf16[128,384]{1,0:T(8,128)(2,1)S(1)}, u32[]{:S(2)}, u32[]{:S(2)}) collective-permute-start(bf16[128,384]{1,0:T(8,128)(2,1)S(1)} %get-tuple-element.32.pack_ref), channel_id=1, source_target_pairs={{0,4},{4,0},{8,12},{12,8},{16,20},{20,16},{24,28},{28,24},{1,5},{5... | collective-permute-start | bytes 294920 | tf_op jit(solution)/shard_map/ppermute | solution.py:375
  6.8 5.6 %collective-permute-start.3 = (bf16[128,384]{1,0:T(8,128)(2,1)S(1)}, bf16[128,384]{1,0:T(8,128)(2,1)S(1)}, u32[]{:S(2)}, u32[]{:S(2)}) collective-permute-start(bf16[128,384]{1,0:T(8,128)(2,1)S(1)} %get-tuple-element.32.pack_ref), channel_id=1, source_target_pairs={{0,8},{4,12},{8,16},{12,20},{16,24},{20,28},{24,0},{28,4},{1,9},{5... | collective-permute-start | bytes 294920 | tf_op jit(solution)/shard_map/ppermute | solution.py:385
  7.0 10.4 %collective-permute-start.5 = (bf16[128,384]{1,0:T(8,128)(2,1)S(1)}, bf16[128,384]{1,0:T(8,128)(2,1)S(1)}, u32[]{:S(2)}, u32[]{:S(2)}) collective-permute-start(bf16[128,384]{1,0:T(8,128)(2,1)S(1)} %get-tuple-element.32.pack_ref), channel_id=1, source_target_pairs={{0,16},{4,20},{8,24},{12,28},{16,0},{20,4},{24,8},{28,12},{1,17},{... | collective-permute-start | bytes 294920 | tf_op jit(solution)/shard_map/ppermute | solution.py:385
  8.9 8.6 %collective-permute-start.7 = (bf16[128,256]{1,0:T(8,128)(2,1)S(1)}, bf16[128,256]{1,0:T(8,128)(2,1)S(1)}, u32[]{:S(2)}, u32[]{:S(2)}) collective-permute-start(bf16[128,256]{1,0:T(8,128)(2,1)S(1)} %shard_map.69), channel_id=1, source_target_pairs={{0,24},{4,28},{8,0},{12,4},{16,8},{20,12},{24,16},{28,20},{1,25},{... | collective-permute-start | bytes 196616 | tf_op jit(solution)/shard_map/ppermute | solution.py:385
  12.3 6.7 %collective-permute-start.4 = (bf16[128,384]{1,0:T(8,128)(2,1)S(1)}, bf16[128,384]{1,0:T(8,128)(2,1)S(1)}, u32[]{:S(2)}, u32[]{:S(2)}) collective-permute-start(bf16[128,384]{1,0:T(8,128)(2,1)S(1)} %collective-permute-done.3.straight_ref), channel_id=1, source_target_pairs={{0,4},{4,0},{8,12},{12,8},{16,20},{20,16},{24,28},{28,24},{1,5},{5... | collective-permute-start | bytes 294920 | tf_op jit(solution)/shard_map/ppermute | solution.py:375
  17.5 2.9 %collective-permute-start.6 = (bf16[128,384]{1,0:T(8,128)(2,1)S(1)}, bf16[128,384]{1,0:T(8,128)(2,1)S(1)}, u32[]{:S(2)}, u32[]{:S(2)}) collective-permute-start(bf16[128,384]{1,0:T(8,128)(2,1)S(1)} %collective-permute-done.5.straight_ref), channel_id=1, source_target_pairs={{0,4},{4,0},{8,12},{12,8},{16,20},{20,16},{24,28},{28,24},{1,5},{5... | collective-permute-start | bytes 294920 | tf_op jit(solution)/shard_map/ppermute | solution.py:375
  17.5 4.2 %collective-permute-start.8 = (bf16[128,256]{1,0:T(8,128)(2,1)S(1)}, bf16[128,256]{1,0:T(8,128)(2,1)S(1)}, u32[]{:S(2)}, u32[]{:S(2)}) collective-permute-start(bf16[128,256]{1,0:T(8,128)(2,1)S(1)} %collective-permute-done.7.refs_7_), channel_id=1, source_target_pairs={{0,4},{4,0},{8,12},{12,8},{16,20},{20,16},{24,28},{28,24},{1,5},{5... | collective-permute-start | bytes 196616 | tf_op jit(solution)/shard_map/ppermute | solution.py:375
